TPU v7x, 128 devices: a whole 4x4x4 slice. The times are simulated.
128 devices in a mesh: frames: 16 (over y, x_lo, core), tiles: 8 (over x_hi, z).
Axes of the slice: x: 4 (x_hi: 2, x_lo: 2; x = x_hi * 2 + x_lo), y: 4, z: 4, core: 2. Of those that a mesh axis runs over, the one named last changes fastest.
Arguments:
- raw: bfloat16 [128, 8, 512, 1024], P('frames', None, None, 'tiles'), may hold values from -6 to 6
- offsets: int32 [128, 3], P('frames'), may hold values from -3 to 3
- taps: float32 [64], replicated, may hold values from -0.75 to 0.75
Outputs:
- activity: bfloat16 [128, 8, 512, 1024], P(None, None, 'frames', 'tiles')
- template: float32 [8, 512, 1024], P(None, 'frames', 'tiles')
All inputs are finite; a program needn't handle non-finite values.
Results may differ from a plain program's by a relative error of at most 0.006.
Values may be sent and summed in bfloat16 or wider, within the bound.
No kernel may reach another device: no remote copies, remote signals or barrier semaphores. Data moves between devices by JAX's collectives and lax.ppermute only.
A program may use at most 192 MiB of HBM per device.

v0:
```python
import jax
import jax.numpy as jnp
from jax import lax
from jax.experimental import pallas as pl
from jax.experimental.pallas import tpu as pltpu
from jax.sharding import PartitionSpec as P

TAPS = 64
SHIFT = 3
RADIUS = 8
HALO = SHIFT + 1
BOX = 2 * RADIUS + 1
LANES = 128
SUB = 8
CHUNKS = (2, 2, 2, 2)
PACK = LANES // (8 * HALO)
VMEM = 56 << 20


def iota(shape, dim):
    return lax.broadcasted_iota(jnp.int32, shape, dim)


def dot(a, b):
    return jnp.dot(a, b, preferred_element_type=jnp.float32)


def pack_body(raw_ref, first_ref, last_ref):
    slot = lax.rem(pl.program_id(0), PACK)
    planes, rows, lanes = raw_ref.shape[1:]
    source = iota((planes * lanes, 2 * LANES), 0)
    target = iota((planes * lanes, 2 * LANES), 1)
    plane, column = source // lanes, source % lanes
    side, lane = target // LANES, target % LANES
    column = column - side * (lanes - HALO)
    wanted = slot * planes * HALO + plane * HALO + column
    pick = ((lane == wanted) & (column >= 0) & (column < HALO)).astype(jnp.float32).astype(jnp.bfloat16)
    wide = jnp.concatenate([raw_ref[0, z] for z in range(planes)], axis=1)
    edges = dot(wide, pick).astype(jnp.bfloat16)

    @pl.when(slot == 0)
    def _():
        first_ref[0] = edges[:, :LANES]
        last_ref[0] = edges[:, LANES:]

    @pl.when(slot != 0)
    def _():
        first_ref[0] += edges[:, :LANES]
        last_ref[0] += edges[:, LANES:]


def pack_edges(raw):
    frames, planes, rows, lanes = raw.shape
    groups = frames // PACK
    edge = jax.ShapeDtypeStruct((groups, rows, LANES), jnp.bfloat16)
    spec = pl.BlockSpec((1, rows, LANES), lambda f: (f // PACK, 0, 0))
    return pl.pallas_call(
        pack_body,
        grid=(frames,),
        in_specs=[pl.BlockSpec((1, planes, rows, lanes), lambda f: (f, 0, 0, 0))],
        out_specs=(spec, spec),
        out_shape=(edge, edge),
        compiler_params=pltpu.CompilerParams(vmem_limit_bytes=VMEM),
        name="pack_edges",
    )(raw)


def register_body(first, count, total, last, meta_ref, raw_ref, left_ref, right_ref, *rest):
    if first > 0:
        sum_in_ref, *rest = rest
    send_ref, *rest = rest
    if not last:
        sum_out_ref, *rest = rest
    matrix, table, edge_table, smooth, summed = rest
    planes, rows, lanes = raw_ref.shape[1:]
    blocks = send_ref.shape[0]
    strip = rows // blocks
    step = pl.program_id(0)

    @pl.when(step == 0)
    def _():
        smooth[0:HALO] = jnp.zeros((HALO, rows, lanes), jnp.float32)
        smooth[HALO + planes :] = jnp.zeros((HALO, rows, lanes), jnp.float32)
        if first > 0:
            summed[SHIFT : SHIFT + planes] = sum_in_ref[...]
        else:
            summed[SHIFT : SHIFT + planes] = jnp.zeros((planes, rows, lanes), jnp.float32)

    def frame():
        index = first + step
        off_z, off_y, off_x = meta_ref[3 * index], meta_ref[3 * index + 1], meta_ref[3 * index + 2]
        at_start, at_end = meta_ref[3 * total], meta_ref[3 * total + 1]

        def fill(block, carry):
            base = pl.multiple_of(block * 64, 64)
            out_row = iota((64, rows), 0) + base
            in_row = iota((64, rows), 1)
            value = jnp.zeros((64, rows), jnp.float32)
            for delta, weight in ((-1, 1.0), (1, 1.0), (0, 2.0)):
                reached = out_row + delta
                source = reached - off_y
                inside = (reached >= 0) & (reached < rows) & (source >= 0) & (source < rows)
                gap = jnp.abs(in_row - source)
                term = jnp.where(gap == 0, BOX - 1.0, jnp.where(gap <= RADIUS, -1.0, 0.0))
                term = jnp.where(inside, term, 0.0)
                value = value + weight * term
                if delta == 0:
                    matrix[pl.ds(rows + base, 64), :] = term.astype(jnp.bfloat16)
            matrix[pl.ds(base, 64), :] = value.astype(jnp.bfloat16)
            return carry

        lax.fori_loop(0, rows // 64, fill, 0)
        both = matrix[...]

        slot = lax.rem(index, PACK)
        source = iota((2 * LANES, LANES), 0)
        target = iota((2 * LANES, LANES), 1)
        side, lane = source // LANES, source % LANES - slot * planes * HALO
        plane, column = lane // HALO, lane % HALO
        chosen = (lane >= 0) & (lane < planes * HALO) & (target == plane * 2 * HALO + side * HALO + column)
        pick = chosen.astype(jnp.float32).astype(jnp.bfloat16)
        edges = dot(jnp.concatenate([left_ref[0], right_ref[0]], axis=1), pick).astype(jnp.bfloat16)
        edge_table[...] = dot(both, edges)

        column = iota((strip, lanes), 1)
        weight_low = jnp.where((column == 0) & (at_start > 0), 0.0, 1.0)
        weight_high = jnp.where((column == lanes - 1) & (at_end > 0), 0.0, 1.0)
        within = {d: (column + d - off_x >= 0) & (column + d - off_x < lanes) for d in (-1, 0, 1)}

        for pair in range(planes // 2):
            table[...] = dot(both, jnp.concatenate([raw_ref[0, 2 * pair], raw_ref[0, 2 * pair + 1]], axis=1))

            def across(block, carry, pair=pair):
                low = pl.multiple_of(block * strip, strip)
                for half in range(2):
                    z = 2 * pair + half
                    base = 2 * HALO * z + HALO

                    def moved(start, delta):
                        body = table[pl.ds(start, strip), half * lanes : (half + 1) * lanes]
                        edge = edge_table[pl.ds(start, strip), :]
                        by = off_x - delta
                        return jnp.where(
                            within[delta],
                            pltpu.roll(body, (by + lanes) & (lanes - 1), 1),
                            pltpu.roll(edge, (by - base + 2 * lanes) & (lanes - 1), 1),
                        )

                    smoothed = weight_low * moved(low, -1) + 2.0 * moved(low, 0) + weight_high * moved(low, 1)
                    smooth[HALO + z, pl.ds(low, strip), :] = smoothed
                    summed[SHIFT + z + off_z, pl.ds(low, strip), :] += moved(rows + low, 0)
                return carry

            lax.fori_loop(0, blocks, across, 0)

        def along(block, carry):
            low = pl.multiple_of(block * strip, strip)
            plane = [smooth[HALO + z - off_z, pl.ds(low, strip), :] for z in range(planes)]
            for z in range(planes):
                value = 2.0 * plane[z]
                if z > 0:
                    value = value + plane[z - 1]
                if z + 1 < planes:
                    value = value + plane[z + 1]
                send_ref[block, 0, z] = (value * (1.0 / (BOX * 64))).astype(jnp.bfloat16)
            return carry

        lax.fori_loop(0, blocks, along, 0)

    if not last:
        frame()

        @pl.when(step == count - 1)
        def _():
            sum_out_ref[...] = summed[SHIFT : SHIFT + planes]
    else:
        pl.when(step < count)(frame)

        @pl.when(step == count)
        def _():
            def hand(block, carry):
                low = pl.multiple_of(block * strip, strip)
                for z in range(planes):
                    send_ref[block, 0, z] = (summed[SHIFT + z, pl.ds(low, strip), :] * (1.0 / BOX)).astype(jnp.bfloat16)
                return carry

            lax.fori_loop(0, blocks, hand, 0)


def register(raw, left, right, meta, summed, first, count, owners, last):
    frames, planes, rows, lanes = raw.shape
    steps = count + 1 if last else count

    def at(f):
        return first + jnp.minimum(f, count - 1)

    edge_spec = pl.BlockSpec((1, rows, LANES), lambda f, m: (at(f) // PACK, 0, 0))
    whole = pl.BlockSpec((planes, rows, lanes), lambda f, m: (0, 0, 0))
    in_specs = [pl.BlockSpec((1, planes, rows, lanes), lambda f, m: (at(f), 0, 0, 0)), edge_spec, edge_spec]
    operands = [raw, left, right]
    if first > 0:
        in_specs.append(whole)
        operands.append(summed)
    strip = rows // owners
    out_specs = [pl.BlockSpec((owners, 1, planes, strip, lanes), lambda f, m: (0, f, 0, 0, 0))]
    out_shape = [jax.ShapeDtypeStruct((owners, steps, planes, strip, lanes), jnp.bfloat16)]
    if not last:
        out_specs.append(whole)
        out_shape.append(jax.ShapeDtypeStruct((planes, rows, lanes), jnp.float32))

    def body(*refs):
        register_body(first, count, frames, last, *refs)

    return pl.pallas_call(
        body,
        grid_spec=pltpu.PrefetchScalarGridSpec(
            num_scalar_prefetch=1,
            grid=(steps,),
            in_specs=in_specs,
            out_specs=tuple(out_specs),
            scratch_shapes=[
                pltpu.VMEM((2 * rows, rows), jnp.bfloat16),
                pltpu.VMEM((2 * rows, 2 * lanes), jnp.float32),
                pltpu.VMEM((2 * rows, LANES), jnp.float32),
                pltpu.VMEM((planes + 2 * HALO, rows, lanes), jnp.float32),
                pltpu.VMEM((planes + 2 * SHIFT, rows, lanes), jnp.float32),
            ],
        ),
        out_shape=tuple(out_shape),
        compiler_params=pltpu.CompilerParams(vmem_limit_bytes=VMEM),
        name=f"register_{first}",
    )(meta, *operands)


def spread_body(taps_ref, order_ref, kernel_ref, rowsum_ref):
    total = order_ref.shape[1]
    frame = iota((total, total), 0)
    lag = frame - jnp.broadcast_to(order_ref[0:1, :], (total, total))
    value = jnp.zeros((total, total), jnp.float32)
    for tap in range(TAPS):
        value = jnp.where(lag == tap, taps_ref[tap], value)
    small = value.astype(jnp.bfloat16)
    rowsum = jnp.sum(small.astype(jnp.float32), axis=1, keepdims=True) * (1.0 / total)
    rowsum_ref[...] = jnp.broadcast_to(rowsum[:, :, None], (total, SUB, LANES)).reshape(total * SUB, LANES)
    repeat = iota((total, total * SUB), 1) // SUB == iota((total, total * SUB), 0)
    wide = dot(small, repeat.astype(jnp.float32).astype(jnp.bfloat16))
    tall = jnp.broadcast_to(wide[:, None, :], (total, SUB, total * SUB)).reshape(total * SUB, total * SUB)
    same = iota(tall.shape, 0) % SUB == iota(tall.shape, 1) % SUB
    kernel_ref[...] = jnp.where(same, tall, 0.0).astype(jnp.bfloat16)


def spread_kernel(taps, order):
    total = order.shape[1]
    return pl.pallas_call(
        spread_body,
        in_specs=[pl.BlockSpec(memory_space=pltpu.SMEM), pl.BlockSpec(memory_space=pltpu.VMEM)],
        out_shape=(
            jax.ShapeDtypeStruct((total * SUB, total * SUB), jnp.bfloat16),
            jax.ShapeDtypeStruct((total * SUB, LANES), jnp.float32),
        ),
        compiler_params=pltpu.CompilerParams(vmem_limit_bytes=VMEM),
        name="spread_kernel",
    )(taps, order)


def filter_body(group, kernel_ref, rowsum_ref, *refs):
    *got, out_ref, template_ref = refs
    owners = got[0].shape[0]
    total, _, strip, lanes = out_ref.shape
    frames = group * (total // owners)
    width = frames * SUB
    reach = -(-TAPS // frames)

    sent = got[-1][:, CHUNKS[-1], 0].astype(jnp.float32)
    template_ref[0] = jnp.sum(sent, axis=0) * (1.0 / total)

    for pair in range(strip // (2 * SUB)):
        tiles = []
        for j in range(owners // group):
            halves = []
            for half in range(2):
                low = (2 * pair + half) * SUB
                parts = []
                for ref, count in zip(got, CHUNKS):
                    part = ref[group * j : group * (j + 1), 0:count, 0, low : low + SUB, :]
                    parts.append(part.reshape(group * count * SUB, lanes))
                halves.append(jnp.concatenate(parts, axis=0))
            tiles.append(jnp.concatenate(halves, axis=1))
        mean = sum(jnp.sum(t.astype(jnp.float32).reshape(frames, SUB, 2 * lanes), axis=0) for t in tiles)
        for i in range(len(tiles)):
            lowest = max(0, i - reach)
            rows = slice(i * width, (i + 1) * width)
            value = None
            for j in range(lowest, i + 1):
                part = dot(kernel_ref[rows, j * width : (j + 1) * width], tiles[j])
                value = part if value is None else value + part
            rowsum = rowsum_ref[rows, :].reshape(frames, SUB, lanes)
            value = value.reshape(frames, SUB, 2 * lanes)
            done = [
                value[:, :, h * lanes : (h + 1) * lanes] - rowsum * mean[None, :, h * lanes : (h + 1) * lanes]
                for h in range(2)
            ]
            both = jnp.concatenate(done, axis=1).astype(jnp.bfloat16)
            out_ref[i * frames : (i + 1) * frames, 0, 2 * SUB * pair : 2 * SUB * (pair + 1), :] = both


def filter_frames(kernel, rowsum, got, total, group):
    owners, _, planes, strip, lanes = got[0].shape
    in_specs = [
        pl.BlockSpec(kernel.shape, lambda z: (0, 0)),
        pl.BlockSpec(rowsum.shape, lambda z: (0, 0)),
    ]
    for part in got:
        in_specs.append(pl.BlockSpec((owners, part.shape[1], 1, strip, lanes), lambda z: (0, 0, z, 0, 0)))

    def body(*refs):
        filter_body(group, *refs)

    return pl.pallas_call(
        body,
        grid=(planes,),
        in_specs=in_specs,
        out_specs=(
            pl.BlockSpec((total, 1, strip, lanes), lambda z: (0, z, 0, 0)),
            pl.BlockSpec((1, strip, lanes), lambda z: (z, 0, 0)),
        ),
        out_shape=(
            jax.ShapeDtypeStruct((total, planes, strip, lanes), jnp.bfloat16),
            jax.ShapeDtypeStruct((planes, strip, lanes), jnp.float32),
        ),
        compiler_params=pltpu.CompilerParams(vmem_limit_bytes=VMEM),
        name="filter_frames",
    )(kernel, rowsum, *got)


def local(raw, offsets, taps):
    frame_dev, planes, rows, lanes = raw.shape
    owners = lax.axis_size("frames")
    tiles = lax.axis_size("tiles")
    total = frame_dev * owners
    group = min(owners, 4)

    first_columns, last_columns = pack_edges(raw)
    upward = [(i, i + 1) for i in range(tiles - 1)]
    left = lax.ppermute(last_columns, "tiles", upward)
    right = lax.ppermute(first_columns, "tiles", [(j, i) for i, j in upward])

    tile = lax.axis_index("tiles")
    ends = jnp.stack([tile == 0, tile == tiles - 1]).astype(jnp.int32)
    meta = jnp.concatenate([offsets.reshape(-1), ends])

    order = []
    for block in range(owners // group):
        low = 0
        for count in CHUNKS:
            for owner in range(group * block, group * (block + 1)):
                order += [owner * frame_dev + low + f for f in range(count)]
            low += count
    kernel, rowsum = spread_kernel(taps, jnp.tile(jnp.array(order, jnp.int32)[None], (SUB, 1)))

    got = []
    summed = None
    low = 0
    for number, count in enumerate(CHUNKS):
        is_last = number == len(CHUNKS) - 1
        made = register(raw, left, right, meta, summed, low, count, owners, is_last)
        if not is_last:
            summed = made[1]
        got.append(lax.all_to_all(made[0], "frames", split_axis=0, concat_axis=0, tiled=True))
        low += count
    return filter_frames(kernel, rowsum, got, total, group)


def solution(mesh):
    placed = (P("frames", None, None, "tiles"), P("frames", None), P())
    return jax.shard_map(
        local,
        mesh=mesh,
        in_specs=placed,
        out_specs=(P(None, None, "frames", "tiles"), P(None, "frames", "tiles")),
        check_vma=False,
    )
```

profile of v0, /device:TPU:96, one launch (start us, length us, event | category | flops | bytes accessed | tf_op | source)
XLA Modules:
  0.0 232.8 jit_solution(5052024346952124967)
XLA Ops:
  0.6 9.4 %pack_edges.1 = (bf16[2,512,128]{2,1,0:T(8,128)(2,1)}, bf16[2,512,128]{2,1,0:T(8,128)(2,1)}) custom-call(bf16[8,8,512,128]{3,2,1,0:T(8,128)(2,1)} %refs_1_.7), custom_call_target="tpu_custom_call" | custom-call | tf_op jit(solution)/shard_map/pack_edges/pallas_call | solution.py:57
  10.1 3.6 %collective-permute-start = (bf16[2,512,128]{2,1,0:T(8,128)(2,1)}, bf16[2,512,128]{2,1,0:T(8,128)(2,1)S(1)}, u32[]{:S(2)}, u32[]{:S(2)}) collective-permute-start(bf16[2,512,128]{2,1,0:T(8,128)(2,1)} %get-tuple-element.14), channel_id=1, source_target_pairs={{0,1},{1,2},{2,3},{3,4},{4,5},{5,6},{6,7},{8,9},{9,10},{10,11},{11... | collective-permute-start | bytes 786440 | tf_op jit(solution)/shard_map/ppermute | solution.py:345
  13.6 2.3 collective-permute-start.1
  15.9 0.1 copy.7
  16.0 0.1 reshape.10
  16.2 0.6 pad_add_fusion.refs_0_
  16.8 3.4 %collective-permute-done.refs_2_ = bf16[2,512,128]{2,1,0:T(8,128)(2,1)S(1)} collective-permute-done((bf16[2,512,128]{2,1,0:T(8,128)(2,1)}, bf16[2,512,128]{2,1,0:T(8,128)(2,1)S(1)}, u32[]{:S(2)}, u32[]{:S(2)}) %collective-permute-start) | collective-permute-done | bytes 262176 | tf_op jit(solution)/shard_map/ppermute | solution.py:345
  20.2 6.9 %collective-permute-done.1.refs_3_ = bf16[2,512,128]{2,1,0:T(8,128)(2,1)S(1)} collective-permute-done((bf16[2,512,128]{2,1,0:T(8,128)(2,1)}, bf16[2,512,128]{2,1,0:T(8,128)(2,1)S(1)}, u32[]{:S(2)}, u32[]{:S(2)}) %collective-permute-start.1) | collective-permute-done | bytes 262176 | tf_op jit(solution)/shard_map/ppermute | solution.py:346
  27.1 0.7 copy-done.4
  27.8 31.4 %register_0.1 = (bf16[16,2,8,32,128]{4,3,2,1,0:T(8,128)(2,1)}, f32[8,512,128]{2,1,0:T(8,128)}) custom-call(s32[26]{0:T(128)} %pad_add_fusion.refs_0_, bf16[8,8,512,128]{3,2,1,0:T(8,128)(2,1)} %refs_1_.7, bf16[2,512,128]{2,1,0:T(8,128)(2,1)} %copy-done.3, bf16[2,512,128]{2,1,0:T(8,128)(2,1)} %copy-done.4), custom_call_target="tpu_custom_call" | custom-call | tf_op jit(solution)/shard_map/register_0/pallas_call | solution.py:214
  59.3 4.6 %all-to-all-start = ((bf16[16,2,8,32,128]{4,3,2,1,0:T(8,128)(2,1)}), bf16[16,2,8,32,128]{4,3,2,1,0:T(8,128)(2,1)S(1)}, u32[]{:S(2)}, u32[]{:S(2)}) async-start(bf16[16,2,8,32,128]{4,3,2,1,0:T(8,128)(2,1)} %get-tuple-element.16), calls=%async_computation | async-start | bytes 4194304 | tf_op jit(solution)/shard_map/all_to_all | solution.py:369
  63.9 32.1 %register_2.1 = (bf16[16,2,8,32,128]{4,3,2,1,0:T(8,128)(2,1)}, f32[8,512,128]{2,1,0:T(8,128)}) custom-call(s32[26]{0:T(128)} %pad_add_fusion.refs_0_, bf16[8,8,512,128]{3,2,1,0:T(8,128)(2,1)} %refs_1_.7, bf16[2,512,128]{2,1,0:T(8,128)(2,1)} %copy-done.3, bf16[2,512,128]{2,1,0:T(8,128)(2,1)} %copy-done.4, f32[8,512,128]{2,1,0:T(8,128)} %get-tuple-element.17.refs_4_), custom_call_target="tpu_custom_call" | custom-call | tf_op jit(solution)/shard_map/register_2/pallas_call | solution.py:214
  96.0 1.3 copy-done.1
  97.3 5.8 %all-to-all-start.1 = ((bf16[16,2,8,32,128]{4,3,2,1,0:T(8,128)(2,1)}), bf16[16,2,8,32,128]{4,3,2,1,0:T(8,128)(2,1)}, u32[]{:S(2)}, u32[]{:S(2)}) async-start(bf16[16,2,8,32,128]{4,3,2,1,0:T(8,128)(2,1)} %get-tuple-element.18), calls=%async_computation.1 | async-start | bytes 4194304 | tf_op jit(solution)/shard_map/all_to_all | solution.py:369
  103.1 32.2 %register_4.1 = (bf16[16,2,8,32,128]{4,3,2,1,0:T(8,128)(2,1)}, f32[8,512,128]{2,1,0:T(8,128)}) custom-call(s32[26]{0:T(128)} %pad_add_fusion.refs_0_, bf16[8,8,512,128]{3,2,1,0:T(8,128)(2,1)} %refs_1_.7, bf16[2,512,128]{2,1,0:T(8,128)(2,1)} %copy-done.3, bf16[2,512,128]{2,1,0:T(8,128)(2,1)} %copy-done.4, f32[8,512,128]{2,1,0:T(8,128)} %get-tuple-element.19.refs_4_), custom_call_target="tpu_custom_call" | custom-call | tf_op jit(solution)/shard_map/register_4/pallas_call | solution.py:214
  135.3 5.7 %all-to-all-start.2 = ((bf16[16,2,8,32,128]{4,3,2,1,0:T(8,128)(2,1)}), bf16[16,2,8,32,128]{4,3,2,1,0:T(8,128)(2,1)S(1)}, u32[]{:S(2)}, u32[]{:S(2)}) async-start(bf16[16,2,8,32,128]{4,3,2,1,0:T(8,128)(2,1)} %get-tuple-element.20), calls=%async_computation.2 | async-start | bytes 4194304 | tf_op jit(solution)/shard_map/all_to_all | solution.py:369
  141.0 31.6 %register_6.1 = bf16[16,3,8,32,128]{4,3,2,1,0:T(8,128)(2,1)} custom-call(s32[26]{0:T(128)} %pad_add_fusion.refs_0_, bf16[8,8,512,128]{3,2,1,0:T(8,128)(2,1)} %refs_1_.7, bf16[2,512,128]{2,1,0:T(8,128)(2,1)} %copy-done.3, bf16[2,512,128]{2,1,0:T(8,128)(2,1)} %copy-done.4, f32[8,512,128]{2,1,0:T(8,128)} %get-tuple-element.21.refs_4_), custom_call_target="tpu_custom_call" | custom-call | tf_op jit(solution)/shard_map/register_6/pallas_call | solution.py:214
  172.6 1.3 copy-done.2
  173.9 5.7 %all-to-all-start.3 = ((bf16[16,3,8,32,128]{4,3,2,1,0:T(8,128)(2,1)}), bf16[16,3,8,32,128]{4,3,2,1,0:T(8,128)(2,1)S(1)}, u32[]{:S(2)}, u32[]{:S(2)}) async-start(bf16[16,3,8,32,128]{4,3,2,1,0:T(8,128)(2,1)} %register_6.1), calls=%async_computation.3 | async-start | bytes 6291456 | tf_op jit(solution)/shard_map/all_to_all | solution.py:369
  179.6 0.6 tile.2.order_ref
  180.2 3.3 %spread_kernel.1 = (bf16[1024,1024]{1,0:T(8,128)(2,1)}, f32[1024,128]{1,0:T(8,128)}) custom-call(f32[64]{0:T(128)} %taps_ref.1, s32[8,128]{1,0:T(8,128)} %tile.2.order_ref), custom_call_target="tpu_custom_call" | custom-call | tf_op jit(solution)/shard_map/spread_kernel/pallas_call | solution.py:254
  183.5 35.2 %all-to-all-done.3.refs_5_ = bf16[16,3,8,32,128]{4,3,2,1,0:T(8,128)(2,1)S(1)} async-done(((bf16[16,3,8,32,128]{4,3,2,1,0:T(8,128)(2,1)}), bf16[16,3,8,32,128]{4,3,2,1,0:T(8,128)(2,1)S(1)}, u32[]{:S(2)}, u32[]{:S(2)}) %all-to-all-start.3) | async-done | bytes 3145760 | tf_op jit(solution)/shard_map/all_to_all | solution.py:369
  218.6 1.7 copy-done
  220.3 12.4 %filter_frames.1 = (bf16[128,8,32,128]{3,2,1,0:T(8,128)(2,1)}, f32[8,32,128]{2,1,0:T(8,128)}) custom-call(bf16[1024,1024]{1,0:T(8,128)(2,1)} %get-tuple-element.12.refs_0_, f32[1024,128]{1,0:T(8,128)} %get-tuple-element.13.refs_1_, bf16[16,2,8,32,128]{4,3,2,1,0:T(8,128)(2,1)} %copy-done.1, bf16[16,2,8,32,128]{4,3,2,1,0:T(8,128)(2,1)} %all-to-all-done.1.refs_3_, ...), custom_call_target="tpu_custom_call" | custom-call | tf_op jit(solution)/shard_map/filter_frames/pallas_call | solution.py:319
  (14 shorter events, 0.1 us)
Async XLA Ops:
  0.6 15.3 %copy-start.5 = (s32[8,3]{0,1:T(4,128)S(1)}, s32[8,3]{0,1:T(4,128)}, u32[]{:S(2)}) copy-start(s32[8,3]{0,1:T(4,128)} %param.5) | copy-start | bytes 292
  10.1 10.1 %collective-permute-start = (bf16[2,512,128]{2,1,0:T(8,128)(2,1)}, bf16[2,512,128]{2,1,0:T(8,128)(2,1)S(1)}, u32[]{:S(2)}, u32[]{:S(2)}) collective-permute-start(bf16[2,512,128]{2,1,0:T(8,128)(2,1)} %get-tuple-element.14), channel_id=1, source_target_pairs={{0,1},{1,2},{2,3},{3,4},{4,5},{5,6},{6,7},{8,9},{9,10},{10,11},{11... | collective-permute-start | bytes 786440 | tf_op jit(solution)/shard_map/ppermute | solution.py:345
  13.6 13.5 %collective-permute-start.1 = (bf16[2,512,128]{2,1,0:T(8,128)(2,1)}, bf16[2,512,128]{2,1,0:T(8,128)(2,1)S(1)}, u32[]{:S(2)}, u32[]{:S(2)}) collective-permute-start(bf16[2,512,128]{2,1,0:T(8,128)(2,1)} %get-tuple-element.15), channel_id=1, source_target_pairs={{1,0},{2,1},{3,2},{4,3},{5,4},{6,5},{7,6},{9,8},{10,9},{11,10},{12... | collective-permute-start | bytes 786440 | tf_op jit(solution)/shard_map/ppermute | solution.py:346
  20.2 6.9 %copy-start.3 = (bf16[2,512,128]{2,1,0:T(8,128)(2,1)}, bf16[2,512,128]{2,1,0:T(8,128)(2,1)S(1)}, u32[]{:S(2)}) copy-start(bf16[2,512,128]{2,1,0:T(8,128)(2,1)S(1)} %collective-permute-done.refs_2_) | copy-start | bytes 786436
  27.1 0.7 copy-start.4
  59.3 36.8 %all-to-all-start = ((bf16[16,2,8,32,128]{4,3,2,1,0:T(8,128)(2,1)}), bf16[16,2,8,32,128]{4,3,2,1,0:T(8,128)(2,1)S(1)}, u32[]{:S(2)}, u32[]{:S(2)}) async-start(bf16[16,2,8,32,128]{4,3,2,1,0:T(8,128)(2,1)} %get-tuple-element.16), calls=%async_computation | async-start | bytes 4194304 | tf_op jit(solution)/shard_map/all_to_all | solution.py:369
  96.0 1.3 copy-start.1
  97.3 38.0 %all-to-all-start.1 = ((bf16[16,2,8,32,128]{4,3,2,1,0:T(8,128)(2,1)}), bf16[16,2,8,32,128]{4,3,2,1,0:T(8,128)(2,1)}, u32[]{:S(2)}, u32[]{:S(2)}) async-start(bf16[16,2,8,32,128]{4,3,2,1,0:T(8,128)(2,1)} %get-tuple-element.18), calls=%async_computation.1 | async-start | bytes 4194304 | tf_op jit(solution)/shard_map/all_to_all | solution.py:369
  135.3 37.3 %all-to-all-start.2 = ((bf16[16,2,8,32,128]{4,3,2,1,0:T(8,128)(2,1)}), bf16[16,2,8,32,128]{4,3,2,1,0:T(8,128)(2,1)S(1)}, u32[]{:S(2)}, u32[]{:S(2)}) async-start(bf16[16,2,8,32,128]{4,3,2,1,0:T(8,128)(2,1)} %get-tuple-element.20), calls=%async_computation.2 | async-start | bytes 4194304 | tf_op jit(solution)/shard_map/all_to_all | solution.py:369
  172.6 7.0 %copy-start.6 = (s32[128]{0:T(128)S(1)}, s32[128]{0:T(128)}, u32[]{:S(2)}) copy-start(s32[128]{0:T(128)} %constant.10.clone) | copy-start | bytes 1540
  172.6 1.3 copy-start.2
  173.9 44.8 %all-to-all-start.3 = ((bf16[16,3,8,32,128]{4,3,2,1,0:T(8,128)(2,1)}), bf16[16,3,8,32,128]{4,3,2,1,0:T(8,128)(2,1)S(1)}, u32[]{:S(2)}, u32[]{:S(2)}) async-start(bf16[16,3,8,32,128]{4,3,2,1,0:T(8,128)(2,1)} %register_6.1), calls=%async_computation.3 | async-start | bytes 6291456 | tf_op jit(solution)/shard_map/all_to_all | solution.py:369
  218.6 1.7 copy-start
where the time goes:
time: 234 us; the launch traced here: 233 us
  Pallas kernels  152 us (65%)
  waiting for transfers between devices  45.5 us (19%)
  starting transfers between devices  27.6 us (12%)
  local copies, waits for them, and re-layouts  5.77 us (2%)
    pallas_call x4, Pallas kernels, register(): pl.pallas_call(body, grid_spec=pltpu.PrefetchScalarGridSpec(num_scalar_pr...  127 us
    all_to_all x4, waiting for transfers between devices, local(): lax.all_to_all(made[0], 'frames', split_axis=0, concat_axis=0, tiled=True)  35.2 us
    all_to_all x4, starting transfers between devices, local(): lax.all_to_all(made[0], 'frames', split_axis=0, concat_axis=0, tiled=True)  21.7 us
    pallas_call x1, Pallas kernels, filter_frames(): pl.pallas_call(body, grid=(planes,), in_specs=in_specs, out_specs=(pl.Blo...  12.4 us
    pallas_call x1, Pallas kernels, pack_edges(): pl.pallas_call(pack_body, grid=(frames,), in_specs=[pl.BlockSpec((1, plan...  9.42 us
    ppermute x1, waiting for transfers between devices, local(): right = lax.ppermute(first_columns, 'tiles', [(j, i) for i, j in upward])  6.9 us
    unnamed x15, local copies, waits for them, and re-layouts  5.1 us
  transfers between devices with their start and end apart: 6, of which 3 were waited for; matrix products, arithmetic and copies ran while one was open for 1% of the time, Pallas kernels for 43%

commit v1 on v0

--- a/solution.py
+++ b/solution.py
@@ -12,7 +12,7 @@
 BOX = 2 * RADIUS + 1
 LANES = 128
 SUB = 8
-CHUNKS = (2, 2, 2, 2)
+CHUNKS = (2, 6)
 PACK = LANES // (8 * HALO)
 VMEM = 56 << 20
 
@@ -25,25 +25,35 @@
     return jnp.dot(a, b, preferred_element_type=jnp.float32)
 
 
-def pack_body(raw_ref, first_ref, last_ref):
-    slot = lax.rem(pl.program_id(0), PACK)
-    planes, rows, lanes = raw_ref.shape[1:]
-    source = iota((planes * lanes, 2 * LANES), 0)
-    target = iota((planes * lanes, 2 * LANES), 1)
-    plane, column = source // lanes, source % lanes
-    side, lane = target // LANES, target % LANES
-    column = column - side * (lanes - HALO)
-    wanted = slot * planes * HALO + plane * HALO + column
-    pick = ((lane == wanted) & (column >= 0) & (column < HALO)).astype(jnp.float32).astype(jnp.bfloat16)
-    wide = jnp.concatenate([raw_ref[0, z] for z in range(planes)], axis=1)
-    edges = dot(wide, pick).astype(jnp.bfloat16)
-
-    @pl.when(slot == 0)
+def pack_body(*refs):
+    *raw_refs, first_ref, last_ref, pick = refs
+    step = pl.program_id(0)
+    planes, rows, lanes = raw_refs[0].shape[1:]
+    half = lax.rem(step, PACK // len(raw_refs))
+
+    @pl.when(step == 0)
+    def _():
+        pick[...] = jnp.zeros(pick.shape, pick.dtype)
+
+    low, lane = iota((SUB, LANES), 0), iota((SUB, LANES), 1)
+    wide = []
+    for f, raw_ref in enumerate(raw_refs):
+        for z in range(planes):
+            start = ((half * len(raw_refs) + f) * planes + z) * HALO
+            head = (low < HALO) & (lane == start + low)
+            tail = (low >= SUB - HALO) & (lane == start + low - (SUB - HALO))
+            row = (f * planes + z) * lanes
+            pick[row : row + SUB, :LANES] = head.astype(jnp.float32).astype(jnp.bfloat16)
+            pick[row + lanes - SUB : row + lanes, LANES:] = tail.astype(jnp.float32).astype(jnp.bfloat16)
+            wide.append(raw_ref[0, z])
+    edges = dot(jnp.concatenate(wide, axis=1), pick[...]).astype(jnp.bfloat16)
+
+    @pl.when(half == 0)
     def _():
         first_ref[0] = edges[:, :LANES]
         last_ref[0] = edges[:, LANES:]
 
-    @pl.when(slot != 0)
+    @pl.when(half != 0)
     def _():
         first_ref[0] += edges[:, :LANES]
         last_ref[0] += edges[:, LANES:]
@@ -51,18 +61,42 @@
 
 def pack_edges(raw):
     frames, planes, rows, lanes = raw.shape
-    groups = frames // PACK
-    edge = jax.ShapeDtypeStruct((groups, rows, LANES), jnp.bfloat16)
-    spec = pl.BlockSpec((1, rows, LANES), lambda f: (f // PACK, 0, 0))
+    each = 2
+    edge = jax.ShapeDtypeStruct((frames // PACK, rows, LANES), jnp.bfloat16)
+    spec = pl.BlockSpec((1, rows, LANES), lambda i: (i * each // PACK, 0, 0))
     return pl.pallas_call(
         pack_body,
-        grid=(frames,),
-        in_specs=[pl.BlockSpec((1, planes, rows, lanes), lambda f: (f, 0, 0, 0))],
+        grid=(frames // each,),
+        in_specs=[
+            pl.BlockSpec((1, planes, rows, lanes), lambda i, f=f: (i * each + f, 0, 0, 0)) for f in range(each)
+        ],
         out_specs=(spec, spec),
         out_shape=(edge, edge),
+        scratch_shapes=[pltpu.VMEM((each * planes * lanes, 2 * LANES), jnp.bfloat16)],
         compiler_params=pltpu.CompilerParams(vmem_limit_bytes=VMEM),
         name="pack_edges",
-    )(raw)
+    )(*[raw] * each)
+
+
+def high_pass(out_row, in_row, off_y, rows):
+    smoothed = 0.0
+    for delta, weight in ((-1, 1.0), (1, 1.0), (0, 2.0)):
+        reached = out_row + delta
+        source = reached - off_y
+        inside = (reached >= 0) & (reached < rows) & (source >= 0) & (source < rows)
+        gap = jnp.abs(in_row - source)
+        term = jnp.where(gap == 0, BOX - 1.0, jnp.where(gap <= RADIUS, -1.0, 0.0))
+        term = jnp.where(inside, term, 0.0)
+        smoothed = smoothed + weight * term
+    return smoothed, term
+
+
+def high_pass_inside(out_row, in_row, off_y):
+    gap = jnp.abs(in_row - out_row + off_y)
+    plain = jnp.where(gap == 0, BOX - 1.0, jnp.where(gap <= RADIUS, -1.0, 0.0))
+    far = jnp.where(gap <= RADIUS - 1, -4.0, jnp.where(gap == RADIUS, -3.0, jnp.where(gap == RADIUS + 1, -1.0, 0.0)))
+    smoothed = jnp.where(gap == 0, 2.0 * BOX - 4.0, jnp.where(gap == 1, BOX - 4.0, far))
+    return smoothed, plain
 
 
 def register_body(first, count, total, last, meta_ref, raw_ref, left_ref, right_ref, *rest):
@@ -71,7 +105,7 @@
     send_ref, *rest = rest
     if not last:
         sum_out_ref, *rest = rest
-    matrix, table, edge_table, smooth, summed = rest
+    smooth_y, plain_y, split, plain, smooth, summed = rest
     planes, rows, lanes = raw_ref.shape[1:]
     blocks = send_ref.shape[0]
     strip = rows // blocks
@@ -79,6 +113,8 @@
 
     @pl.when(step == 0)
     def _():
+        smooth_y[...] = jnp.zeros(smooth_y.shape, smooth_y.dtype)
+        plain_y[...] = jnp.zeros(plain_y.shape, plain_y.dtype)
         smooth[0:HALO] = jnp.zeros((HALO, rows, lanes), jnp.float32)
         smooth[HALO + planes :] = jnp.zeros((HALO, rows, lanes), jnp.float32)
         if first > 0:
@@ -91,26 +127,21 @@
         off_z, off_y, off_x = meta_ref[3 * index], meta_ref[3 * index + 1], meta_ref[3 * index + 2]
         at_start, at_end = meta_ref[3 * total], meta_ref[3 * total + 1]
 
-        def fill(block, carry):
-            base = pl.multiple_of(block * 64, 64)
-            out_row = iota((64, rows), 0) + base
-            in_row = iota((64, rows), 1)
-            value = jnp.zeros((64, rows), jnp.float32)
-            for delta, weight in ((-1, 1.0), (1, 1.0), (0, 2.0)):
-                reached = out_row + delta
-                source = reached - off_y
-                inside = (reached >= 0) & (reached < rows) & (source >= 0) & (source < rows)
-                gap = jnp.abs(in_row - source)
-                term = jnp.where(gap == 0, BOX - 1.0, jnp.where(gap <= RADIUS, -1.0, 0.0))
-                term = jnp.where(inside, term, 0.0)
-                value = value + weight * term
-                if delta == 0:
-                    matrix[pl.ds(rows + base, 64), :] = term.astype(jnp.bfloat16)
-            matrix[pl.ds(base, 64), :] = value.astype(jnp.bfloat16)
-            return carry
-
-        lax.fori_loop(0, rows // 64, fill, 0)
-        both = matrix[...]
+        def put(low, tall, lane, pair):
+            smoothed, unsmoothed = (value.astype(jnp.bfloat16) for value in pair)
+            wide = unsmoothed.shape[1]
+            smooth_y[low : low + tall, lane : lane + wide] = smoothed
+            smooth_y[low : low + tall, rows + lane : rows + lane + wide] = smoothed
+            plain_y[low : low + tall, lane : lane + wide] = unsmoothed
+
+        tall, wide, edge = 64, min(2 * LANES, rows), 16
+        for low in range(0, rows, tall):
+            lane = min(max((low - RADIUS - HALO) // LANES, 0) * LANES, rows - wide)
+            out_row, in_row = iota((tall, wide), 0) + low, iota((tall, wide), 1) + lane
+            put(low, tall, lane, high_pass_inside(out_row, in_row, off_y))
+        for low, lane in ((0, 0), (rows - edge, rows - wide)):
+            out_row, in_row = iota((edge, wide), 0) + low, iota((edge, wide), 1) + lane
+            put(low, edge, lane, high_pass(out_row, in_row, off_y, rows))
 
         slot = lax.rem(index, PACK)
         source = iota((2 * LANES, LANES), 0)
@@ -120,38 +151,43 @@
         chosen = (lane >= 0) & (lane < planes * HALO) & (target == plane * 2 * HALO + side * HALO + column)
         pick = chosen.astype(jnp.float32).astype(jnp.bfloat16)
         edges = dot(jnp.concatenate([left_ref[0], right_ref[0]], axis=1), pick).astype(jnp.bfloat16)
-        edge_table[...] = dot(both, edges)
-
-        column = iota((strip, lanes), 1)
-        weight_low = jnp.where((column == 0) & (at_start > 0), 0.0, 1.0)
-        weight_high = jnp.where((column == lanes - 1) & (at_end > 0), 0.0, 1.0)
-        within = {d: (column + d - off_x >= 0) & (column + d - off_x < lanes) for d in (-1, 0, 1)}
+
+        def across(source):
+            column = iota(source.shape, 1)
+            second = column >= lanes
+            column = jnp.where(second, column - lanes, column)
+            gap = source - column + off_x
+            low = jnp.where(second | ((column == 0) & (at_start > 0)), 0.0, 1.0)
+            high = jnp.where(second | ((column == lanes - 1) & (at_end > 0)), 0.0, 1.0)
+            middle = jnp.where(second, 1.0, 2.0)
+            return jnp.where(gap == 0, middle, jnp.where(gap == -1, low, jnp.where(gap == 1, high, 0.0)))
+
+        inner = across(iota((lanes, 2 * lanes), 0)).astype(jnp.bfloat16)
+        outer = iota((2 * HALO, 2 * lanes), 0)
+        outer = across(jnp.where(outer < HALO, outer - HALO, outer - HALO + lanes))
 
         for pair in range(planes // 2):
-            table[...] = dot(both, jnp.concatenate([raw_ref[0, 2 * pair], raw_ref[0, 2 * pair + 1]], axis=1))
-
-            def across(block, carry, pair=pair):
-                low = pl.multiple_of(block * strip, strip)
-                for half in range(2):
-                    z = 2 * pair + half
-                    base = 2 * HALO * z + HALO
-
-                    def moved(start, delta):
-                        body = table[pl.ds(start, strip), half * lanes : (half + 1) * lanes]
-                        edge = edge_table[pl.ds(start, strip), :]
-                        by = off_x - delta
-                        return jnp.where(
-                            within[delta],
-                            pltpu.roll(body, (by + lanes) & (lanes - 1), 1),
-                            pltpu.roll(edge, (by - base + 2 * lanes) & (lanes - 1), 1),
-                        )
-
-                    smoothed = weight_low * moved(low, -1) + 2.0 * moved(low, 0) + weight_high * moved(low, 1)
-                    smooth[HALO + z, pl.ds(low, strip), :] = smoothed
-                    summed[SHIFT + z + off_z, pl.ds(low, strip), :] += moved(rows + low, 0)
-                return carry
-
-            lax.fori_loop(0, blocks, across, 0)
+            for half in range(2):
+                z = 2 * pair + half
+                pieces = [outer]
+                if z > 0:
+                    pieces.insert(0, jnp.zeros((2 * HALO * z, 2 * lanes), jnp.float32))
+                left_over = LANES - 2 * HALO * (z + 1)
+                pieces.append(jnp.zeros((left_over, 2 * lanes), jnp.float32))
+                weights = jnp.concatenate([inner, jnp.concatenate(pieces, axis=0).astype(jnp.bfloat16)], axis=0)
+                moved = dot(jnp.concatenate([raw_ref[0, z], edges], axis=1), weights)
+                big = moved[:, :lanes].astype(jnp.bfloat16)
+                columns = slice(half * lanes, (half + 1) * lanes)
+                split[:rows, columns] = big
+                split[rows:, columns] = (moved[:, :lanes] - big.astype(jnp.float32)).astype(jnp.bfloat16)
+                plain[:, columns] = moved[:, lanes:].astype(jnp.bfloat16)
+            smoothed = dot(smooth_y[...], split[...])
+            shifted = dot(plain_y[...], plain[...])
+            for half in range(2):
+                z = 2 * pair + half
+                columns = slice(half * lanes, (half + 1) * lanes)
+                smooth[HALO + z] = smoothed[:, columns]
+                summed[SHIFT + z + off_z] += shifted[:, columns]
 
         def along(block, carry):
             low = pl.multiple_of(block * strip, strip)
@@ -191,12 +227,10 @@
     frames, planes, rows, lanes = raw.shape
     steps = count + 1 if last else count
 
-    def at(f):
-        return first + jnp.minimum(f, count - 1)
-
-    edge_spec = pl.BlockSpec((1, rows, LANES), lambda f, m: (at(f) // PACK, 0, 0))
+    edge_spec = pl.BlockSpec((1, rows, LANES), lambda f, m: ((first + jnp.minimum(f, count - 1)) // PACK, 0, 0))
     whole = pl.BlockSpec((planes, rows, lanes), lambda f, m: (0, 0, 0))
-    in_specs = [pl.BlockSpec((1, planes, rows, lanes), lambda f, m: (at(f), 0, 0, 0)), edge_spec, edge_spec]
+    raw_spec = pl.BlockSpec((1, planes, rows, lanes), lambda f, m: (first + jnp.minimum(f, count - 1), 0, 0, 0))
+    in_specs = [raw_spec, edge_spec, edge_spec]
     operands = [raw, left, right]
     if first > 0:
         in_specs.append(whole)
@@ -219,9 +253,10 @@
             in_specs=in_specs,
             out_specs=tuple(out_specs),
             scratch_shapes=[
-                pltpu.VMEM((2 * rows, rows), jnp.bfloat16),
-                pltpu.VMEM((2 * rows, 2 * lanes), jnp.float32),
-                pltpu.VMEM((2 * rows, LANES), jnp.float32),
+                pltpu.VMEM((rows, 2 * rows), jnp.bfloat16),
+                pltpu.VMEM((rows, rows), jnp.bfloat16),
+                pltpu.VMEM((2 * rows, 2 * lanes), jnp.bfloat16),
+                pltpu.VMEM((rows, 2 * lanes), jnp.bfloat16),
                 pltpu.VMEM((planes + 2 * HALO, rows, lanes), jnp.float32),
                 pltpu.VMEM((planes + 2 * SHIFT, rows, lanes), jnp.float32),
             ],

time: 234 us -> 174 us (0.74)
  Pallas kernels: 152 us -> 62.3 us
  waiting for transfers between devices: 45.5 us -> 90.6 us
  starting transfers between devices: 27.6 us -> 16.2 us
  local copies, waits for them, and re-layouts: 5.77 us -> 2.77 us
    pallas_call x4 -> x2, Pallas kernels: 127 us -> 40 us  [register(): pl.pallas_call(body, grid_spec=pltpu.PrefetchScalarGridSpec(num_scalar_pr...]
    all_to_all x4 -> x2, waiting for transfers between devices: 35.2 us -> 80.2 us  [local(): lax.all_to_all(made[0], 'frames', split_axis=0, concat_axis=0, tiled=True)]
    all_to_all x4 -> x2, starting transfers between devices: 21.7 us -> 10.4 us  [local(): lax.all_to_all(made[0], 'frames', split_axis=0, concat_axis=0, tiled=True)]
    unnamed x15 -> x11, local copies, waits for them, and re-layouts: 5.1 us -> 2.1 us
    pallas_call x1, Pallas kernels: 9.42 us -> 6.49 us  [pack_edges(): pl.pallas_call(pack_body, grid=(frames // each,), in_specs=[pl.BlockSpec(...]
  transfers between devices with their start and end apart: 6 -> 4, of which waited for: 3 -> 3; matrix products, arithmetic and copies ran while one was open for 1% -> 1% of each run, Pallas kernels for 43% -> 18%
where the time goes in v1:
time: 174 us; the launch traced here: 173 us
  waiting for transfers between devices  90.6 us (52%)
  Pallas kernels  62.3 us (36%)
  starting transfers between devices  16.2 us (9%)
  local copies, waits for them, and re-layouts  2.77 us (2%)
    all_to_all x2, waiting for transfers between devices, local(): lax.all_to_all(made[0], 'frames', split_axis=0, concat_axis=0, tiled=True)  80.2 us
    pallas_call x2, Pallas kernels, register(): pl.pallas_call(body, grid_spec=pltpu.PrefetchScalarGridSpec(num_scalar_pr...  40 us
    pallas_call x1, Pallas kernels, filter_frames(): pl.pallas_call(body, grid=(planes,), in_specs=in_specs, out_specs=(pl.Blo...  12.6 us
    all_to_all x2, starting transfers between devices, local(): lax.all_to_all(made[0], 'frames', split_axis=0, concat_axis=0, tiled=True)  10.4 us
    ppermute x1, waiting for transfers between devices, local(): right = lax.ppermute(first_columns, 'tiles', [(j, i) for i, j in upward])  6.9 us
    pallas_call x1, Pallas kernels, pack_edges(): pl.pallas_call(pack_body, grid=(frames // each,), in_specs=[pl.BlockSpec(...  6.49 us
    ppermute x1, starting transfers between devices, local(): left = lax.ppermute(last_columns, 'tiles', upward)  3.55 us
  transfers between devices with their start and end apart: 4, of which 3 were waited for; matrix products, arithmetic and copies ran while one was open for 1% of the time, Pallas kernels for 18%

profile of v1, /device:TPU:96, one launch (start us, length us, event | category | flops | bytes accessed | tf_op | source)
XLA Modules:
  0.0 173.2 jit_solution(3962766671234878642)
XLA Ops:
  0.6 0.0 copy-start.3
  0.6 6.5 %pack_edges.1 = (bf16[2,512,128]{2,1,0:T(8,128)(2,1)}, bf16[2,512,128]{2,1,0:T(8,128)(2,1)}) custom-call(bf16[8,8,512,128]{3,2,1,0:T(8,128)(2,1)} %refs_1_.5, bf16[8,8,512,128]{3,2,1,0:T(8,128)(2,1)} %refs_1_.5), custom_call_target="tpu_custom_call" | custom-call | tf_op jit(solution)/shard_map/pack_edges/pallas_call | solution.py:67
  7.1 3.6 %collective-permute-start = (bf16[2,512,128]{2,1,0:T(8,128)(2,1)}, bf16[2,512,128]{2,1,0:T(8,128)(2,1)S(1)}, u32[]{:S(2)}, u32[]{:S(2)}) collective-permute-start(bf16[2,512,128]{2,1,0:T(8,128)(2,1)} %get-tuple-element.10), channel_id=1, source_target_pairs={{0,1},{1,2},{2,3},{3,4},{4,5},{5,6},{6,7},{8,9},{9,10},{10,11},{11... | collective-permute-start | bytes 786440 | tf_op jit(solution)/shard_map/ppermute | solution.py:380
  10.7 2.3 %collective-permute-start.1 = (bf16[2,512,128]{2,1,0:T(8,128)(2,1)}, bf16[2,512,128]{2,1,0:T(8,128)(2,1)S(1)}, u32[]{:S(2)}, u32[]{:S(2)}) collective-permute-start(bf16[2,512,128]{2,1,0:T(8,128)(2,1)} %get-tuple-element.11), channel_id=1, source_target_pairs={{1,0},{2,1},{3,2},{4,3},{5,4},{6,5},{7,6},{9,8},{10,9},{11,10},{12... | collective-permute-start | bytes 786440 | tf_op jit(solution)/shard_map/ppermute | solution.py:381
  13.0 0.0 copy-done.3
  13.0 0.1 copy.7
  13.1 0.1 reshape.10
  13.2 0.1 add_convert_fusion
  13.2 0.6 pad_add_fusion.refs_0_
  13.8 3.4 %collective-permute-done.refs_2_ = bf16[2,512,128]{2,1,0:T(8,128)(2,1)S(1)} collective-permute-done((bf16[2,512,128]{2,1,0:T(8,128)(2,1)}, bf16[2,512,128]{2,1,0:T(8,128)(2,1)S(1)}, u32[]{:S(2)}, u32[]{:S(2)}) %collective-permute-start) | collective-permute-done | bytes 262176 | tf_op jit(solution)/shard_map/ppermute | solution.py:380
  17.3 6.9 %collective-permute-done.1.refs_3_ = bf16[2,512,128]{2,1,0:T(8,128)(2,1)S(1)} collective-permute-done((bf16[2,512,128]{2,1,0:T(8,128)(2,1)}, bf16[2,512,128]{2,1,0:T(8,128)(2,1)S(1)}, u32[]{:S(2)}, u32[]{:S(2)}) %collective-permute-start.1) | collective-permute-done | bytes 262176 | tf_op jit(solution)/shard_map/ppermute | solution.py:381
  24.2 0.0 copy-done.1
  24.2 0.7 copy-done.2
  24.9 12.0 %register_0.1 = (bf16[16,2,8,32,128]{4,3,2,1,0:T(8,128)(2,1)}, f32[8,512,128]{2,1,0:T(8,128)}) custom-call(s32[26]{0:T(128)} %pad_add_fusion.refs_0_, bf16[8,8,512,128]{3,2,1,0:T(8,128)(2,1)} %refs_1_.5, bf16[2,512,128]{2,1,0:T(8,128)(2,1)} %copy-done.1, bf16[2,512,128]{2,1,0:T(8,128)(2,1)} %copy-done.2), custom_call_target="tpu_custom_call" | custom-call | tf_op jit(solution)/shard_map/register_0/pallas_call | solution.py:248
  36.9 4.6 %all-to-all-start = ((bf16[16,2,8,32,128]{4,3,2,1,0:T(8,128)(2,1)}), bf16[16,2,8,32,128]{4,3,2,1,0:T(8,128)(2,1)S(1)}, u32[]{:S(2)}, u32[]{:S(2)}) async-start(bf16[16,2,8,32,128]{4,3,2,1,0:T(8,128)(2,1)} %get-tuple-element.12), calls=%async_computation | async-start | bytes 4194304 | tf_op jit(solution)/shard_map/all_to_all | solution.py:404
  41.5 28.0 %register_2.1 = bf16[16,7,8,32,128]{4,3,2,1,0:T(8,128)(2,1)} custom-call(s32[26]{0:T(128)} %pad_add_fusion.refs_0_, bf16[8,8,512,128]{3,2,1,0:T(8,128)(2,1)} %refs_1_.5, bf16[2,512,128]{2,1,0:T(8,128)(2,1)} %copy-done.1, bf16[2,512,128]{2,1,0:T(8,128)(2,1)} %copy-done.2, f32[8,512,128]{2,1,0:T(8,128)} %get-tuple-element.13.refs_4_), custom_call_target="tpu_custom_call" | custom-call | tf_op jit(solution)/shard_map/register_2/pallas_call | solution.py:248
  69.5 0.0 all-to-all-done.refs_2_
  69.5 0.0 copy-start
  69.5 1.3 copy-done
  70.8 5.7 %all-to-all-start.1 = ((bf16[16,7,8,32,128]{4,3,2,1,0:T(8,128)(2,1)}), bf16[16,7,8,32,128]{4,3,2,1,0:T(8,128)(2,1)}, u32[]{:S(2)}, u32[]{:S(2)}) async-start(bf16[16,7,8,32,128]{4,3,2,1,0:T(8,128)(2,1)} %register_2.1), calls=%async_computation.1 | async-start | bytes 14680064 | tf_op jit(solution)/shard_map/all_to_all | solution.py:404
  76.5 0.6 tile.2.order_ref
  77.1 3.2 %spread_kernel.1 = (bf16[1024,1024]{1,0:T(8,128)(2,1)}, f32[1024,128]{1,0:T(8,128)}) custom-call(f32[64]{0:T(128)} %taps_ref.1, s32[8,128]{1,0:T(8,128)} %tile.2.order_ref), custom_call_target="tpu_custom_call" | custom-call | tf_op jit(solution)/shard_map/spread_kernel/pallas_call | solution.py:289
  80.4 80.2 %all-to-all-done.1.refs_3_ = bf16[16,7,8,32,128]{4,3,2,1,0:T(8,128)(2,1)} async-done(((bf16[16,7,8,32,128]{4,3,2,1,0:T(8,128)(2,1)}), bf16[16,7,8,32,128]{4,3,2,1,0:T(8,128)(2,1)}, u32[]{:S(2)}, u32[]{:S(2)}) %all-to-all-start.1) | async-done | bytes 7340064 | tf_op jit(solution)/shard_map/all_to_all | solution.py:404
  160.6 12.6 %filter_frames.1 = (bf16[128,8,32,128]{3,2,1,0:T(8,128)(2,1)}, f32[8,32,128]{2,1,0:T(8,128)}) custom-call(bf16[1024,1024]{1,0:T(8,128)(2,1)} %get-tuple-element.8.refs_0_, f32[1024,128]{1,0:T(8,128)} %get-tuple-element.9.refs_1_, bf16[16,2,8,32,128]{4,3,2,1,0:T(8,128)(2,1)} %copy-done, bf16[16,7,8,32,128]{4,3,2,1,0:T(8,128)(2,1)} %all-to-all-done.1.refs_3_), custom_call_target="tpu_custom_call" | custom-call | tf_op jit(solution)/shard_map/filter_frames/pallas_call | solution.py:354
  (4 shorter events, 0.0 us)
Async XLA Ops:
  0.6 12.4 %copy-start.3 = (s32[8,3]{0,1:T(4,128)S(1)}, s32[8,3]{0,1:T(4,128)}, u32[]{:S(2)}) copy-start(s32[8,3]{0,1:T(4,128)} %param.5) | copy-start | bytes 292
  7.1 10.1 %collective-permute-start = (bf16[2,512,128]{2,1,0:T(8,128)(2,1)}, bf16[2,512,128]{2,1,0:T(8,128)(2,1)S(1)}, u32[]{:S(2)}, u32[]{:S(2)}) collective-permute-start(bf16[2,512,128]{2,1,0:T(8,128)(2,1)} %get-tuple-element.10), channel_id=1, source_target_pairs={{0,1},{1,2},{2,3},{3,4},{4,5},{5,6},{6,7},{8,9},{9,10},{10,11},{11... | collective-permute-start | bytes 786440 | tf_op jit(solution)/shard_map/ppermute | solution.py:380
  10.7 13.5 %collective-permute-start.1 = (bf16[2,512,128]{2,1,0:T(8,128)(2,1)}, bf16[2,512,128]{2,1,0:T(8,128)(2,1)S(1)}, u32[]{:S(2)}, u32[]{:S(2)}) collective-permute-start(bf16[2,512,128]{2,1,0:T(8,128)(2,1)} %get-tuple-element.11), channel_id=1, source_target_pairs={{1,0},{2,1},{3,2},{4,3},{5,4},{6,5},{7,6},{9,8},{10,9},{11,10},{12... | collective-permute-start | bytes 786440 | tf_op jit(solution)/shard_map/ppermute | solution.py:381
  17.3 6.9 %copy-start.1 = (bf16[2,512,128]{2,1,0:T(8,128)(2,1)}, bf16[2,512,128]{2,1,0:T(8,128)(2,1)S(1)}, u32[]{:S(2)}) copy-start(bf16[2,512,128]{2,1,0:T(8,128)(2,1)S(1)} %collective-permute-done.refs_2_) | copy-start | bytes 786436
  24.2 0.7 copy-start.2
  36.9 32.6 %all-to-all-start = ((bf16[16,2,8,32,128]{4,3,2,1,0:T(8,128)(2,1)}), bf16[16,2,8,32,128]{4,3,2,1,0:T(8,128)(2,1)S(1)}, u32[]{:S(2)}, u32[]{:S(2)}) async-start(bf16[16,2,8,32,128]{4,3,2,1,0:T(8,128)(2,1)} %get-tuple-element.12), calls=%async_computation | async-start | bytes 4194304 | tf_op jit(solution)/shard_map/all_to_all | solution.py:404
  69.5 7.1 %copy-start.4 = (s32[128]{0:T(128)S(1)}, s32[128]{0:T(128)}, u32[]{:S(2)}) copy-start(s32[128]{0:T(128)} %constant.10.clone) | copy-start | bytes 1540
  69.5 1.3 copy-start
  70.8 89.8 %all-to-all-start.1 = ((bf16[16,7,8,32,128]{4,3,2,1,0:T(8,128)(2,1)}), bf16[16,7,8,32,128]{4,3,2,1,0:T(8,128)(2,1)}, u32[]{:S(2)}, u32[]{:S(2)}) async-start(bf16[16,7,8,32,128]{4,3,2,1,0:T(8,128)(2,1)} %register_2.1), calls=%async_computation.1 | async-start | bytes 14680064 | tf_op jit(solution)/shard_map/all_to_all | solution.py:404

commit v2 on v1

--- a/solution.py
+++ b/solution.py
@@ -4,6 +4,7 @@
 from jax.experimental import pallas as pl
 from jax.experimental.pallas import tpu as pltpu
 from jax.sharding import PartitionSpec as P
+
 
 TAPS = 64
 SHIFT = 3
@@ -13,7 +14,7 @@
 LANES = 128
 SUB = 8
 CHUNKS = (2, 6)
-PACK = LANES // (8 * HALO)
+PACK = 2
 VMEM = 56 << 20
 
 
@@ -27,55 +28,50 @@
 
 def pack_body(*refs):
     *raw_refs, first_ref, last_ref, pick = refs
-    step = pl.program_id(0)
     planes, rows, lanes = raw_refs[0].shape[1:]
-    half = lax.rem(step, PACK // len(raw_refs))
-
-    @pl.when(step == 0)
+    half_rows = rows // 2
+    half_lanes = PACK * planes * HALO
+
+    @pl.when(pl.program_id(0) == 0)
     def _():
         pick[...] = jnp.zeros(pick.shape, pick.dtype)
-
-    low, lane = iota((SUB, LANES), 0), iota((SUB, LANES), 1)
-    wide = []
-    for f, raw_ref in enumerate(raw_refs):
-        for z in range(planes):
-            start = ((half * len(raw_refs) + f) * planes + z) * HALO
-            head = (low < HALO) & (lane == start + low)
-            tail = (low >= SUB - HALO) & (lane == start + low - (SUB - HALO))
-            row = (f * planes + z) * lanes
-            pick[row : row + SUB, :LANES] = head.astype(jnp.float32).astype(jnp.bfloat16)
-            pick[row + lanes - SUB : row + lanes, LANES:] = tail.astype(jnp.float32).astype(jnp.bfloat16)
-            wide.append(raw_ref[0, z])
-    edges = dot(jnp.concatenate(wide, axis=1), pick[...]).astype(jnp.bfloat16)
-
-    @pl.when(half == 0)
-    def _():
-        first_ref[0] = edges[:, :LANES]
-        last_ref[0] = edges[:, LANES:]
-
-    @pl.when(half != 0)
-    def _():
-        first_ref[0] += edges[:, :LANES]
-        last_ref[0] += edges[:, LANES:]
-
-
-def pack_edges(raw):
-    frames, planes, rows, lanes = raw.shape
-    each = 2
-    edge = jax.ShapeDtypeStruct((frames // PACK, rows, LANES), jnp.bfloat16)
-    spec = pl.BlockSpec((1, rows, LANES), lambda i: (i * each // PACK, 0, 0))
+        low, lane = iota((SUB, LANES), 0), iota((SUB, LANES), 1)
+        for half in range(2):
+            for f in range(PACK):
+                for z in range(planes):
+                    start = half * half_lanes + (f * planes + z) * HALO
+                    head = (low < HALO) & (lane == start + low)
+                    tail = (low >= SUB - HALO) & (lane == start + low - (SUB - HALO))
+                    row = (f * planes + z) * lanes
+                    pick[half, row : row + SUB, :LANES] = head.astype(jnp.float32).astype(jnp.bfloat16)
+                    row += lanes - SUB
+                    pick[half, row : row + SUB, LANES:] = tail.astype(jnp.float32).astype(jnp.bfloat16)
+
+    edges = 0.0
+    for half in range(2):
+        part = slice(half * half_rows, (half + 1) * half_rows)
+        wide = [raw_ref[0, z, part] for raw_ref in raw_refs for z in range(planes)]
+        edges = edges + dot(jnp.concatenate(wide, axis=1), pick[half])
+    edges = edges.astype(jnp.bfloat16)
+    first_ref[0] = edges[:, :LANES]
+    last_ref[0] = edges[:, LANES:]
+
+
+def pack_edges(raw, first, count):
+    _, planes, rows, lanes = raw.shape
+    edge = jax.ShapeDtypeStruct((count // PACK, rows // 2, LANES), jnp.bfloat16)
+    spec = pl.BlockSpec((1, rows // 2, LANES), lambda i: (i, 0, 0))
     return pl.pallas_call(
         pack_body,
-        grid=(frames // each,),
+        grid=(count // PACK,),
         in_specs=[
-            pl.BlockSpec((1, planes, rows, lanes), lambda i, f=f: (i * each + f, 0, 0, 0)) for f in range(each)
+            pl.BlockSpec((1, planes, rows, lanes), lambda i, f=f: (first + i * PACK + f, 0, 0, 0)) for f in range(PACK)
         ],
         out_specs=(spec, spec),
         out_shape=(edge, edge),
-        scratch_shapes=[pltpu.VMEM((each * planes * lanes, 2 * LANES), jnp.bfloat16)],
+        scratch_shapes=[pltpu.VMEM((2, PACK * planes * lanes, 2 * LANES), jnp.bfloat16)],
         compiler_params=pltpu.CompilerParams(vmem_limit_bytes=VMEM),
-        name="pack_edges",
-    )(*[raw] * each)
+    )(*[raw] * PACK)
 
 
 def high_pass(out_row, in_row, off_y, rows):
@@ -143,14 +139,18 @@
             out_row, in_row = iota((edge, wide), 0) + low, iota((edge, wide), 1) + lane
             put(low, edge, lane, high_pass(out_row, in_row, off_y, rows))
 
-        slot = lax.rem(index, PACK)
+        slot = lax.rem(step, PACK)
         source = iota((2 * LANES, LANES), 0)
         target = iota((2 * LANES, LANES), 1)
         side, lane = source // LANES, source % LANES - slot * planes * HALO
-        plane, column = lane // HALO, lane % HALO
-        chosen = (lane >= 0) & (lane < planes * HALO) & (target == plane * 2 * HALO + side * HALO + column)
-        pick = chosen.astype(jnp.float32).astype(jnp.bfloat16)
-        edges = dot(jnp.concatenate([left_ref[0], right_ref[0]], axis=1), pick).astype(jnp.bfloat16)
+        packed = jnp.concatenate([left_ref[0], right_ref[0]], axis=1)
+        edges = []
+        for half in range(2):
+            own = lane - half * PACK * planes * HALO
+            plane, column = own // HALO, own % HALO
+            chosen = (own >= 0) & (own < planes * HALO) & (target == plane * 2 * HALO + side * HALO + column)
+            edges.append(dot(packed, chosen.astype(jnp.float32).astype(jnp.bfloat16)).astype(jnp.bfloat16))
+        edges = jnp.concatenate(edges, axis=0)
 
         def across(source):
             column = iota(source.shape, 1)
@@ -227,7 +227,7 @@
     frames, planes, rows, lanes = raw.shape
     steps = count + 1 if last else count
 
-    edge_spec = pl.BlockSpec((1, rows, LANES), lambda f, m: ((first + jnp.minimum(f, count - 1)) // PACK, 0, 0))
+    edge_spec = pl.BlockSpec((1, rows // 2, LANES), lambda f, m: (jnp.minimum(f, count - 1) // PACK, 0, 0))
     whole = pl.BlockSpec((planes, rows, lanes), lambda f, m: (0, 0, 0))
     raw_spec = pl.BlockSpec((1, planes, rows, lanes), lambda f, m: (first + jnp.minimum(f, count - 1), 0, 0, 0))
     in_specs = [raw_spec, edge_spec, edge_spec]
@@ -263,34 +263,45 @@
         ),
         out_shape=tuple(out_shape),
         compiler_params=pltpu.CompilerParams(vmem_limit_bytes=VMEM),
-        name=f"register_{first}",
     )(meta, *operands)
 
 
 def spread_body(taps_ref, order_ref, kernel_ref, rowsum_ref):
-    total = order_ref.shape[1]
-    frame = iota((total, total), 0)
-    lag = frame - jnp.broadcast_to(order_ref[0:1, :], (total, total))
-    value = jnp.zeros((total, total), jnp.float32)
+    total = rowsum_ref.shape[0] // SUB
+    frames = order_ref.shape[1] // 2
+    reach = kernel_ref.shape[1] // (frames * SUB) - 1
+    for back in range(reach + 1):
+        lag = iota((frames, 2 * frames), 0) + (back * frames - order_ref[0:1, :])
+        value = jnp.zeros(lag.shape, jnp.float32)
+        for tap in range(TAPS):
+            value = jnp.where(lag == tap, taps_ref[tap], value)
+        small = value.astype(jnp.bfloat16)
+        shape = (2 * frames, frames * SUB)
+        repeat = iota(shape, 1) // SUB == iota(shape, 0)
+        wide = dot(small, repeat.astype(jnp.float32).astype(jnp.bfloat16))
+        width = frames * SUB
+        tall = jnp.broadcast_to(wide[:, None, :], (frames, SUB, width)).reshape(width, width)
+        same = iota(tall.shape, 0) % SUB == iota(tall.shape, 1) % SUB
+        low = (reach - back) * width
+        kernel_ref[:, low : low + width] = jnp.where(same, tall, 0.0).astype(jnp.bfloat16)
+
+    lag = iota((total, LANES), 0) - iota((total, LANES), 1)
+    value = jnp.zeros(lag.shape, jnp.float32)
     for tap in range(TAPS):
-        value = jnp.where(lag == tap, taps_ref[tap], value)
-    small = value.astype(jnp.bfloat16)
-    rowsum = jnp.sum(small.astype(jnp.float32), axis=1, keepdims=True) * (1.0 / total)
+        value = jnp.where((lag >= 0) & (iota(lag.shape, 1) == tap), taps_ref[tap], value)
+    rowsum = jnp.sum(value.astype(jnp.bfloat16).astype(jnp.float32), axis=1, keepdims=True) * (1.0 / total)
     rowsum_ref[...] = jnp.broadcast_to(rowsum[:, :, None], (total, SUB, LANES)).reshape(total * SUB, LANES)
-    repeat = iota((total, total * SUB), 1) // SUB == iota((total, total * SUB), 0)
-    wide = dot(small, repeat.astype(jnp.float32).astype(jnp.bfloat16))
-    tall = jnp.broadcast_to(wide[:, None, :], (total, SUB, total * SUB)).reshape(total * SUB, total * SUB)
-    same = iota(tall.shape, 0) % SUB == iota(tall.shape, 1) % SUB
-    kernel_ref[...] = jnp.where(same, tall, 0.0).astype(jnp.bfloat16)
-
-
-def spread_kernel(taps, order):
-    total = order.shape[1]
+
+
+def spread_kernel(taps, order, total, frames, reach):
+    def body(*refs):
+        spread_body(*refs)
+
     return pl.pallas_call(
-        spread_body,
+        body,
         in_specs=[pl.BlockSpec(memory_space=pltpu.SMEM), pl.BlockSpec(memory_space=pltpu.VMEM)],
         out_shape=(
-            jax.ShapeDtypeStruct((total * SUB, total * SUB), jnp.bfloat16),
+            jax.ShapeDtypeStruct((frames * SUB, (reach + 1) * frames * SUB), jnp.bfloat16),
             jax.ShapeDtypeStruct((total * SUB, LANES), jnp.float32),
         ),
         compiler_params=pltpu.CompilerParams(vmem_limit_bytes=VMEM),
@@ -298,107 +309,144 @@
     )(taps, order)
 
 
-def filter_body(group, kernel_ref, rowsum_ref, *refs):
-    *got, out_ref, template_ref = refs
-    owners = got[0].shape[0]
-    total, _, strip, lanes = out_ref.shape
-    frames = group * (total // owners)
+def filter_body(groups, kernel_ref, rowsum_ref, *refs):
+    *got, out_ref, template_ref, done, sems = refs
+    group = got[0].shape[0]
+    strip, lanes = done.shape[2:]
+    total = done.shape[1]
+    frames = total // groups
     width = frames * SUB
-    reach = -(-TAPS // frames)
-
-    sent = got[-1][:, CHUNKS[-1], 0].astype(jnp.float32)
-    template_ref[0] = jnp.sum(sent, axis=0) * (1.0 / total)
-
+    reach = kernel_ref.shape[1] // width - 1
+    step = pl.program_id(0)
+    slot = lax.rem(step, 2)
+    got = [got[c * groups : (c + 1) * groups] for c in range(len(CHUNKS))]
+
+    def copy(z, slot, i):
+        part = pl.ds(i * frames, frames)
+        return pltpu.make_async_copy(done.at[slot, part], out_ref.at[part, z], sems.at[slot, i])
+
+    sent = sum(jnp.sum(ref[:, CHUNKS[-1], 0].astype(jnp.float32), axis=0) for ref in got[-1])
+    template_ref[0] = sent * (1.0 / total)
+
+    tiles = []
+    means = []
     for pair in range(strip // (2 * SUB)):
-        tiles = []
-        for j in range(owners // group):
+        stack = []
+        for j in range(groups):
             halves = []
             for half in range(2):
                 low = (2 * pair + half) * SUB
                 parts = []
-                for ref, count in zip(got, CHUNKS):
-                    part = ref[group * j : group * (j + 1), 0:count, 0, low : low + SUB, :]
+                for refs, count in zip(got, CHUNKS):
+                    part = refs[j][:, 0:count, 0, low : low + SUB, :]
                     parts.append(part.reshape(group * count * SUB, lanes))
                 halves.append(jnp.concatenate(parts, axis=0))
-            tiles.append(jnp.concatenate(halves, axis=1))
-        mean = sum(jnp.sum(t.astype(jnp.float32).reshape(frames, SUB, 2 * lanes), axis=0) for t in tiles)
-        for i in range(len(tiles)):
+            stack.append(jnp.concatenate(halves, axis=1))
+        means.append(sum(jnp.sum(t.astype(jnp.float32).reshape(frames, SUB, 2 * lanes), axis=0) for t in stack))
+        tiles.append(stack)
+
+    @pl.when(step >= 2)
+    def _():
+        for i in range(groups):
+            copy(step - 2, slot, i).wait()
+
+    for i in range(groups):
+        rows = slice(i * width, (i + 1) * width)
+        for pair in range(len(tiles)):
             lowest = max(0, i - reach)
-            rows = slice(i * width, (i + 1) * width)
-            value = None
-            for j in range(lowest, i + 1):
-                part = dot(kernel_ref[rows, j * width : (j + 1) * width], tiles[j])
-                value = part if value is None else value + part
+            value = dot(
+                kernel_ref[:, (reach - i + lowest) * width :],
+                jnp.concatenate(tiles[pair][lowest : i + 1], axis=0),
+            ).reshape(frames, SUB, 2 * lanes)
             rowsum = rowsum_ref[rows, :].reshape(frames, SUB, lanes)
-            value = value.reshape(frames, SUB, 2 * lanes)
-            done = [
-                value[:, :, h * lanes : (h + 1) * lanes] - rowsum * mean[None, :, h * lanes : (h + 1) * lanes]
+            both = [
+                value[:, :, h * lanes : (h + 1) * lanes] - rowsum * means[pair][None, :, h * lanes : (h + 1) * lanes]
                 for h in range(2)
             ]
-            both = jnp.concatenate(done, axis=1).astype(jnp.bfloat16)
-            out_ref[i * frames : (i + 1) * frames, 0, 2 * SUB * pair : 2 * SUB * (pair + 1), :] = both
+            both = jnp.concatenate(both, axis=1).astype(jnp.bfloat16)
+            done[slot, i * frames : (i + 1) * frames, 2 * SUB * pair : 2 * SUB * (pair + 1), :] = both
+        copy(step, slot, i).start()
+
+    @pl.when(step == pl.num_programs(0) - 1)
+    def _():
+        for i in range(groups):
+            copy(step - 1, 1 - slot, i).wait()
+        for i in range(groups):
+            copy(step, slot, i).wait()
 
 
 def filter_frames(kernel, rowsum, got, total, group):
     owners, _, planes, strip, lanes = got[0].shape
+    groups = owners // group
     in_specs = [
         pl.BlockSpec(kernel.shape, lambda z: (0, 0)),
         pl.BlockSpec(rowsum.shape, lambda z: (0, 0)),
     ]
+    operands = []
     for part in got:
-        in_specs.append(pl.BlockSpec((owners, part.shape[1], 1, strip, lanes), lambda z: (0, 0, z, 0, 0)))
+        for j in range(groups):
+            in_specs.append(pl.BlockSpec((group, part.shape[1], 1, strip, lanes), lambda z, j=j: (j, 0, z, 0, 0)))
+            operands.append(part)
 
     def body(*refs):
-        filter_body(group, *refs)
+        filter_body(groups, *refs)
 
     return pl.pallas_call(
         body,
         grid=(planes,),
         in_specs=in_specs,
         out_specs=(
-            pl.BlockSpec((total, 1, strip, lanes), lambda z: (0, z, 0, 0)),
+            pl.BlockSpec(memory_space=pl.ANY),
             pl.BlockSpec((1, strip, lanes), lambda z: (z, 0, 0)),
         ),
         out_shape=(
             jax.ShapeDtypeStruct((total, planes, strip, lanes), jnp.bfloat16),
             jax.ShapeDtypeStruct((planes, strip, lanes), jnp.float32),
         ),
+        scratch_shapes=[pltpu.VMEM((2, total, strip, lanes), jnp.bfloat16), pltpu.SemaphoreType.DMA((2, groups))],
         compiler_params=pltpu.CompilerParams(vmem_limit_bytes=VMEM),
         name="filter_frames",
-    )(kernel, rowsum, *got)
+    )(kernel, rowsum, *operands)
 
 
 def local(raw, offsets, taps):
-    frame_dev, planes, rows, lanes = raw.shape
+    frame_dev, _, _, _ = raw.shape
     owners = lax.axis_size("frames")
     tiles = lax.axis_size("tiles")
     total = frame_dev * owners
     group = min(owners, 4)
 
-    first_columns, last_columns = pack_edges(raw)
     upward = [(i, i + 1) for i in range(tiles - 1)]
-    left = lax.ppermute(last_columns, "tiles", upward)
-    right = lax.ppermute(first_columns, "tiles", [(j, i) for i, j in upward])
+    sides = []
+    low = 0
+    for count in CHUNKS:
+        first_columns, last_columns = pack_edges(raw, low, count)
+        left = lax.ppermute(last_columns, "tiles", upward)
+        right = lax.ppermute(first_columns, "tiles", [(j, i) for i, j in upward])
+        sides.append((left, right))
+        low += count
 
     tile = lax.axis_index("tiles")
     ends = jnp.stack([tile == 0, tile == tiles - 1]).astype(jnp.int32)
     meta = jnp.concatenate([offsets.reshape(-1), ends])
 
     order = []
-    for block in range(owners // group):
-        low = 0
-        for count in CHUNKS:
-            for owner in range(group * block, group * (block + 1)):
-                order += [owner * frame_dev + low + f for f in range(count)]
-            low += count
-    kernel, rowsum = spread_kernel(taps, jnp.tile(jnp.array(order, jnp.int32)[None], (SUB, 1)))
+    low = 0
+    for count in CHUNKS:
+        for owner in range(group):
+            order += [owner * frame_dev + low + f for f in range(count)]
+        low += count
+    frames = group * frame_dev
+    reach = min(-(-TAPS // frames), owners // group - 1)
+    order = jnp.array(order + [1 << 20] * frames, jnp.int32)
+    kernel, rowsum = spread_kernel(taps, jnp.tile(order[None], (SUB, 1)), total, frames, reach)
 
     got = []
     summed = None
     low = 0
     for number, count in enumerate(CHUNKS):
         is_last = number == len(CHUNKS) - 1
-        made = register(raw, left, right, meta, summed, low, count, owners, is_last)
+        made = register(raw, *sides[number], meta, summed, low, count, owners, is_last)
         if not is_last:
             summed = made[1]
         got.append(lax.all_to_all(made[0], "frames", split_axis=0, concat_axis=0, tiled=True))

time: 174 us -> 202 us (1.16)
  the two profiles are of different devices: /device:TPU:96 before, /device:TPU:4 now
where the time goes in v2:
time: 202 us; the launch traced here: 201 us
  waiting for transfers between devices  102 us (50%)
  Pallas kernels  64.5 us (32%)
  starting transfers between devices  29.6 us (15%)
  local copies, waits for them, and re-layouts  3.53 us (2%)
    all_to_all x2, waiting for transfers between devices, local(): lax.all_to_all(made[0], 'frames', split_axis=0, concat_axis=0, tiled=True)  81.1 us
    pallas_call x2, Pallas kernels, register(): pl.pallas_call(body, grid_spec=pltpu.PrefetchScalarGridSpec(num_scalar_pr...  40.8 us
    ppermute x2, waiting for transfers between devices, local(): left = lax.ppermute(last_columns, 'tiles', upward)  19.9 us
    pallas_call x1, Pallas kernels, filter_frames(): pl.pallas_call(body, grid=(planes,), in_specs=in_specs, out_specs=(pl.Blo...  13 us
    ppermute x2, starting transfers between devices, local(): right = lax.ppermute(first_columns, 'tiles', [(j, i) for i, j in upward])  12.7 us
    all_to_all x2, starting transfers between devices, local(): lax.all_to_all(made[0], 'frames', split_axis=0, concat_axis=0, tiled=True)  10.7 us
    pallas_call x2, Pallas kernels, pack_edges(): pl.pallas_call(pack_body, grid=(count // PACK,), in_specs=[pl.BlockSpec((...  8.36 us
    ppermute x2, starting transfers between devices, local(): left = lax.ppermute(last_columns, 'tiles', upward)  6.15 us
  transfers between devices with their start and end apart: 6, of which 3 were waited for; matrix products, arithmetic and copies ran while one was open for 1% of the time, Pallas kernels for 18%

profile of v2, /device:TPU:4, one launch (start us, length us, event | category | flops | bytes accessed | tf_op | source)
XLA Modules:
  0.0 201.4 jit_solution(14688707103499759938)
XLA Ops:
  0.6 2.9 %shard_map.59 = (bf16[1,256,128]{2,1,0:T(8,128)(2,1)}, bf16[1,256,128]{2,1,0:T(8,128)(2,1)}) custom-call(bf16[8,8,512,128]{3,2,1,0:T(8,128)(2,1)} %refs_1_.7, bf16[8,8,512,128]{3,2,1,0:T(8,128)(2,1)} %refs_1_.7), custom_call_target="tpu_custom_call" | custom-call | tf_op jit(solution)/shard_map/pallas_call | solution.py:64
  3.6 3.8 %collective-permute-start = (bf16[1,256,128]{2,1,0:T(8,128)(2,1)}, bf16[1,256,128]{2,1,0:T(8,128)(2,1)S(1)}, u32[]{:S(2)}, u32[]{:S(2)}) collective-permute-start(bf16[1,256,128]{2,1,0:T(8,128)(2,1)} %get-tuple-element.12), channel_id=1, source_target_pairs={{0,1},{1,2},{2,3},{3,4},{4,5},{5,6},{6,7},{8,9},{9,10},{10,11},{11... | collective-permute-start | bytes 196616 | tf_op jit(solution)/shard_map/ppermute | solution.py:424
  7.4 5.6 %collective-permute-start.1 = (bf16[1,256,128]{2,1,0:T(8,128)(2,1)}, bf16[1,256,128]{2,1,0:T(8,128)(2,1)S(1)}, u32[]{:S(2)}, u32[]{:S(2)}) collective-permute-start(bf16[1,256,128]{2,1,0:T(8,128)(2,1)} %get-tuple-element.13), channel_id=1, source_target_pairs={{1,0},{2,1},{3,2},{4,3},{5,4},{6,5},{7,6},{9,8},{10,9},{11,10},{12... | collective-permute-start | bytes 196616 | tf_op jit(solution)/shard_map/ppermute | solution.py:425
  13.1 0.1 copy.7
  13.1 0.1 reshape.10
  13.2 0.1 add_convert_fusion
  13.3 0.7 pad_add_fusion.refs_0_
  14.0 1.3 collective-permute-done.1.refs_3_
  15.3 0.6 copy-done.4
  15.9 12.2 %shard_map.60 = (bf16[16,2,8,32,128]{4,3,2,1,0:T(8,128)(2,1)}, f32[8,512,128]{2,1,0:T(8,128)}) custom-call(s32[26]{0:T(128)} %pad_add_fusion.refs_0_, bf16[8,8,512,128]{3,2,1,0:T(8,128)(2,1)} %refs_1_.7, bf16[1,256,128]{2,1,0:T(8,128)(2,1)} %copy-done.3, bf16[1,256,128]{2,1,0:T(8,128)(2,1)} %copy-done.4), custom_call_target="tpu_custom_call" | custom-call | tf_op jit(solution)/shard_map/pallas_call | solution.py:248
  28.1 5.2 %all-to-all-start = ((bf16[16,2,8,32,128]{4,3,2,1,0:T(8,128)(2,1)}), bf16[16,2,8,32,128]{4,3,2,1,0:T(8,128)(2,1)S(1)}, u32[]{:S(2)}, u32[]{:S(2)}) async-start(bf16[16,2,8,32,128]{4,3,2,1,0:T(8,128)(2,1)} %get-tuple-element.14), calls=%async_computation | async-start | bytes 4194304 | tf_op jit(solution)/shard_map/all_to_all | solution.py:452
  33.3 5.4 %shard_map.61 = (bf16[3,256,128]{2,1,0:T(8,128)(2,1)}, bf16[3,256,128]{2,1,0:T(8,128)(2,1)}) custom-call(bf16[8,8,512,128]{3,2,1,0:T(8,128)(2,1)} %refs_1_.7, bf16[8,8,512,128]{3,2,1,0:T(8,128)(2,1)} %refs_1_.7), custom_call_target="tpu_custom_call" | custom-call | tf_op jit(solution)/shard_map/pallas_call | solution.py:64
  38.7 2.3 %collective-permute-start.2 = (bf16[3,256,128]{2,1,0:T(8,128)(2,1)}, bf16[3,256,128]{2,1,0:T(8,128)(2,1)S(1)}, u32[]{:S(2)}, u32[]{:S(2)}) collective-permute-start(bf16[3,256,128]{2,1,0:T(8,128)(2,1)} %get-tuple-element.15), channel_id=1, source_target_pairs={{0,1},{1,2},{2,3},{3,4},{4,5},{5,6},{6,7},{8,9},{9,10},{10,11},{11... | collective-permute-start | bytes 589832 | tf_op jit(solution)/shard_map/ppermute | solution.py:424
  41.1 7.1 %collective-permute-start.3 = (bf16[3,256,128]{2,1,0:T(8,128)(2,1)}, bf16[3,256,128]{2,1,0:T(8,128)(2,1)S(1)}, u32[]{:S(2)}, u32[]{:S(2)}) collective-permute-start(bf16[3,256,128]{2,1,0:T(8,128)(2,1)} %get-tuple-element.16), channel_id=1, source_target_pairs={{1,0},{2,1},{3,2},{4,3},{5,4},{6,5},{7,6},{9,8},{10,9},{11,10},{12... | collective-permute-start | bytes 589832 | tf_op jit(solution)/shard_map/ppermute | solution.py:425
  48.2 19.9 %collective-permute-done.2.refs_2_ = bf16[3,256,128]{2,1,0:T(8,128)(2,1)S(1)} collective-permute-done((bf16[3,256,128]{2,1,0:T(8,128)(2,1)}, bf16[3,256,128]{2,1,0:T(8,128)(2,1)S(1)}, u32[]{:S(2)}, u32[]{:S(2)}) %collective-permute-start.2) | collective-permute-done | bytes 196640 | tf_op jit(solution)/shard_map/ppermute | solution.py:424
  68.1 0.7 copy-done.1
  68.8 0.1 copy-done.2
  68.8 28.6 %shard_map.62 = bf16[16,7,8,32,128]{4,3,2,1,0:T(8,128)(2,1)} custom-call(s32[26]{0:T(128)} %pad_add_fusion.refs_0_, bf16[8,8,512,128]{3,2,1,0:T(8,128)(2,1)} %refs_1_.7, bf16[3,256,128]{2,1,0:T(8,128)(2,1)} %copy-done.1, bf16[3,256,128]{2,1,0:T(8,128)(2,1)} %copy-done.2, f32[8,512,128]{2,1,0:T(8,128)} %get-tuple-element.17.refs_4_), custom_call_target="tpu_custom_call" | custom-call | tf_op jit(solution)/shard_map/pallas_call | solution.py:248
  97.5 1.4 copy-done
  98.9 5.5 %all-to-all-start.1 = ((bf16[16,7,8,32,128]{4,3,2,1,0:T(8,128)(2,1)}), bf16[16,7,8,32,128]{4,3,2,1,0:T(8,128)(2,1)}, u32[]{:S(2)}, u32[]{:S(2)}) async-start(bf16[16,7,8,32,128]{4,3,2,1,0:T(8,128)(2,1)} %shard_map.62), calls=%async_computation.1 | async-start | bytes 14680064 | tf_op jit(solution)/shard_map/all_to_all | solution.py:452
  104.4 0.6 tile.2.refs_1_
  105.0 2.4 %spread_kernel.1 = (bf16[256,768]{1,0:T(8,128)(2,1)}, f32[1024,128]{1,0:T(8,128)}) custom-call(f32[64]{0:T(128)} %refs_0_.3, s32[8,64]{1,0:T(8,128)} %tile.2.refs_1_), custom_call_target="tpu_custom_call" | custom-call | tf_op jit(solution)/shard_map/spread_kernel/pallas_call | solution.py:300
  107.3 81.1 %all-to-all-done.1.refs_6_.refs_7_.refs_8_.refs_9_ = bf16[16,7,8,32,128]{4,3,2,1,0:T(8,128)(2,1)} async-done(((bf16[16,7,8,32,128]{4,3,2,1,0:T(8,128)(2,1)}), bf16[16,7,8,32,128]{4,3,2,1,0:T(8,128)(2,1)}, u32[]{:S(2)}, u32[]{:S(2)}) %all-to-all-start.1) | async-done | bytes 7340064 | tf_op jit(solution)/shard_map/all_to_all | solution.py:452
  188.4 13.0 %filter_frames.1 = (bf16[128,8,32,128]{3,2,1,0:T(8,128)(2,1)}, f32[8,32,128]{2,1,0:T(8,128)}) custom-call(bf16[256,768]{1,0:T(8,128)(2,1)} %get-tuple-element.10.refs_0_, f32[1024,128]{1,0:T(8,128)} %get-tuple-element.11.refs_1_, bf16[16,2,8,32,128]{4,3,2,1,0:T(8,128)(2,1)} %copy-done, bf16[16,2,8,32,128]{4,3,2,1,0:T(8,128)(2,1)} %copy-done, ...), custom_call_target="tpu_custom_call" | custom-call | tf_op jit(solution)/shard_map/filter_frames/pallas_call | solution.py:394
  (13 shorter events, 0.0 us)
Async XLA Ops:
  0.6 12.4 %copy-start.5 = (s32[8,3]{0,1:T(4,128)S(1)}, s32[8,3]{0,1:T(4,128)}, u32[]{:S(2)}) copy-start(s32[8,3]{0,1:T(4,128)} %param.5) | copy-start | bytes 292
  3.6 10.4 %collective-permute-start = (bf16[1,256,128]{2,1,0:T(8,128)(2,1)}, bf16[1,256,128]{2,1,0:T(8,128)(2,1)S(1)}, u32[]{:S(2)}, u32[]{:S(2)}) collective-permute-start(bf16[1,256,128]{2,1,0:T(8,128)(2,1)} %get-tuple-element.12), channel_id=1, source_target_pairs={{0,1},{1,2},{2,3},{3,4},{4,5},{5,6},{6,7},{8,9},{9,10},{10,11},{11... | collective-permute-start | bytes 196616 | tf_op jit(solution)/shard_map/ppermute | solution.py:424
  7.4 7.8 %collective-permute-start.1 = (bf16[1,256,128]{2,1,0:T(8,128)(2,1)}, bf16[1,256,128]{2,1,0:T(8,128)(2,1)S(1)}, u32[]{:S(2)}, u32[]{:S(2)}) collective-permute-start(bf16[1,256,128]{2,1,0:T(8,128)(2,1)} %get-tuple-element.13), channel_id=1, source_target_pairs={{1,0},{2,1},{3,2},{4,3},{5,4},{6,5},{7,6},{9,8},{10,9},{11,10},{12... | collective-permute-start | bytes 196616 | tf_op jit(solution)/shard_map/ppermute | solution.py:425
  14.0 1.3 copy-start.3
  15.2 0.6 copy-start.4
  28.1 69.4 %all-to-all-start = ((bf16[16,2,8,32,128]{4,3,2,1,0:T(8,128)(2,1)}), bf16[16,2,8,32,128]{4,3,2,1,0:T(8,128)(2,1)S(1)}, u32[]{:S(2)}, u32[]{:S(2)}) async-start(bf16[16,2,8,32,128]{4,3,2,1,0:T(8,128)(2,1)} %get-tuple-element.14), calls=%async_computation | async-start | bytes 4194304 | tf_op jit(solution)/shard_map/all_to_all | solution.py:452
  38.7 29.4 %collective-permute-start.2 = (bf16[3,256,128]{2,1,0:T(8,128)(2,1)}, bf16[3,256,128]{2,1,0:T(8,128)(2,1)S(1)}, u32[]{:S(2)}, u32[]{:S(2)}) collective-permute-start(bf16[3,256,128]{2,1,0:T(8,128)(2,1)} %get-tuple-element.15), channel_id=1, source_target_pairs={{0,1},{1,2},{2,3},{3,4},{4,5},{5,6},{6,7},{8,9},{9,10},{10,11},{11... | collective-permute-start | bytes 589832 | tf_op jit(solution)/shard_map/ppermute | solution.py:424
  41.1 27.0 %collective-permute-start.3 = (bf16[3,256,128]{2,1,0:T(8,128)(2,1)}, bf16[3,256,128]{2,1,0:T(8,128)(2,1)S(1)}, u32[]{:S(2)}, u32[]{:S(2)}) collective-permute-start(bf16[3,256,128]{2,1,0:T(8,128)(2,1)} %get-tuple-element.16), channel_id=1, source_target_pairs={{1,0},{2,1},{3,2},{4,3},{5,4},{6,5},{7,6},{9,8},{10,9},{11,10},{12... | collective-permute-start | bytes 589832 | tf_op jit(solution)/shard_map/ppermute | solution.py:425
  68.1 0.7 copy-start.1
  68.1 0.8 copy-start.2
  97.5 6.9 %copy-start.6 = (s32[64]{0:T(128)S(1)}, s32[64]{0:T(128)}, u32[]{:S(2)}) copy-start(s32[64]{0:T(128)} %constant.10.clone) | copy-start | bytes 772
  97.5 1.4 copy-start
  98.9 89.6 %all-to-all-start.1 = ((bf16[16,7,8,32,128]{4,3,2,1,0:T(8,128)(2,1)}), bf16[16,7,8,32,128]{4,3,2,1,0:T(8,128)(2,1)}, u32[]{:S(2)}, u32[]{:S(2)}) async-start(bf16[16,7,8,32,128]{4,3,2,1,0:T(8,128)(2,1)} %shard_map.62), calls=%async_computation.1 | async-start | bytes 14680064 | tf_op jit(solution)/shard_map/all_to_all | solution.py:452

commit v3 on v1

--- a/solution.py
+++ b/solution.py
@@ -4,6 +4,7 @@
 from jax.experimental import pallas as pl
 from jax.experimental.pallas import tpu as pltpu
 from jax.sharding import PartitionSpec as P
+
 
 TAPS = 64
 SHIFT = 3
@@ -28,7 +29,7 @@
 def pack_body(*refs):
     *raw_refs, first_ref, last_ref, pick = refs
     step = pl.program_id(0)
-    planes, rows, lanes = raw_refs[0].shape[1:]
+    planes, _, lanes = raw_refs[0].shape[1:]
     half = lax.rem(step, PACK // len(raw_refs))
 
     @pl.when(step == 0)
@@ -99,12 +100,10 @@
     return smoothed, plain
 
 
-def register_body(first, count, total, last, meta_ref, raw_ref, left_ref, right_ref, *rest):
+def register_body(first, count, total, meta_ref, raw_ref, left_ref, right_ref, *rest):
     if first > 0:
         sum_in_ref, *rest = rest
-    send_ref, *rest = rest
-    if not last:
-        sum_out_ref, *rest = rest
+    send_ref, sum_out_ref, *rest = rest
     smooth_y, plain_y, split, plain, smooth, summed = rest
     planes, rows, lanes = raw_ref.shape[1:]
     blocks = send_ref.shape[0]
@@ -118,7 +117,7 @@
         smooth[0:HALO] = jnp.zeros((HALO, rows, lanes), jnp.float32)
         smooth[HALO + planes :] = jnp.zeros((HALO, rows, lanes), jnp.float32)
         if first > 0:
-            summed[SHIFT : SHIFT + planes] = sum_in_ref[...]
+            summed[SHIFT : SHIFT + planes] = sum_in_ref[...] * BOX
         else:
             summed[SHIFT : SHIFT + planes] = jnp.zeros((planes, rows, lanes), jnp.float32)
 
@@ -203,33 +202,19 @@
 
         lax.fori_loop(0, blocks, along, 0)
 
-    if not last:
-        frame()
-
-        @pl.when(step == count - 1)
-        def _():
-            sum_out_ref[...] = summed[SHIFT : SHIFT + planes]
-    else:
-        pl.when(step < count)(frame)
-
-        @pl.when(step == count)
-        def _():
-            def hand(block, carry):
-                low = pl.multiple_of(block * strip, strip)
-                for z in range(planes):
-                    send_ref[block, 0, z] = (summed[SHIFT + z, pl.ds(low, strip), :] * (1.0 / BOX)).astype(jnp.bfloat16)
-                return carry
-
-            lax.fori_loop(0, blocks, hand, 0)
-
-
-def register(raw, left, right, meta, summed, first, count, owners, last):
+    frame()
+
+    @pl.when(step == count - 1)
+    def _():
+        sum_out_ref[...] = summed[SHIFT : SHIFT + planes] * (1.0 / BOX)
+
+
+def register(raw, left, right, meta, summed, first, count, owners):
     frames, planes, rows, lanes = raw.shape
-    steps = count + 1 if last else count
-
-    edge_spec = pl.BlockSpec((1, rows, LANES), lambda f, m: ((first + jnp.minimum(f, count - 1)) // PACK, 0, 0))
+
+    edge_spec = pl.BlockSpec((1, rows, LANES), lambda f, m: ((first + f) // PACK, 0, 0))
     whole = pl.BlockSpec((planes, rows, lanes), lambda f, m: (0, 0, 0))
-    raw_spec = pl.BlockSpec((1, planes, rows, lanes), lambda f, m: (first + jnp.minimum(f, count - 1), 0, 0, 0))
+    raw_spec = pl.BlockSpec((1, planes, rows, lanes), lambda f, m: (first + f, 0, 0, 0))
     in_specs = [raw_spec, edge_spec, edge_spec]
     operands = [raw, left, right]
     if first > 0:
@@ -237,19 +222,18 @@
         operands.append(summed)
     strip = rows // owners
     out_specs = [pl.BlockSpec((owners, 1, planes, strip, lanes), lambda f, m: (0, f, 0, 0, 0))]
-    out_shape = [jax.ShapeDtypeStruct((owners, steps, planes, strip, lanes), jnp.bfloat16)]
-    if not last:
-        out_specs.append(whole)
-        out_shape.append(jax.ShapeDtypeStruct((planes, rows, lanes), jnp.float32))
+    out_shape = [jax.ShapeDtypeStruct((owners, count, planes, strip, lanes), jnp.bfloat16)]
+    out_specs.append(whole)
+    out_shape.append(jax.ShapeDtypeStruct((planes, rows, lanes), jnp.float32))
 
     def body(*refs):
-        register_body(first, count, frames, last, *refs)
+        register_body(first, count, frames, *refs)
 
     return pl.pallas_call(
         body,
         grid_spec=pltpu.PrefetchScalarGridSpec(
             num_scalar_prefetch=1,
-            grid=(steps,),
+            grid=(count,),
             in_specs=in_specs,
             out_specs=tuple(out_specs),
             scratch_shapes=[
@@ -263,7 +247,6 @@
         ),
         out_shape=tuple(out_shape),
         compiler_params=pltpu.CompilerParams(vmem_limit_bytes=VMEM),
-        name=f"register_{first}",
     )(meta, *operands)
 
 
@@ -299,15 +282,12 @@
 
 
 def filter_body(group, kernel_ref, rowsum_ref, *refs):
-    *got, out_ref, template_ref = refs
+    *got, out_ref = refs
     owners = got[0].shape[0]
     total, _, strip, lanes = out_ref.shape
     frames = group * (total // owners)
     width = frames * SUB
     reach = -(-TAPS // frames)
-
-    sent = got[-1][:, CHUNKS[-1], 0].astype(jnp.float32)
-    template_ref[0] = jnp.sum(sent, axis=0) * (1.0 / total)
 
     for pair in range(strip // (2 * SUB)):
         tiles = []
@@ -355,21 +335,15 @@
         body,
         grid=(planes,),
         in_specs=in_specs,
-        out_specs=(
-            pl.BlockSpec((total, 1, strip, lanes), lambda z: (0, z, 0, 0)),
-            pl.BlockSpec((1, strip, lanes), lambda z: (z, 0, 0)),
-        ),
-        out_shape=(
-            jax.ShapeDtypeStruct((total, planes, strip, lanes), jnp.bfloat16),
-            jax.ShapeDtypeStruct((planes, strip, lanes), jnp.float32),
-        ),
+        out_specs=pl.BlockSpec((total, 1, strip, lanes), lambda z: (0, z, 0, 0)),
+        out_shape=jax.ShapeDtypeStruct((total, planes, strip, lanes), jnp.bfloat16),
         compiler_params=pltpu.CompilerParams(vmem_limit_bytes=VMEM),
         name="filter_frames",
     )(kernel, rowsum, *got)
 
 
 def local(raw, offsets, taps):
-    frame_dev, planes, rows, lanes = raw.shape
+    frame_dev, _, _, _ = raw.shape
     owners = lax.axis_size("frames")
     tiles = lax.axis_size("tiles")
     total = frame_dev * owners
@@ -396,14 +370,37 @@
     got = []
     summed = None
     low = 0
-    for number, count in enumerate(CHUNKS):
-        is_last = number == len(CHUNKS) - 1
-        made = register(raw, left, right, meta, summed, low, count, owners, is_last)
-        if not is_last:
-            summed = made[1]
-        got.append(lax.all_to_all(made[0], "frames", split_axis=0, concat_axis=0, tiled=True))
+    for count in CHUNKS:
+        sent, summed = register(raw, left, right, meta, summed, low, count, owners)
+        got.append(lax.all_to_all(sent, "frames", split_axis=0, concat_axis=0, tiled=True))
         low += count
-    return filter_frames(kernel, rowsum, got, total, group)
+    template = summed_over_frames(summed, owners) * (1.0 / total)
+    return filter_frames(kernel, rowsum, got, total, group), template
+
+
+def summed_over_frames(value, owners):
+    planes, rows, lanes = value.shape
+    ring = owners // 4
+    value = value.reshape(planes, ring, 2, 2, rows // owners, lanes)
+    index = lax.axis_index("frames")
+
+    def block(array, axis, at):
+        return lax.dynamic_index_in_dim(array, at, axis, keepdims=False)
+
+    core = index % 2
+    other = lax.ppermute(block(value, 3, 1 - core), "frames", [(i, i ^ 1) for i in range(owners)])
+    value = block(value, 3, core) + other
+    pair = index // 2 % 2
+    sent = block(value, 2, 1 - pair).astype(jnp.bfloat16)
+    other = lax.ppermute(sent, "frames", [(i, i ^ 2) for i in range(owners)])
+    value = block(value, 2, pair) + other.astype(jnp.float32)
+    place = index // 4
+    whole = block(value, 1, place)
+    for turn in range(1, ring):
+        sent = block(value, 1, (place + turn) % ring).astype(jnp.bfloat16)
+        other = lax.ppermute(sent, "frames", [(i, (i + 4 * turn) % owners) for i in range(owners)])
+        whole = whole + other.astype(jnp.float32)
+    return whole
 
 
 def solution(mesh):

time: 174 us -> 177 us (1.017)
  starting transfers between devices: 16.2 us -> 23.9 us
  waiting for transfers between devices: 90.6 us -> 83 us
  local copies, waits for them, and re-layouts: 2.77 us -> 4.81 us
    all_to_all x2, waiting for transfers between devices: 80.2 us -> 0.01 us  [local(): lax.all_to_all(sent, 'frames', split_axis=0, concat_axis=0, tiled=True)]
    ppermute x0 -> x5, waiting for transfers between devices: none -> 72.7 us  [the longest x1 70.3 us: summed_over_frames(): other = lax.ppermute(sent, 'frames', [(i, i ^ 2) for i in range(owners)])]
    ppermute x0 -> x5, starting transfers between devices: none -> 7.72 us  [the longest x3 5.38 us: summed_over_frames(): lax.ppermute(sent, 'frames', [(i, (i + 4 * turn) % owners) for i in range...]
    dynamic_slice x0 -> x2, local copies, waits for them, and re-layouts: none -> 1.86 us  [block(): return lax.dynamic_index_in_dim(array, at, axis, keepdims=False)]
  transfers between devices with their start and end apart: 4 -> 9, of which waited for: 3 -> 4; matrix products, arithmetic and copies ran while one was open for 1% -> 2% of each run, Pallas kernels for 18% -> 18%
where the time goes in v3:
time: 177 us
  waiting for transfers between devices  83 us (47%)
  Pallas kernels  62.5 us (35%)
  starting transfers between devices  23.9 us (14%)
  local copies, waits for them, and re-layouts  4.81 us (3%)
    ppermute x1, waiting for transfers between devices, summed_over_frames(): other = lax.ppermute(sent, 'frames', [(i, i ^ 2) for i in range(owners)])  70.3 us
    pallas_call x2, Pallas kernels, register(): pl.pallas_call(body, grid_spec=pltpu.PrefetchScalarGridSpec(num_scalar_pr...  40.5 us
    pallas_call x1, Pallas kernels, filter_frames(): pl.pallas_call(body, grid=(planes,), in_specs=in_specs, out_specs=pl.Bloc...  12.2 us
    all_to_all x2, starting transfers between devices, local(): lax.all_to_all(sent, 'frames', split_axis=0, concat_axis=0, tiled=True)  10.4 us
    ppermute x1, waiting for transfers between devices, local(): right = lax.ppermute(first_columns, 'tiles', [(j, i) for i, j in upward])  6.9 us
    pallas_call x1, Pallas kernels, pack_edges(): pl.pallas_call(pack_body, grid=(frames // each,), in_specs=[pl.BlockSpec(...  6.5 us
    ppermute x3, starting transfers between devices, summed_over_frames(): lax.ppermute(sent, 'frames', [(i, (i + 4 * turn) % owners) for i in range...  5.38 us
    ppermute x1, starting transfers between devices, local(): left = lax.ppermute(last_columns, 'tiles', upward)  3.55 us
  transfers between devices with their start and end apart: 9, of which 4 were waited for; matrix products, arithmetic and copies ran while one was open for 2% of the time, Pallas kernels for 18%

profile of v3, /device:TPU:96, one launch (start us, length us, event | category | flops | bytes accessed | tf_op | source)
XLA Modules:
  0.0 176.7 jit_solution(10471212281117285216)
XLA Ops:
  0.6 6.5 %pack_edges.1 = (bf16[2,512,128]{2,1,0:T(8,128)(2,1)}, bf16[2,512,128]{2,1,0:T(8,128)(2,1)}) custom-call(bf16[8,8,512,128]{3,2,1,0:T(8,128)(2,1)} %refs_1_.5, bf16[8,8,512,128]{3,2,1,0:T(8,128)(2,1)} %refs_1_.5), custom_call_target="tpu_custom_call" | custom-call | tf_op jit(solution)/shard_map/pack_edges/pallas_call | solution.py:68
  7.1 3.6 %collective-permute-start = (bf16[2,512,128]{2,1,0:T(8,128)(2,1)}, bf16[2,512,128]{2,1,0:T(8,128)(2,1)S(1)}, u32[]{:S(2)}, u32[]{:S(2)}) collective-permute-start(bf16[2,512,128]{2,1,0:T(8,128)(2,1)} %get-tuple-element.12), channel_id=1, source_target_pairs={{0,1},{1,2},{2,3},{3,4},{4,5},{5,6},{6,7},{8,9},{9,10},{10,11},{11... | collective-permute-start | bytes 786440 | tf_op jit(solution)/shard_map/ppermute | solution.py:354
  10.7 2.3 %collective-permute-start.1 = (bf16[2,512,128]{2,1,0:T(8,128)(2,1)}, bf16[2,512,128]{2,1,0:T(8,128)(2,1)S(1)}, u32[]{:S(2)}, u32[]{:S(2)}) collective-permute-start(bf16[2,512,128]{2,1,0:T(8,128)(2,1)} %get-tuple-element.13), channel_id=1, source_target_pairs={{1,0},{2,1},{3,2},{4,3},{5,4},{6,5},{7,6},{9,8},{10,9},{11,10},{12... | collective-permute-start | bytes 786440 | tf_op jit(solution)/shard_map/ppermute | solution.py:355
  13.2 0.6 pad_add_fusion.refs_0_
  13.8 3.4 %collective-permute-done.refs_2_ = bf16[2,512,128]{2,1,0:T(8,128)(2,1)S(1)} collective-permute-done((bf16[2,512,128]{2,1,0:T(8,128)(2,1)}, bf16[2,512,128]{2,1,0:T(8,128)(2,1)S(1)}, u32[]{:S(2)}, u32[]{:S(2)}) %collective-permute-start) | collective-permute-done | bytes 262176 | tf_op jit(solution)/shard_map/ppermute | solution.py:354
  17.3 6.9 %collective-permute-done.1.refs_3_ = bf16[2,512,128]{2,1,0:T(8,128)(2,1)S(1)} collective-permute-done((bf16[2,512,128]{2,1,0:T(8,128)(2,1)}, bf16[2,512,128]{2,1,0:T(8,128)(2,1)S(1)}, u32[]{:S(2)}, u32[]{:S(2)}) %collective-permute-start.1) | collective-permute-done | bytes 262176 | tf_op jit(solution)/shard_map/ppermute | solution.py:355
  24.2 0.7 copy-done.2
  24.9 12.0 %shard_map.59 = (bf16[16,2,8,32,128]{4,3,2,1,0:T(8,128)(2,1)}, f32[8,512,128]{2,1,0:T(8,128)}) custom-call(s32[26]{0:T(128)} %pad_add_fusion.refs_0_, bf16[8,8,512,128]{3,2,1,0:T(8,128)(2,1)} %refs_1_.5, bf16[2,512,128]{2,1,0:T(8,128)(2,1)} %copy-done.1, bf16[2,512,128]{2,1,0:T(8,128)(2,1)} %copy-done.2), custom_call_target="tpu_custom_call" | custom-call | tf_op jit(solution)/shard_map/pallas_call | solution.py:232
  36.9 4.6 %all-to-all-start = ((bf16[16,2,8,32,128]{4,3,2,1,0:T(8,128)(2,1)}), bf16[16,2,8,32,128]{4,3,2,1,0:T(8,128)(2,1)S(1)}, u32[]{:S(2)}, u32[]{:S(2)}) async-start(bf16[16,2,8,32,128]{4,3,2,1,0:T(8,128)(2,1)} %get-tuple-element.14), calls=%async_computation | async-start | bytes 4194304 | tf_op jit(solution)/shard_map/all_to_all | solution.py:375
  41.5 28.6 %shard_map.60 = (bf16[16,6,8,32,128]{4,3,2,1,0:T(8,128)(2,1)}, f32[8,512,128]{2,1,0:T(8,128)}) custom-call(s32[26]{0:T(128)} %pad_add_fusion.refs_0_, bf16[8,8,512,128]{3,2,1,0:T(8,128)(2,1)} %refs_1_.5, bf16[2,512,128]{2,1,0:T(8,128)(2,1)} %copy-done.1, bf16[2,512,128]{2,1,0:T(8,128)(2,1)} %copy-done.2, f32[8,512,128]{2,1,0:T(8,128)} %get-tuple-element.15.refs_4_), custom_call_target="tpu_custom_call" | custom-call | tf_op jit(solution)/shard_map/pallas_call | solution.py:232
  70.1 1.4 copy-done
  71.5 5.8 %all-to-all-start.1 = ((bf16[16,6,8,32,128]{4,3,2,1,0:T(8,128)(2,1)}), bf16[16,6,8,32,128]{4,3,2,1,0:T(8,128)(2,1)}, u32[]{:S(2)}, u32[]{:S(2)}) async-start(bf16[16,6,8,32,128]{4,3,2,1,0:T(8,128)(2,1)} %get-tuple-element.16), calls=%async_computation.1 | async-start | bytes 12582912 | tf_op jit(solution)/shard_map/all_to_all | solution.py:375
  77.2 1.8 %constant_dynamic-slice_fusion.1 = (f32[8,4,2,1,32,128]{5,4,3,2,1,0:T(8,128)S(1)}, f32[8,4,2,1,32,128]{5,4,3,2,1,0:T(8,128)S(1)}) fusion(f32[8,4,2,2,32,128]{5,4,3,2,1,0:T(8,128)} %bitcast.26, s32[]{:T(128)S(6)} %select_n.58, s32[]{:T(128)S(6)} %select_n.59), kind=kLoop, calls=%fused_computation.16 | loop fusion | bytes 4194312 | tf_op jit(solution)/shard_map/jit(dynamic_index_in_dim)/dynamic_slice | solution.py:388
  79.1 0.4 collective-permute-start.2
  79.5 2.3 %collective-permute-done.2 = f32[8,4,2,32,128]{4,3,0,1,2:T(8,128)S(1)} collective-permute-done((f32[8,4,2,32,128]{4,3,0,1,2:T(8,128)S(1)}, f32[8,4,2,32,128]{4,3,0,1,2:T(8,128)S(1)}, u32[]{:S(2)}, u32[]{:S(2)}) %collective-permute-start.2) | collective-permute-done | bytes 1048608 | tf_op jit(solution)/shard_map/ppermute | solution.py:391
  82.1 1.9 %collective-permute-start.3 = (bf16[8,4,32,128]{3,2,0,1:T(8,128)(2,1)S(1)}, bf16[8,4,32,128]{3,2,0,1:T(8,128)(2,1)S(1)}, u32[]{:S(2)}, u32[]{:S(2)}) collective-permute-start(bf16[8,4,32,128]{3,2,0,1:T(8,128)(2,1)S(1)} %fusion), channel_id=1, source_target_pairs={{0,16},{8,24},{16,0},{24,8},{32,48},{40,56},{48,32},{56,40},{64,80... | collective-permute-start | bytes 786440 | tf_op jit(solution)/shard_map/ppermute | solution.py:395
  84.1 70.3 %collective-permute-done.3 = bf16[8,4,32,128]{3,2,0,1:T(8,128)(2,1)S(1)} collective-permute-done((bf16[8,4,32,128]{3,2,0,1:T(8,128)(2,1)S(1)}, bf16[8,4,32,128]{3,2,0,1:T(8,128)(2,1)S(1)}, u32[]{:S(2)}, u32[]{:S(2)}) %collective-permute-start.3) | collective-permute-done | bytes 262176 | tf_op jit(solution)/shard_map/ppermute | solution.py:395
  154.5 0.6 collective-permute-start.4
  155.1 2.7 %collective-permute-start.5 = (bf16[8,32,128]{2,1,0:T(8,128)(2,1)S(1)}, bf16[8,32,128]{2,1,0:T(8,128)(2,1)S(1)}, u32[]{:S(2)}, u32[]{:S(2)}) collective-permute-start(bf16[8,32,128]{2,1,0:T(8,128)(2,1)S(1)} %get-tuple-element.22), channel_id=1, source_target_pairs={{0,64},{8,72},{16,80},{24,88},{32,96},{40,104},{48,112},{56,120},{... | collective-permute-start | bytes 196616 | tf_op jit(solution)/shard_map/ppermute | solution.py:401
  157.8 2.1 %collective-permute-start.6 = (bf16[8,32,128]{2,1,0:T(8,128)(2,1)S(1)}, bf16[8,32,128]{2,1,0:T(8,128)(2,1)S(1)}, u32[]{:S(2)}, u32[]{:S(2)}) collective-permute-start(bf16[8,32,128]{2,1,0:T(8,128)(2,1)S(1)} %get-tuple-element.21), channel_id=1, source_target_pairs={{0,96},{8,104},{16,112},{24,120},{32,0},{40,8},{48,16},{56,24},{64... | collective-permute-start | bytes 196616 | tf_op jit(solution)/shard_map/ppermute | solution.py:401
  159.9 0.6 tile.2.order_ref
  160.5 3.3 %spread_kernel.1 = (bf16[1024,1024]{1,0:T(8,128)(2,1)}, f32[1024,128]{1,0:T(8,128)}) custom-call(f32[64]{0:T(128)} %taps_ref.1, s32[8,128]{1,0:T(8,128)} %tile.2.order_ref), custom_call_target="tpu_custom_call" | custom-call | tf_op jit(solution)/shard_map/spread_kernel/pallas_call | solution.py:272
  163.8 0.7 fusion.3
  164.5 12.2 %filter_frames.1 = bf16[128,8,32,128]{3,2,1,0:T(8,128)(2,1)} custom-call(bf16[1024,1024]{1,0:T(8,128)(2,1)} %get-tuple-element.10.refs_0_, f32[1024,128]{1,0:T(8,128)} %get-tuple-element.11.refs_1_, bf16[16,2,8,32,128]{4,3,2,1,0:T(8,128)(2,1)} %copy-done, bf16[16,6,8,32,128]{4,3,2,1,0:T(8,128)(2,1)} %all-to-all-done.1.refs_3_), custom_call_target="tpu_custom_call" | custom-call | tf_op jit(solution)/shard_map/filter_frames/pallas_call | solution.py:334
  (21 shorter events, 0.7 us)
Async XLA Ops:
  0.6 12.4 %copy-start.3 = (s32[8,3]{0,1:T(4,128)S(1)}, s32[8,3]{0,1:T(4,128)}, u32[]{:S(2)}) copy-start(s32[8,3]{0,1:T(4,128)} %param.5) | copy-start | bytes 292
  7.1 10.1 %collective-permute-start = (bf16[2,512,128]{2,1,0:T(8,128)(2,1)}, bf16[2,512,128]{2,1,0:T(8,128)(2,1)S(1)}, u32[]{:S(2)}, u32[]{:S(2)}) collective-permute-start(bf16[2,512,128]{2,1,0:T(8,128)(2,1)} %get-tuple-element.12), channel_id=1, source_target_pairs={{0,1},{1,2},{2,3},{3,4},{4,5},{5,6},{6,7},{8,9},{9,10},{10,11},{11... | collective-permute-start | bytes 786440 | tf_op jit(solution)/shard_map/ppermute | solution.py:354
  10.7 13.5 %collective-permute-start.1 = (bf16[2,512,128]{2,1,0:T(8,128)(2,1)}, bf16[2,512,128]{2,1,0:T(8,128)(2,1)S(1)}, u32[]{:S(2)}, u32[]{:S(2)}) collective-permute-start(bf16[2,512,128]{2,1,0:T(8,128)(2,1)} %get-tuple-element.13), channel_id=1, source_target_pairs={{1,0},{2,1},{3,2},{4,3},{5,4},{6,5},{7,6},{9,8},{10,9},{11,10},{12... | collective-permute-start | bytes 786440 | tf_op jit(solution)/shard_map/ppermute | solution.py:355
  17.3 6.9 %copy-start.1 = (bf16[2,512,128]{2,1,0:T(8,128)(2,1)}, bf16[2,512,128]{2,1,0:T(8,128)(2,1)S(1)}, u32[]{:S(2)}) copy-start(bf16[2,512,128]{2,1,0:T(8,128)(2,1)S(1)} %collective-permute-done.refs_2_) | copy-start | bytes 786436
  24.2 0.7 copy-start.2
  36.9 33.2 %all-to-all-start = ((bf16[16,2,8,32,128]{4,3,2,1,0:T(8,128)(2,1)}), bf16[16,2,8,32,128]{4,3,2,1,0:T(8,128)(2,1)S(1)}, u32[]{:S(2)}, u32[]{:S(2)}) async-start(bf16[16,2,8,32,128]{4,3,2,1,0:T(8,128)(2,1)} %get-tuple-element.14), calls=%async_computation | async-start | bytes 4194304 | tf_op jit(solution)/shard_map/all_to_all | solution.py:375
  70.1 1.4 copy-start
  71.5 93.0 %all-to-all-start.1 = ((bf16[16,6,8,32,128]{4,3,2,1,0:T(8,128)(2,1)}), bf16[16,6,8,32,128]{4,3,2,1,0:T(8,128)(2,1)}, u32[]{:S(2)}, u32[]{:S(2)}) async-start(bf16[16,6,8,32,128]{4,3,2,1,0:T(8,128)(2,1)} %get-tuple-element.16), calls=%async_computation.1 | async-start | bytes 12582912 | tf_op jit(solution)/shard_map/all_to_all | solution.py:375
  79.1 2.7 %collective-permute-start.2 = (f32[8,4,2,32,128]{4,3,0,1,2:T(8,128)S(1)}, f32[8,4,2,32,128]{4,3,0,1,2:T(8,128)S(1)}, u32[]{:S(2)}, u32[]{:S(2)}) collective-permute-start(f32[8,4,2,32,128]{4,3,0,1,2:T(8,128)S(1)} %bitcast.27), channel_id=1, source_target_pairs={{0,8},{8,0},{16,24},{24,16},{32,40},{40,32},{48,56},{56,48},{64,72... | collective-permute-start | bytes 3145736 | tf_op jit(solution)/shard_map/ppermute | solution.py:391
  81.9 78.0 %copy-start.4 = (s32[128]{0:T(128)S(1)}, s32[128]{0:T(128)}, u32[]{:S(2)}) copy-start(s32[128]{0:T(128)} %constant.96.clone) | copy-start | bytes 1540
  82.1 72.3 %collective-permute-start.3 = (bf16[8,4,32,128]{3,2,0,1:T(8,128)(2,1)S(1)}, bf16[8,4,32,128]{3,2,0,1:T(8,128)(2,1)S(1)}, u32[]{:S(2)}, u32[]{:S(2)}) collective-permute-start(bf16[8,4,32,128]{3,2,0,1:T(8,128)(2,1)S(1)} %fusion), channel_id=1, source_target_pairs={{0,16},{8,24},{16,0},{24,8},{32,48},{40,56},{48,32},{56,40},{64,80... | collective-permute-start | bytes 786440 | tf_op jit(solution)/shard_map/ppermute | solution.py:395
  154.5 9.3 %collective-permute-start.4 = (bf16[8,32,128]{2,1,0:T(8,128)(2,1)S(1)}, bf16[8,32,128]{2,1,0:T(8,128)(2,1)S(1)}, u32[]{:S(2)}, u32[]{:S(2)}) collective-permute-start(bf16[8,32,128]{2,1,0:T(8,128)(2,1)S(1)} %get-tuple-element.20), channel_id=1, source_target_pairs={{0,32},{8,40},{16,48},{24,56},{32,64},{40,72},{48,80},{56,88},{64,... | collective-permute-start | bytes 196616 | tf_op jit(solution)/shard_map/ppermute | solution.py:401
  155.1 8.7 %collective-permute-start.5 = (bf16[8,32,128]{2,1,0:T(8,128)(2,1)S(1)}, bf16[8,32,128]{2,1,0:T(8,128)(2,1)S(1)}, u32[]{:S(2)}, u32[]{:S(2)}) collective-permute-start(bf16[8,32,128]{2,1,0:T(8,128)(2,1)S(1)} %get-tuple-element.22), channel_id=1, source_target_pairs={{0,64},{8,72},{16,80},{24,88},{32,96},{40,104},{48,112},{56,120},{... | collective-permute-start | bytes 196616 | tf_op jit(solution)/shard_map/ppermute | solution.py:401
  157.8 6.0 %collective-permute-start.6 = (bf16[8,32,128]{2,1,0:T(8,128)(2,1)S(1)}, bf16[8,32,128]{2,1,0:T(8,128)(2,1)S(1)}, u32[]{:S(2)}, u32[]{:S(2)}) collective-permute-start(bf16[8,32,128]{2,1,0:T(8,128)(2,1)S(1)} %get-tuple-element.21), channel_id=1, source_target_pairs={{0,96},{8,104},{16,112},{24,120},{32,0},{40,8},{48,16},{56,24},{64... | collective-permute-start | bytes 196616 | tf_op jit(solution)/shard_map/ppermute | solution.py:401

commit v4 on v3

--- a/solution.py
+++ b/solution.py
@@ -380,25 +380,21 @@
 
 def summed_over_frames(value, owners):
     planes, rows, lanes = value.shape
-    ring = owners // 4
-    value = value.reshape(planes, ring, 2, 2, rows // owners, lanes)
+    chips = owners // 2
+    value = value.reshape(planes, chips, 2, rows // owners, lanes)
     index = lax.axis_index("frames")
+    chip, core = lax.shift_right_logical(index, 1), lax.bitwise_and(index, 1)
 
     def block(array, axis, at):
         return lax.dynamic_index_in_dim(array, at, axis, keepdims=False)
 
-    core = index % 2
-    other = lax.ppermute(block(value, 3, 1 - core), "frames", [(i, i ^ 1) for i in range(owners)])
-    value = block(value, 3, core) + other
-    pair = index // 2 % 2
-    sent = block(value, 2, 1 - pair).astype(jnp.bfloat16)
-    other = lax.ppermute(sent, "frames", [(i, i ^ 2) for i in range(owners)])
-    value = block(value, 2, pair) + other.astype(jnp.float32)
-    place = index // 4
-    whole = block(value, 1, place)
-    for turn in range(1, ring):
-        sent = block(value, 1, (place + turn) % ring).astype(jnp.bfloat16)
-        other = lax.ppermute(sent, "frames", [(i, (i + 4 * turn) % owners) for i in range(owners)])
+    other = lax.ppermute(block(value, 2, 1 - core), "frames", [(i, i ^ 1) for i in range(owners)])
+    value = block(value, 2, core) + other
+    whole = block(value, 1, chip)
+    for turn in range(1, chips):
+        to = lax.bitwise_and(chip + turn, chips - 1)
+        sent = block(value, 1, to).astype(jnp.bfloat16)
+        other = lax.ppermute(sent, "frames", [(i, (i + 2 * turn) % owners) for i in range(owners)])
         whole = whole + other.astype(jnp.float32)
     return whole
 

time: 177 us -> 172 us (0.972)
  waiting for transfers between devices: 83 us -> 72.1 us
  starting transfers between devices: 23.9 us -> 29.2 us
    ppermute x5 -> x8, waiting for transfers between devices: 72.7 us -> 61.8 us  [the longest x7 59.5 us: summed_over_frames(): lax.ppermute(sent, 'frames', [(i, (i + 2 * turn) % owners) for i in range...]
    ppermute x5 -> x8, starting transfers between devices: 7.72 us -> 13 us  [the longest x7 12.5 us: summed_over_frames(): lax.ppermute(sent, 'frames', [(i, (i + 2 * turn) % owners) for i in range...]
  transfers between devices with their start and end apart: 9 -> 12, of which waited for: 4 -> 4; matrix products, arithmetic and copies ran while one was open for 2% -> 3% of each run, Pallas kernels for 18% -> 19%
where the time goes in v4:
time: 172 us; the launch traced here: 171 us
  waiting for transfers between devices  72.1 us (42%)
  Pallas kernels  62.5 us (36%)
  starting transfers between devices  29.2 us (17%)
  local copies, waits for them, and re-layouts  4.86 us (3%)
    ppermute x7, waiting for transfers between devices, summed_over_frames(): lax.ppermute(sent, 'frames', [(i, (i + 2 * turn) % owners) for i in range...  59.5 us
    pallas_call x2, Pallas kernels, register(): pl.pallas_call(body, grid_spec=pltpu.PrefetchScalarGridSpec(num_scalar_pr...  40.5 us
    ppermute x7, starting transfers between devices, summed_over_frames(): lax.ppermute(sent, 'frames', [(i, (i + 2 * turn) % owners) for i in range...  12.5 us
    pallas_call x1, Pallas kernels, filter_frames(): pl.pallas_call(body, grid=(planes,), in_specs=in_specs, out_specs=pl.Bloc...  12.2 us
    all_to_all x2, starting transfers between devices, local(): lax.all_to_all(sent, 'frames', split_axis=0, concat_axis=0, tiled=True)  10.4 us
    ppermute x1, waiting for transfers between devices, local(): right = lax.ppermute(first_columns, 'tiles', [(j, i) for i, j in upward])  6.9 us
    pallas_call x1, Pallas kernels, pack_edges(): pl.pallas_call(pack_body, grid=(frames // each,), in_specs=[pl.BlockSpec(...  6.5 us
    ppermute x1, starting transfers between devices, local(): left = lax.ppermute(last_columns, 'tiles', upward)  3.55 us
  transfers between devices with their start and end apart: 12, of which 4 were waited for; matrix products, arithmetic and copies ran while one was open for 3% of the time, Pallas kernels for 19%

profile of v4, /device:TPU:96, one launch (start us, length us, event | category | flops | bytes accessed | tf_op | source)
XLA Modules:
  0.0 171.1 jit_solution(18104396217828765337)
XLA Ops:
  0.6 6.5 %pack_edges.1 = (bf16[2,512,128]{2,1,0:T(8,128)(2,1)}, bf16[2,512,128]{2,1,0:T(8,128)(2,1)}) custom-call(bf16[8,8,512,128]{3,2,1,0:T(8,128)(2,1)} %refs_1_.5, bf16[8,8,512,128]{3,2,1,0:T(8,128)(2,1)} %refs_1_.5), custom_call_target="tpu_custom_call" | custom-call | tf_op jit(solution)/shard_map/pack_edges/pallas_call | solution.py:68
  7.1 3.6 %collective-permute-start = (bf16[2,512,128]{2,1,0:T(8,128)(2,1)}, bf16[2,512,128]{2,1,0:T(8,128)(2,1)S(1)}, u32[]{:S(2)}, u32[]{:S(2)}) collective-permute-start(bf16[2,512,128]{2,1,0:T(8,128)(2,1)} %get-tuple-element.12), channel_id=1, source_target_pairs={{0,1},{1,2},{2,3},{3,4},{4,5},{5,6},{6,7},{8,9},{9,10},{10,11},{11... | collective-permute-start | bytes 786440 | tf_op jit(solution)/shard_map/ppermute | solution.py:354
  10.7 2.3 %collective-permute-start.1 = (bf16[2,512,128]{2,1,0:T(8,128)(2,1)}, bf16[2,512,128]{2,1,0:T(8,128)(2,1)S(1)}, u32[]{:S(2)}, u32[]{:S(2)}) collective-permute-start(bf16[2,512,128]{2,1,0:T(8,128)(2,1)} %get-tuple-element.13), channel_id=1, source_target_pairs={{1,0},{2,1},{3,2},{4,3},{5,4},{6,5},{7,6},{9,8},{10,9},{11,10},{12... | collective-permute-start | bytes 786440 | tf_op jit(solution)/shard_map/ppermute | solution.py:355
  13.8 3.4 %collective-permute-done.refs_2_ = bf16[2,512,128]{2,1,0:T(8,128)(2,1)S(1)} collective-permute-done((bf16[2,512,128]{2,1,0:T(8,128)(2,1)}, bf16[2,512,128]{2,1,0:T(8,128)(2,1)S(1)}, u32[]{:S(2)}, u32[]{:S(2)}) %collective-permute-start) | collective-permute-done | bytes 262176 | tf_op jit(solution)/shard_map/ppermute | solution.py:354
  17.3 6.9 %collective-permute-done.1.refs_3_ = bf16[2,512,128]{2,1,0:T(8,128)(2,1)S(1)} collective-permute-done((bf16[2,512,128]{2,1,0:T(8,128)(2,1)}, bf16[2,512,128]{2,1,0:T(8,128)(2,1)S(1)}, u32[]{:S(2)}, u32[]{:S(2)}) %collective-permute-start.1) | collective-permute-done | bytes 262176 | tf_op jit(solution)/shard_map/ppermute | solution.py:355
  24.2 0.7 copy-done.2
  24.9 12.0 %shard_map.59 = (bf16[16,2,8,32,128]{4,3,2,1,0:T(8,128)(2,1)}, f32[8,512,128]{2,1,0:T(8,128)}) custom-call(s32[26]{0:T(128)} %pad_add_fusion.refs_0_, bf16[8,8,512,128]{3,2,1,0:T(8,128)(2,1)} %refs_1_.5, bf16[2,512,128]{2,1,0:T(8,128)(2,1)} %copy-done.1, bf16[2,512,128]{2,1,0:T(8,128)(2,1)} %copy-done.2), custom_call_target="tpu_custom_call" | custom-call | tf_op jit(solution)/shard_map/pallas_call | solution.py:232
  36.9 4.6 %all-to-all-start = ((bf16[16,2,8,32,128]{4,3,2,1,0:T(8,128)(2,1)}), bf16[16,2,8,32,128]{4,3,2,1,0:T(8,128)(2,1)S(1)}, u32[]{:S(2)}, u32[]{:S(2)}) async-start(bf16[16,2,8,32,128]{4,3,2,1,0:T(8,128)(2,1)} %get-tuple-element.14), calls=%async_computation | async-start | bytes 4194304 | tf_op jit(solution)/shard_map/all_to_all | solution.py:375
  41.5 28.6 %shard_map.60 = (bf16[16,6,8,32,128]{4,3,2,1,0:T(8,128)(2,1)}, f32[8,512,128]{2,1,0:T(8,128)}) custom-call(s32[26]{0:T(128)} %pad_add_fusion.refs_0_, bf16[8,8,512,128]{3,2,1,0:T(8,128)(2,1)} %refs_1_.5, bf16[2,512,128]{2,1,0:T(8,128)(2,1)} %copy-done.1, bf16[2,512,128]{2,1,0:T(8,128)(2,1)} %copy-done.2, f32[8,512,128]{2,1,0:T(8,128)} %get-tuple-element.15.refs_4_), custom_call_target="tpu_custom_call" | custom-call | tf_op jit(solution)/shard_map/pallas_call | solution.py:232
  70.1 1.4 copy-done
  71.5 5.7 %all-to-all-start.1 = ((bf16[16,6,8,32,128]{4,3,2,1,0:T(8,128)(2,1)}), bf16[16,6,8,32,128]{4,3,2,1,0:T(8,128)(2,1)}, u32[]{:S(2)}, u32[]{:S(2)}) async-start(bf16[16,6,8,32,128]{4,3,2,1,0:T(8,128)(2,1)} %get-tuple-element.16), calls=%async_computation.1 | async-start | bytes 12582912 | tf_op jit(solution)/shard_map/all_to_all | solution.py:375
  77.2 1.8 %constant_dynamic-slice_fusion.1 = (f32[8,8,1,32,128]{4,3,2,1,0:T(8,128)S(1)}, f32[8,8,1,32,128]{4,3,2,1,0:T(8,128)S(1)}) fusion(f32[8,8,2,32,128]{4,3,2,1,0:T(8,128)} %bitcast.38, s32[]{:T(128)S(6)} %select_n.32, s32[]{:T(128)S(6)} %select_n.33), kind=kLoop, calls=%fused_computation.25 | loop fusion | bytes 4194312 | tf_op jit(solution)/shard_map/jit(dynamic_index_in_dim)/dynamic_slice | solution.py:389
  79.6 2.3 %collective-permute-done.2 = f32[8,8,32,128]{3,2,0,1:T(8,128)S(1)} collective-permute-done((f32[8,8,32,128]{3,2,0,1:T(8,128)S(1)}, f32[8,8,32,128]{3,2,0,1:T(8,128)S(1)}, u32[]{:S(2)}, u32[]{:S(2)}) %collective-permute-start.2) | collective-permute-done | bytes 1048608 | tf_op jit(solution)/shard_map/ppermute | solution.py:391
  82.2 1.9 %collective-permute-start.3 = (bf16[8,32,128]{2,1,0:T(8,128)(2,1)S(1)}, bf16[8,32,128]{2,1,0:T(8,128)(2,1)S(1)}, u32[]{:S(2)}, u32[]{:S(2)}) collective-permute-start(bf16[8,32,128]{2,1,0:T(8,128)(2,1)S(1)} %get-tuple-element.20), channel_id=1, source_target_pairs={{0,16},{8,24},{16,32},{24,40},{32,48},{40,56},{48,64},{56,72},{64,... | collective-permute-start | bytes 196616 | tf_op jit(solution)/shard_map/ppermute | solution.py:397
  84.1 1.5 collective-permute-start.4
  85.6 2.1 %collective-permute-start.5 = (bf16[8,32,128]{2,1,0:T(8,128)(2,1)S(1)}, bf16[8,32,128]{2,1,0:T(8,128)(2,1)S(1)}, u32[]{:S(2)}, u32[]{:S(2)}) collective-permute-start(bf16[8,32,128]{2,1,0:T(8,128)(2,1)S(1)} %get-tuple-element.25), channel_id=1, source_target_pairs={{0,48},{8,56},{16,64},{24,72},{32,80},{40,88},{48,96},{56,104},{64... | collective-permute-start | bytes 196616 | tf_op jit(solution)/shard_map/ppermute | solution.py:397
  87.7 2.1 %collective-permute-start.6 = (bf16[8,32,128]{2,1,0:T(8,128)(2,1)S(1)}, bf16[8,32,128]{2,1,0:T(8,128)(2,1)S(1)}, u32[]{:S(2)}, u32[]{:S(2)}) collective-permute-start(bf16[8,32,128]{2,1,0:T(8,128)(2,1)S(1)} %get-tuple-element.24), channel_id=1, source_target_pairs={{0,64},{8,72},{16,80},{24,88},{32,96},{40,104},{48,112},{56,120},{... | collective-permute-start | bytes 196616 | tf_op jit(solution)/shard_map/ppermute | solution.py:397
  89.7 3.0 %collective-permute-start.7 = (bf16[8,32,128]{2,1,0:T(8,128)(2,1)S(1)}, bf16[8,32,128]{2,1,0:T(8,128)(2,1)S(1)}, u32[]{:S(2)}, u32[]{:S(2)}) collective-permute-start(bf16[8,32,128]{2,1,0:T(8,128)(2,1)S(1)} %get-tuple-element.23), channel_id=1, source_target_pairs={{0,80},{8,88},{16,96},{24,104},{32,112},{40,120},{48,0},{56,8},{64... | collective-permute-start | bytes 196616 | tf_op jit(solution)/shard_map/ppermute | solution.py:397
  92.7 59.4 %collective-permute-done.3 = bf16[8,32,128]{2,1,0:T(8,128)(2,1)S(1)} collective-permute-done((bf16[8,32,128]{2,1,0:T(8,128)(2,1)S(1)}, bf16[8,32,128]{2,1,0:T(8,128)(2,1)S(1)}, u32[]{:S(2)}, u32[]{:S(2)}) %collective-permute-start.3) | collective-permute-done | bytes 65568 | tf_op jit(solution)/shard_map/ppermute | solution.py:397
  152.2 1.4 collective-permute-start.8
  153.5 0.7 collective-permute-start.9
  154.8 3.3 %spread_kernel.1 = (bf16[1024,1024]{1,0:T(8,128)(2,1)}, f32[1024,128]{1,0:T(8,128)}) custom-call(f32[64]{0:T(128)} %taps_ref.1, s32[8,128]{1,0:T(8,128)} %tile.2.order_ref), custom_call_target="tpu_custom_call" | custom-call | tf_op jit(solution)/shard_map/spread_kernel/pallas_call | solution.py:272
  158.1 0.7 fusion.6
  158.8 12.2 %filter_frames.1 = bf16[128,8,32,128]{3,2,1,0:T(8,128)(2,1)} custom-call(bf16[1024,1024]{1,0:T(8,128)(2,1)} %get-tuple-element.10.refs_0_, f32[1024,128]{1,0:T(8,128)} %get-tuple-element.11.refs_1_, bf16[16,2,8,32,128]{4,3,2,1,0:T(8,128)(2,1)} %copy-done, bf16[16,6,8,32,128]{4,3,2,1,0:T(8,128)(2,1)} %all-to-all-done.1.refs_3_), custom_call_target="tpu_custom_call" | custom-call | tf_op jit(solution)/shard_map/filter_frames/pallas_call | solution.py:334
  (25 shorter events, 2.3 us)
Async XLA Ops:
  0.6 12.4 %copy-start.3 = (s32[8,3]{0,1:T(4,128)S(1)}, s32[8,3]{0,1:T(4,128)}, u32[]{:S(2)}) copy-start(s32[8,3]{0,1:T(4,128)} %param.5) | copy-start | bytes 292
  7.1 10.1 %collective-permute-start = (bf16[2,512,128]{2,1,0:T(8,128)(2,1)}, bf16[2,512,128]{2,1,0:T(8,128)(2,1)S(1)}, u32[]{:S(2)}, u32[]{:S(2)}) collective-permute-start(bf16[2,512,128]{2,1,0:T(8,128)(2,1)} %get-tuple-element.12), channel_id=1, source_target_pairs={{0,1},{1,2},{2,3},{3,4},{4,5},{5,6},{6,7},{8,9},{9,10},{10,11},{11... | collective-permute-start | bytes 786440 | tf_op jit(solution)/shard_map/ppermute | solution.py:354
  10.7 13.5 %collective-permute-start.1 = (bf16[2,512,128]{2,1,0:T(8,128)(2,1)}, bf16[2,512,128]{2,1,0:T(8,128)(2,1)S(1)}, u32[]{:S(2)}, u32[]{:S(2)}) collective-permute-start(bf16[2,512,128]{2,1,0:T(8,128)(2,1)} %get-tuple-element.13), channel_id=1, source_target_pairs={{1,0},{2,1},{3,2},{4,3},{5,4},{6,5},{7,6},{9,8},{10,9},{11,10},{12... | collective-permute-start | bytes 786440 | tf_op jit(solution)/shard_map/ppermute | solution.py:355
  17.3 6.9 %copy-start.1 = (bf16[2,512,128]{2,1,0:T(8,128)(2,1)}, bf16[2,512,128]{2,1,0:T(8,128)(2,1)S(1)}, u32[]{:S(2)}) copy-start(bf16[2,512,128]{2,1,0:T(8,128)(2,1)S(1)} %collective-permute-done.refs_2_) | copy-start | bytes 786436
  24.2 0.7 copy-start.2
  36.9 33.2 %all-to-all-start = ((bf16[16,2,8,32,128]{4,3,2,1,0:T(8,128)(2,1)}), bf16[16,2,8,32,128]{4,3,2,1,0:T(8,128)(2,1)S(1)}, u32[]{:S(2)}, u32[]{:S(2)}) async-start(bf16[16,2,8,32,128]{4,3,2,1,0:T(8,128)(2,1)} %get-tuple-element.14), calls=%async_computation | async-start | bytes 4194304 | tf_op jit(solution)/shard_map/all_to_all | solution.py:375
  70.1 1.4 copy-start
  71.5 87.4 %all-to-all-start.1 = ((bf16[16,6,8,32,128]{4,3,2,1,0:T(8,128)(2,1)}), bf16[16,6,8,32,128]{4,3,2,1,0:T(8,128)(2,1)}, u32[]{:S(2)}, u32[]{:S(2)}) async-start(bf16[16,6,8,32,128]{4,3,2,1,0:T(8,128)(2,1)} %get-tuple-element.16), calls=%async_computation.1 | async-start | bytes 12582912 | tf_op jit(solution)/shard_map/all_to_all | solution.py:375
  79.1 75.1 %copy-start.4 = (s32[128]{0:T(128)S(1)}, s32[128]{0:T(128)}, u32[]{:S(2)}) copy-start(s32[128]{0:T(128)} %constant.55.clone) | copy-start | bytes 1540
  79.2 2.7 %collective-permute-start.2 = (f32[8,8,32,128]{3,2,0,1:T(8,128)S(1)}, f32[8,8,32,128]{3,2,0,1:T(8,128)S(1)}, u32[]{:S(2)}, u32[]{:S(2)}) collective-permute-start(f32[8,8,32,128]{3,2,0,1:T(8,128)S(1)} %bitcast.39), channel_id=1, source_target_pairs={{0,8},{8,0},{16,24},{24,16},{32,40},{40,32},{48,56},{56,48},{64,72... | collective-permute-start | bytes 3145736 | tf_op jit(solution)/shard_map/ppermute | solution.py:391
  82.2 69.9 %collective-permute-start.3 = (bf16[8,32,128]{2,1,0:T(8,128)(2,1)S(1)}, bf16[8,32,128]{2,1,0:T(8,128)(2,1)S(1)}, u32[]{:S(2)}, u32[]{:S(2)}) collective-permute-start(bf16[8,32,128]{2,1,0:T(8,128)(2,1)S(1)} %get-tuple-element.20), channel_id=1, source_target_pairs={{0,16},{8,24},{16,32},{24,40},{32,48},{40,56},{48,64},{56,72},{64,... | collective-permute-start | bytes 196616 | tf_op jit(solution)/shard_map/ppermute | solution.py:397
  84.1 69.4 %collective-permute-start.4 = (bf16[8,32,128]{2,1,0:T(8,128)(2,1)S(1)}, bf16[8,32,128]{2,1,0:T(8,128)(2,1)S(1)}, u32[]{:S(2)}, u32[]{:S(2)}) collective-permute-start(bf16[8,32,128]{2,1,0:T(8,128)(2,1)S(1)} %get-tuple-element.26), channel_id=1, source_target_pairs={{0,32},{8,40},{16,48},{24,56},{32,64},{40,72},{48,80},{56,88},{64,... | collective-permute-start | bytes 196616 | tf_op jit(solution)/shard_map/ppermute | solution.py:397
  85.6 72.5 %collective-permute-start.5 = (bf16[8,32,128]{2,1,0:T(8,128)(2,1)S(1)}, bf16[8,32,128]{2,1,0:T(8,128)(2,1)S(1)}, u32[]{:S(2)}, u32[]{:S(2)}) collective-permute-start(bf16[8,32,128]{2,1,0:T(8,128)(2,1)S(1)} %get-tuple-element.25), channel_id=1, source_target_pairs={{0,48},{8,56},{16,64},{24,72},{32,80},{40,88},{48,96},{56,104},{64... | collective-permute-start | bytes 196616 | tf_op jit(solution)/shard_map/ppermute | solution.py:397
  87.7 70.4 %collective-permute-start.6 = (bf16[8,32,128]{2,1,0:T(8,128)(2,1)S(1)}, bf16[8,32,128]{2,1,0:T(8,128)(2,1)S(1)}, u32[]{:S(2)}, u32[]{:S(2)}) collective-permute-start(bf16[8,32,128]{2,1,0:T(8,128)(2,1)S(1)} %get-tuple-element.24), channel_id=1, source_target_pairs={{0,64},{8,72},{16,80},{24,88},{32,96},{40,104},{48,112},{56,120},{... | collective-permute-start | bytes 196616 | tf_op jit(solution)/shard_map/ppermute | solution.py:397
  89.7 68.3 %collective-permute-start.7 = (bf16[8,32,128]{2,1,0:T(8,128)(2,1)S(1)}, bf16[8,32,128]{2,1,0:T(8,128)(2,1)S(1)}, u32[]{:S(2)}, u32[]{:S(2)}) collective-permute-start(bf16[8,32,128]{2,1,0:T(8,128)(2,1)S(1)} %get-tuple-element.23), channel_id=1, source_target_pairs={{0,80},{8,88},{16,96},{24,104},{32,112},{40,120},{48,0},{56,8},{64... | collective-permute-start | bytes 196616 | tf_op jit(solution)/shard_map/ppermute | solution.py:397
  152.2 5.9 %collective-permute-start.8 = (bf16[8,32,128]{2,1,0:T(8,128)(2,1)S(1)}, bf16[8,32,128]{2,1,0:T(8,128)(2,1)S(1)}, u32[]{:S(2)}, u32[]{:S(2)}) collective-permute-start(bf16[8,32,128]{2,1,0:T(8,128)(2,1)S(1)} %get-tuple-element.22), channel_id=1, source_target_pairs={{0,96},{8,104},{16,112},{24,120},{32,0},{40,8},{48,16},{56,24},{64... | collective-permute-start | bytes 196616 | tf_op jit(solution)/shard_map/ppermute | solution.py:397
  153.5 4.6 %collective-permute-start.9 = (bf16[8,32,128]{2,1,0:T(8,128)(2,1)S(1)}, bf16[8,32,128]{2,1,0:T(8,128)(2,1)S(1)}, u32[]{:S(2)}, u32[]{:S(2)}) collective-permute-start(bf16[8,32,128]{2,1,0:T(8,128)(2,1)S(1)} %get-tuple-element.21), channel_id=1, source_target_pairs={{0,112},{8,120},{16,0},{24,8},{32,16},{40,24},{48,32},{56,40},{64,... | collective-permute-start | bytes 196616 | tf_op jit(solution)/shard_map/ppermute | solution.py:397

commit v5 on v4

--- a/solution.py
+++ b/solution.py
@@ -100,11 +100,46 @@
     return smoothed, plain
 
 
-def register_body(first, count, total, meta_ref, raw_ref, left_ref, right_ref, *rest):
-    if first > 0:
-        sum_in_ref, *rest = rest
-    send_ref, sum_out_ref, *rest = rest
-    smooth_y, plain_y, split, plain, smooth, summed = rest
+def fill_rows(off_y, rows, put):
+    tall, wide, edge = 64, min(2 * LANES, rows), 16
+    for low in range(0, rows, tall):
+        lane = min(max((low - RADIUS - HALO) // LANES, 0) * LANES, rows - wide)
+        out_row, in_row = iota((tall, wide), 0) + low, iota((tall, wide), 1) + lane
+        put(low, lane, *high_pass_inside(out_row, in_row, off_y))
+    for low, lane in ((0, 0), (rows - edge, rows - wide)):
+        out_row, in_row = iota((edge, wide), 0) + low, iota((edge, wide), 1) + lane
+        put(low, lane, *high_pass(out_row, in_row, off_y, rows))
+
+
+def edge_columns(left, right, slot, planes):
+    source = iota((2 * LANES, LANES), 0)
+    target = iota((2 * LANES, LANES), 1)
+    side, lane = source // LANES, source % LANES - slot * planes * HALO
+    plane, column = lane // HALO, lane % HALO
+    chosen = (lane >= 0) & (lane < planes * HALO) & (target == plane * 2 * HALO + side * HALO + column)
+    pick = chosen.astype(jnp.float32).astype(jnp.bfloat16)
+    return dot(jnp.concatenate([left, right], axis=1), pick).astype(jnp.bfloat16)
+
+
+def column_weights(planes, lanes, off_x, weigh):
+    def across(source):
+        column = iota(source.shape, 1)
+        return weigh(source - column + off_x, column)
+
+    inner = across(iota((lanes, lanes), 0)).astype(jnp.bfloat16)
+    outer = iota((2 * HALO, lanes), 0)
+    outer = across(jnp.where(outer < HALO, outer - HALO, outer - HALO + lanes))
+    weights = []
+    for z in range(planes):
+        pieces = [outer]
+        if z > 0:
+            pieces.insert(0, jnp.zeros((2 * HALO * z, lanes), jnp.float32))
+        pieces.append(jnp.zeros((LANES - 2 * HALO * (z + 1), lanes), jnp.float32))
+        weights.append(jnp.concatenate([inner, jnp.concatenate(pieces, axis=0).astype(jnp.bfloat16)], axis=0))
+    return weights
+
+
+def register_body(first, total, meta_ref, raw_ref, left_ref, right_ref, send_ref, smooth_y, split, smooth):
     planes, rows, lanes = raw_ref.shape[1:]
     blocks = send_ref.shape[0]
     strip = rows // blocks
@@ -113,141 +148,137 @@
     @pl.when(step == 0)
     def _():
         smooth_y[...] = jnp.zeros(smooth_y.shape, smooth_y.dtype)
-        plain_y[...] = jnp.zeros(plain_y.shape, plain_y.dtype)
         smooth[0:HALO] = jnp.zeros((HALO, rows, lanes), jnp.float32)
         smooth[HALO + planes :] = jnp.zeros((HALO, rows, lanes), jnp.float32)
-        if first > 0:
-            summed[SHIFT : SHIFT + planes] = sum_in_ref[...] * BOX
-        else:
-            summed[SHIFT : SHIFT + planes] = jnp.zeros((planes, rows, lanes), jnp.float32)
-
-    def frame():
-        index = first + step
-        off_z, off_y, off_x = meta_ref[3 * index], meta_ref[3 * index + 1], meta_ref[3 * index + 2]
-        at_start, at_end = meta_ref[3 * total], meta_ref[3 * total + 1]
-
-        def put(low, tall, lane, pair):
-            smoothed, unsmoothed = (value.astype(jnp.bfloat16) for value in pair)
-            wide = unsmoothed.shape[1]
-            smooth_y[low : low + tall, lane : lane + wide] = smoothed
-            smooth_y[low : low + tall, rows + lane : rows + lane + wide] = smoothed
-            plain_y[low : low + tall, lane : lane + wide] = unsmoothed
-
-        tall, wide, edge = 64, min(2 * LANES, rows), 16
-        for low in range(0, rows, tall):
-            lane = min(max((low - RADIUS - HALO) // LANES, 0) * LANES, rows - wide)
-            out_row, in_row = iota((tall, wide), 0) + low, iota((tall, wide), 1) + lane
-            put(low, tall, lane, high_pass_inside(out_row, in_row, off_y))
-        for low, lane in ((0, 0), (rows - edge, rows - wide)):
-            out_row, in_row = iota((edge, wide), 0) + low, iota((edge, wide), 1) + lane
-            put(low, edge, lane, high_pass(out_row, in_row, off_y, rows))
-
-        slot = lax.rem(index, PACK)
-        source = iota((2 * LANES, LANES), 0)
-        target = iota((2 * LANES, LANES), 1)
-        side, lane = source // LANES, source % LANES - slot * planes * HALO
-        plane, column = lane // HALO, lane % HALO
-        chosen = (lane >= 0) & (lane < planes * HALO) & (target == plane * 2 * HALO + side * HALO + column)
-        pick = chosen.astype(jnp.float32).astype(jnp.bfloat16)
-        edges = dot(jnp.concatenate([left_ref[0], right_ref[0]], axis=1), pick).astype(jnp.bfloat16)
-
-        def across(source):
-            column = iota(source.shape, 1)
-            second = column >= lanes
-            column = jnp.where(second, column - lanes, column)
-            gap = source - column + off_x
-            low = jnp.where(second | ((column == 0) & (at_start > 0)), 0.0, 1.0)
-            high = jnp.where(second | ((column == lanes - 1) & (at_end > 0)), 0.0, 1.0)
-            middle = jnp.where(second, 1.0, 2.0)
-            return jnp.where(gap == 0, middle, jnp.where(gap == -1, low, jnp.where(gap == 1, high, 0.0)))
-
-        inner = across(iota((lanes, 2 * lanes), 0)).astype(jnp.bfloat16)
-        outer = iota((2 * HALO, 2 * lanes), 0)
-        outer = across(jnp.where(outer < HALO, outer - HALO, outer - HALO + lanes))
-
-        for pair in range(planes // 2):
-            for half in range(2):
-                z = 2 * pair + half
-                pieces = [outer]
-                if z > 0:
-                    pieces.insert(0, jnp.zeros((2 * HALO * z, 2 * lanes), jnp.float32))
-                left_over = LANES - 2 * HALO * (z + 1)
-                pieces.append(jnp.zeros((left_over, 2 * lanes), jnp.float32))
-                weights = jnp.concatenate([inner, jnp.concatenate(pieces, axis=0).astype(jnp.bfloat16)], axis=0)
-                moved = dot(jnp.concatenate([raw_ref[0, z], edges], axis=1), weights)
-                big = moved[:, :lanes].astype(jnp.bfloat16)
-                columns = slice(half * lanes, (half + 1) * lanes)
-                split[:rows, columns] = big
-                split[rows:, columns] = (moved[:, :lanes] - big.astype(jnp.float32)).astype(jnp.bfloat16)
-                plain[:, columns] = moved[:, lanes:].astype(jnp.bfloat16)
-            smoothed = dot(smooth_y[...], split[...])
-            shifted = dot(plain_y[...], plain[...])
-            for half in range(2):
-                z = 2 * pair + half
-                columns = slice(half * lanes, (half + 1) * lanes)
-                smooth[HALO + z] = smoothed[:, columns]
-                summed[SHIFT + z + off_z] += shifted[:, columns]
-
-        def along(block, carry):
-            low = pl.multiple_of(block * strip, strip)
-            plane = [smooth[HALO + z - off_z, pl.ds(low, strip), :] for z in range(planes)]
-            for z in range(planes):
-                value = 2.0 * plane[z]
-                if z > 0:
-                    value = value + plane[z - 1]
-                if z + 1 < planes:
-                    value = value + plane[z + 1]
-                send_ref[block, 0, z] = (value * (1.0 / (BOX * 64))).astype(jnp.bfloat16)
-            return carry
-
-        lax.fori_loop(0, blocks, along, 0)
-
-    frame()
-
-    @pl.when(step == count - 1)
-    def _():
-        sum_out_ref[...] = summed[SHIFT : SHIFT + planes] * (1.0 / BOX)
-
-
-def register(raw, left, right, meta, summed, first, count, owners):
+
+    index = first + step
+    off_z, off_y, off_x = meta_ref[3 * index], meta_ref[3 * index + 1], meta_ref[3 * index + 2]
+    at_start, at_end = meta_ref[3 * total], meta_ref[3 * total + 1]
+
+    def put(low, lane, smoothed, unsmoothed):
+        smoothed = smoothed.astype(jnp.bfloat16)
+        tall, wide = smoothed.shape
+        smooth_y[low : low + tall, lane : lane + wide] = smoothed
+        smooth_y[low : low + tall, rows + lane : rows + lane + wide] = smoothed
+
+    fill_rows(off_y, rows, put)
+    edges = edge_columns(left_ref[0], right_ref[0], lax.rem(index, PACK), planes)
+
+    def weigh(gap, column):
+        low = jnp.where((column == 0) & (at_start > 0), 0.0, 1.0)
+        high = jnp.where((column == lanes - 1) & (at_end > 0), 0.0, 1.0)
+        return jnp.where(gap == 0, 2.0, jnp.where(gap == -1, low, jnp.where(gap == 1, high, 0.0)))
+
+    weights = column_weights(planes, lanes, off_x, weigh)
+    for pair in range(planes // 2):
+        for half in range(2):
+            z = 2 * pair + half
+            moved = dot(jnp.concatenate([raw_ref[0, z], edges], axis=1), weights[z])
+            big = moved.astype(jnp.bfloat16)
+            columns = slice(half * lanes, (half + 1) * lanes)
+            split[:rows, columns] = big
+            split[rows:, columns] = (moved - big.astype(jnp.float32)).astype(jnp.bfloat16)
+        smoothed = dot(smooth_y[...], split[...])
+        for half in range(2):
+            smooth[HALO + 2 * pair + half] = smoothed[:, half * lanes : (half + 1) * lanes]
+
+    def along(block, carry):
+        low = pl.multiple_of(block * strip, strip)
+        plane = [smooth[HALO + z - off_z, pl.ds(low, strip), :] for z in range(planes)]
+        for z in range(planes):
+            value = 2.0 * plane[z]
+            if z > 0:
+                value = value + plane[z - 1]
+            if z + 1 < planes:
+                value = value + plane[z + 1]
+            send_ref[block, 0, z] = (value * (1.0 / (BOX * 64))).astype(jnp.bfloat16)
+        return carry
+
+    lax.fori_loop(0, blocks, along, 0)
+
+
+def register(raw, left, right, meta, first, count, owners):
     frames, planes, rows, lanes = raw.shape
-
+    strip = rows // owners
     edge_spec = pl.BlockSpec((1, rows, LANES), lambda f, m: ((first + f) // PACK, 0, 0))
-    whole = pl.BlockSpec((planes, rows, lanes), lambda f, m: (0, 0, 0))
-    raw_spec = pl.BlockSpec((1, planes, rows, lanes), lambda f, m: (first + f, 0, 0, 0))
-    in_specs = [raw_spec, edge_spec, edge_spec]
-    operands = [raw, left, right]
-    if first > 0:
-        in_specs.append(whole)
-        operands.append(summed)
-    strip = rows // owners
-    out_specs = [pl.BlockSpec((owners, 1, planes, strip, lanes), lambda f, m: (0, f, 0, 0, 0))]
-    out_shape = [jax.ShapeDtypeStruct((owners, count, planes, strip, lanes), jnp.bfloat16)]
-    out_specs.append(whole)
-    out_shape.append(jax.ShapeDtypeStruct((planes, rows, lanes), jnp.float32))
 
     def body(*refs):
-        register_body(first, count, frames, *refs)
+        register_body(first, frames, *refs)
 
     return pl.pallas_call(
         body,
         grid_spec=pltpu.PrefetchScalarGridSpec(
             num_scalar_prefetch=1,
             grid=(count,),
-            in_specs=in_specs,
-            out_specs=tuple(out_specs),
+            in_specs=[
+                pl.BlockSpec((1, planes, rows, lanes), lambda f, m: (first + f, 0, 0, 0)),
+                edge_spec,
+                edge_spec,
+            ],
+            out_specs=pl.BlockSpec((owners, 1, planes, strip, lanes), lambda f, m: (0, f, 0, 0, 0)),
             scratch_shapes=[
                 pltpu.VMEM((rows, 2 * rows), jnp.bfloat16),
+                pltpu.VMEM((2 * rows, 2 * lanes), jnp.bfloat16),
+                pltpu.VMEM((planes + 2 * HALO, rows, lanes), jnp.float32),
+            ],
+        ),
+        out_shape=jax.ShapeDtypeStruct((owners, count, planes, strip, lanes), jnp.bfloat16),
+        compiler_params=pltpu.CompilerParams(vmem_limit_bytes=VMEM),
+    )(meta, raw, left, right)
+
+
+def frame_sum_body(meta_ref, raw_ref, left_ref, right_ref, out_ref, plain_y, plain, summed):
+    planes, rows, lanes = raw_ref.shape[1:]
+    index = pl.program_id(0)
+
+    @pl.when(index == 0)
+    def _():
+        plain_y[...] = jnp.zeros(plain_y.shape, plain_y.dtype)
+        summed[...] = jnp.zeros(summed.shape, summed.dtype)
+
+    off_z, off_y, off_x = meta_ref[3 * index], meta_ref[3 * index + 1], meta_ref[3 * index + 2]
+
+    def put(low, lane, smoothed, unsmoothed):
+        tall, wide = unsmoothed.shape
+        plain_y[low : low + tall, lane : lane + wide] = unsmoothed.astype(jnp.bfloat16)
+
+    fill_rows(off_y, rows, put)
+    edges = edge_columns(left_ref[0], right_ref[0], lax.rem(index, PACK), planes)
+    weights = column_weights(planes, lanes, off_x, lambda gap, column: jnp.where(gap == 0, 1.0, 0.0))
+    for pair in range(planes // 2):
+        for half in range(2):
+            z = 2 * pair + half
+            moved = dot(jnp.concatenate([raw_ref[0, z], edges], axis=1), weights[z])
+            plain[:, half * lanes : (half + 1) * lanes] = moved.astype(jnp.bfloat16)
+        shifted = dot(plain_y[...], plain[...])
+        for half in range(2):
+            summed[SHIFT + 2 * pair + half + off_z] += shifted[:, half * lanes : (half + 1) * lanes]
+
+    @pl.when(index == pl.num_programs(0) - 1)
+    def _():
+        out_ref[...] = summed[SHIFT : SHIFT + planes] * (1.0 / BOX)
+
+
+def frame_sum(raw, left, right, meta):
+    frames, planes, rows, lanes = raw.shape
+    edge_spec = pl.BlockSpec((1, rows, LANES), lambda f, m: (f // PACK, 0, 0))
+    return pl.pallas_call(
+        frame_sum_body,
+        grid_spec=pltpu.PrefetchScalarGridSpec(
+            num_scalar_prefetch=1,
+            grid=(frames,),
+            in_specs=[pl.BlockSpec((1, planes, rows, lanes), lambda f, m: (f, 0, 0, 0)), edge_spec, edge_spec],
+            out_specs=pl.BlockSpec((planes, rows, lanes), lambda f, m: (0, 0, 0)),
+            scratch_shapes=[
                 pltpu.VMEM((rows, rows), jnp.bfloat16),
-                pltpu.VMEM((2 * rows, 2 * lanes), jnp.bfloat16),
                 pltpu.VMEM((rows, 2 * lanes), jnp.bfloat16),
-                pltpu.VMEM((planes + 2 * HALO, rows, lanes), jnp.float32),
                 pltpu.VMEM((planes + 2 * SHIFT, rows, lanes), jnp.float32),
             ],
         ),
-        out_shape=tuple(out_shape),
+        out_shape=jax.ShapeDtypeStruct((planes, rows, lanes), jnp.float32),
         compiler_params=pltpu.CompilerParams(vmem_limit_bytes=VMEM),
-    )(meta, *operands)
+        name="frame_sum",
+    )(meta, raw, left, right)
 
 
 def spread_body(taps_ref, order_ref, kernel_ref, rowsum_ref):
@@ -368,13 +399,12 @@
     kernel, rowsum = spread_kernel(taps, jnp.tile(jnp.array(order, jnp.int32)[None], (SUB, 1)))
 
     got = []
-    summed = None
     low = 0
     for count in CHUNKS:
-        sent, summed = register(raw, left, right, meta, summed, low, count, owners)
+        sent = register(raw, left, right, meta, low, count, owners)
         got.append(lax.all_to_all(sent, "frames", split_axis=0, concat_axis=0, tiled=True))
         low += count
-    template = summed_over_frames(summed, owners) * (1.0 / total)
+    template = summed_over_frames(frame_sum(raw, left, right, meta), owners) * (1.0 / total)
     return filter_frames(kernel, rowsum, got, total, group), template
 
 

time: 172 us -> 168 us (0.977)
  waiting for transfers between devices: 72.1 us -> 60.8 us
  Pallas kernels: 62.5 us -> 73.4 us
  starting transfers between devices: 29.2 us -> 26 us
    pallas_call x0 -> x1, Pallas kernels: none -> 21.2 us  [frame_sum(): pl.pallas_call(frame_sum_body, grid_spec=pltpu.PrefetchScalarGridSpec(num...]
    ppermute x7, waiting for transfers between devices: 59.5 us -> 41.2 us  [summed_over_frames(): lax.ppermute(sent, 'frames', [(i, (i + 2 * turn) % owners) for i in range...]
    pallas_call x2, Pallas kernels: 40.5 us -> 30.1 us  [register(): pl.pallas_call(body, grid_spec=pltpu.PrefetchScalarGridSpec(num_scalar_pr...]
    all_to_all x2, waiting for transfers between devices: 0.01 us -> 6.79 us  [local(): lax.all_to_all(sent, 'frames', split_axis=0, concat_axis=0, tiled=True)]
    ppermute x7, starting transfers between devices: 12.5 us -> 10.6 us  [summed_over_frames(): lax.ppermute(sent, 'frames', [(i, (i + 2 * turn) % owners) for i in range...]
  transfers between devices with their start and end apart: 12 -> 12, of which waited for: 4 -> 6; matrix products, arithmetic and copies ran while one was open for 3% -> 3% of each run, Pallas kernels for 19% -> 27%
where the time goes in v5:
time: 168 us; the launch traced here: 167 us
  Pallas kernels  73.4 us (44%)
  waiting for transfers between devices  60.8 us (36%)
  starting transfers between devices  26 us (15%)
  local copies, waits for them, and re-layouts  4.82 us (3%)
    ppermute x7, waiting for transfers between devices, summed_over_frames(): lax.ppermute(sent, 'frames', [(i, (i + 2 * turn) % owners) for i in range...  41.2 us
    pallas_call x2, Pallas kernels, register(): pl.pallas_call(body, grid_spec=pltpu.PrefetchScalarGridSpec(num_scalar_pr...  30.1 us
    pallas_call x1, Pallas kernels, frame_sum(): pl.pallas_call(frame_sum_body, grid_spec=pltpu.PrefetchScalarGridSpec(num...  21.2 us
    pallas_call x1, Pallas kernels, filter_frames(): pl.pallas_call(body, grid=(planes,), in_specs=in_specs, out_specs=pl.Bloc...  12.2 us
    ppermute x7, starting transfers between devices, summed_over_frames(): lax.ppermute(sent, 'frames', [(i, (i + 2 * turn) % owners) for i in range...  10.6 us
    all_to_all x2, starting transfers between devices, local(): lax.all_to_all(sent, 'frames', split_axis=0, concat_axis=0, tiled=True)  9.25 us
    ppermute x1, waiting for transfers between devices, local(): right = lax.ppermute(first_columns, 'tiles', [(j, i) for i, j in upward])  6.9 us
    all_to_all x2, waiting for transfers between devices, local(): lax.all_to_all(sent, 'frames', split_axis=0, concat_axis=0, tiled=True)  6.79 us
  transfers between devices with their start and end apart: 12, of which 6 were waited for; matrix products, arithmetic and copies ran while one was open for 3% of the time, Pallas kernels for 27%

profile of v5, /device:TPU:96, one launch (start us, length us, event | category | flops | bytes accessed | tf_op | source)
XLA Modules:
  0.0 167.3 jit_solution(13778174816617269613)
XLA Ops:
  0.6 6.5 %pack_edges.1 = (bf16[2,512,128]{2,1,0:T(8,128)(2,1)}, bf16[2,512,128]{2,1,0:T(8,128)(2,1)}) custom-call(bf16[8,8,512,128]{3,2,1,0:T(8,128)(2,1)} %raw_ref.1, bf16[8,8,512,128]{3,2,1,0:T(8,128)(2,1)} %raw_ref.1), custom_call_target="tpu_custom_call" | custom-call | tf_op jit(solution)/shard_map/pack_edges/pallas_call | solution.py:68
  7.1 3.6 %collective-permute-start = (bf16[2,512,128]{2,1,0:T(8,128)(2,1)}, bf16[2,512,128]{2,1,0:T(8,128)(2,1)S(1)}, u32[]{:S(2)}, u32[]{:S(2)}) collective-permute-start(bf16[2,512,128]{2,1,0:T(8,128)(2,1)} %get-tuple-element.8), channel_id=1, source_target_pairs={{0,1},{1,2},{2,3},{3,4},{4,5},{5,6},{6,7},{8,9},{9,10},{10,11},{11... | collective-permute-start | bytes 786440 | tf_op jit(solution)/shard_map/ppermute | solution.py:385
  10.7 2.3 %collective-permute-start.1 = (bf16[2,512,128]{2,1,0:T(8,128)(2,1)}, bf16[2,512,128]{2,1,0:T(8,128)(2,1)S(1)}, u32[]{:S(2)}, u32[]{:S(2)}) collective-permute-start(bf16[2,512,128]{2,1,0:T(8,128)(2,1)} %get-tuple-element.9), channel_id=1, source_target_pairs={{1,0},{2,1},{3,2},{4,3},{5,4},{6,5},{7,6},{9,8},{10,9},{11,10},{12... | collective-permute-start | bytes 786440 | tf_op jit(solution)/shard_map/ppermute | solution.py:386
  13.8 3.4 %collective-permute-done.refs_2_.left_ref = bf16[2,512,128]{2,1,0:T(8,128)(2,1)S(1)} collective-permute-done((bf16[2,512,128]{2,1,0:T(8,128)(2,1)}, bf16[2,512,128]{2,1,0:T(8,128)(2,1)S(1)}, u32[]{:S(2)}, u32[]{:S(2)}) %collective-permute-start) | collective-permute-done | bytes 262176 | tf_op jit(solution)/shard_map/ppermute | solution.py:385
  17.3 6.9 %collective-permute-done.1.refs_3_.right_ref = bf16[2,512,128]{2,1,0:T(8,128)(2,1)S(1)} collective-permute-done((bf16[2,512,128]{2,1,0:T(8,128)(2,1)}, bf16[2,512,128]{2,1,0:T(8,128)(2,1)S(1)}, u32[]{:S(2)}, u32[]{:S(2)}) %collective-permute-start.1) | collective-permute-done | bytes 262176 | tf_op jit(solution)/shard_map/ppermute | solution.py:386
  24.9 9.1 %shard_map.59 = bf16[16,2,8,32,128]{4,3,2,1,0:T(8,128)(2,1)} custom-call(s32[26]{0:T(128)} %pad_add_fusion.refs_0_.meta_ref, bf16[8,8,512,128]{3,2,1,0:T(8,128)(2,1)} %raw_ref.1, bf16[2,512,128]{2,1,0:T(8,128)(2,1)} %copy-done.1, bf16[2,512,128]{2,1,0:T(8,128)(2,1)} %copy-done.2), custom_call_target="tpu_custom_call" | custom-call | tf_op jit(solution)/shard_map/pallas_call | solution.py:208
  34.0 4.6 %all-to-all-start = ((bf16[16,2,8,32,128]{4,3,2,1,0:T(8,128)(2,1)}), bf16[16,2,8,32,128]{4,3,2,1,0:T(8,128)(2,1)S(1)}, u32[]{:S(2)}, u32[]{:S(2)}) async-start(bf16[16,2,8,32,128]{4,3,2,1,0:T(8,128)(2,1)} %shard_map.59), calls=%async_computation | async-start | bytes 4194304 | tf_op jit(solution)/shard_map/all_to_all | solution.py:405
  38.6 21.0 %shard_map.60 = bf16[16,6,8,32,128]{4,3,2,1,0:T(8,128)(2,1)} custom-call(s32[26]{0:T(128)} %pad_add_fusion.refs_0_.meta_ref, bf16[8,8,512,128]{3,2,1,0:T(8,128)(2,1)} %raw_ref.1, bf16[2,512,128]{2,1,0:T(8,128)(2,1)} %copy-done.1, bf16[2,512,128]{2,1,0:T(8,128)(2,1)} %copy-done.2), custom_call_target="tpu_custom_call" | custom-call | tf_op jit(solution)/shard_map/pallas_call | solution.py:208
  59.7 6.8 %all-to-all-done.refs_2_ = bf16[16,2,8,32,128]{4,3,2,1,0:T(8,128)(2,1)S(1)} async-done(((bf16[16,2,8,32,128]{4,3,2,1,0:T(8,128)(2,1)}), bf16[16,2,8,32,128]{4,3,2,1,0:T(8,128)(2,1)S(1)}, u32[]{:S(2)}, u32[]{:S(2)}) %all-to-all-start) | async-done | bytes 2097184 | tf_op jit(solution)/shard_map/all_to_all | solution.py:405
  66.4 1.4 copy-done
  67.8 4.6 %all-to-all-start.1 = ((bf16[16,6,8,32,128]{4,3,2,1,0:T(8,128)(2,1)}), bf16[16,6,8,32,128]{4,3,2,1,0:T(8,128)(2,1)}, u32[]{:S(2)}, u32[]{:S(2)}) async-start(bf16[16,6,8,32,128]{4,3,2,1,0:T(8,128)(2,1)} %shard_map.60), calls=%async_computation.1 | async-start | bytes 12582912 | tf_op jit(solution)/shard_map/all_to_all | solution.py:405
  72.5 21.2 %frame_sum.1 = f32[8,512,128]{2,1,0:T(8,128)} custom-call(s32[26]{0:T(128)} %pad_add_fusion.refs_0_.meta_ref, bf16[8,8,512,128]{3,2,1,0:T(8,128)(2,1)} %raw_ref.1, bf16[2,512,128]{2,1,0:T(8,128)(2,1)} %copy-done.1, bf16[2,512,128]{2,1,0:T(8,128)(2,1)} %copy-done.2), custom_call_target="tpu_custom_call" | custom-call | tf_op jit(solution)/shard_map/frame_sum/pallas_call | solution.py:265
  93.7 1.8 %constant_dynamic-slice_fusion.1 = (f32[8,8,1,32,128]{4,3,2,1,0:T(8,128)S(1)}, f32[8,8,1,32,128]{4,3,2,1,0:T(8,128)S(1)}) fusion(f32[8,8,2,32,128]{4,3,2,1,0:T(8,128)} %bitcast.38, s32[]{:T(128)S(6)} %select_n.32, s32[]{:T(128)S(6)} %select_n.33), kind=kLoop, calls=%fused_computation.25 | loop fusion | bytes 4194312 | tf_op jit(solution)/shard_map/jit(dynamic_index_in_dim)/dynamic_slice | solution.py:419
  95.9 2.4 %collective-permute-done.2 = f32[8,8,32,128]{3,2,0,1:T(8,128)S(1)} collective-permute-done((f32[8,8,32,128]{3,2,0,1:T(8,128)S(1)}, f32[8,8,32,128]{3,2,0,1:T(8,128)S(1)}, u32[]{:S(2)}, u32[]{:S(2)}) %collective-permute-start.2) | collective-permute-done | bytes 1048608 | tf_op jit(solution)/shard_map/ppermute | solution.py:421
  98.6 1.8 %collective-permute-start.3 = (bf16[8,32,128]{2,1,0:T(8,128)(2,1)S(1)}, bf16[8,32,128]{2,1,0:T(8,128)(2,1)S(1)}, u32[]{:S(2)}, u32[]{:S(2)}) collective-permute-start(bf16[8,32,128]{2,1,0:T(8,128)(2,1)S(1)} %get-tuple-element.12), channel_id=1, source_target_pairs={{0,16},{8,24},{16,32},{24,40},{32,48},{40,56},{48,64},{56,72},{64,... | collective-permute-start | bytes 196616 | tf_op jit(solution)/shard_map/ppermute | solution.py:427
  100.4 2.4 %collective-permute-start.9 = (bf16[8,32,128]{2,1,0:T(8,128)(2,1)S(1)}, bf16[8,32,128]{2,1,0:T(8,128)(2,1)S(1)}, u32[]{:S(2)}, u32[]{:S(2)}) collective-permute-start(bf16[8,32,128]{2,1,0:T(8,128)(2,1)S(1)} %get-tuple-element.13), channel_id=1, source_target_pairs={{0,112},{8,120},{16,0},{24,8},{32,16},{40,24},{48,32},{56,40},{64,... | collective-permute-start | bytes 196616 | tf_op jit(solution)/shard_map/ppermute | solution.py:427
  102.8 1.8 %collective-permute-start.8 = (bf16[8,32,128]{2,1,0:T(8,128)(2,1)S(1)}, bf16[8,32,128]{2,1,0:T(8,128)(2,1)S(1)}, u32[]{:S(2)}, u32[]{:S(2)}) collective-permute-start(bf16[8,32,128]{2,1,0:T(8,128)(2,1)S(1)} %get-tuple-element.14), channel_id=1, source_target_pairs={{0,96},{8,104},{16,112},{24,120},{32,0},{40,8},{48,16},{56,24},{64... | collective-permute-start | bytes 196616 | tf_op jit(solution)/shard_map/ppermute | solution.py:427
  104.6 0.8 collective-permute-start.7
  105.5 2.7 %collective-permute-start.6 = (bf16[8,32,128]{2,1,0:T(8,128)(2,1)S(1)}, bf16[8,32,128]{2,1,0:T(8,128)(2,1)S(1)}, u32[]{:S(2)}, u32[]{:S(2)}) collective-permute-start(bf16[8,32,128]{2,1,0:T(8,128)(2,1)S(1)} %get-tuple-element.16), channel_id=1, source_target_pairs={{0,64},{8,72},{16,80},{24,88},{32,96},{40,104},{48,112},{56,120},{... | collective-permute-start | bytes 196616 | tf_op jit(solution)/shard_map/ppermute | solution.py:427
  108.2 39.5 %collective-permute-done.3 = bf16[8,32,128]{2,1,0:T(8,128)(2,1)S(1)} collective-permute-done((bf16[8,32,128]{2,1,0:T(8,128)(2,1)S(1)}, bf16[8,32,128]{2,1,0:T(8,128)(2,1)S(1)}, u32[]{:S(2)}, u32[]{:S(2)}) %collective-permute-start.3) | collective-permute-done | bytes 65568 | tf_op jit(solution)/shard_map/ppermute | solution.py:427
  147.7 1.0 collective-permute-start.4
  149.3 3.3 %spread_kernel.1 = (bf16[1024,1024]{1,0:T(8,128)(2,1)}, f32[1024,128]{1,0:T(8,128)}) custom-call(f32[64]{0:T(128)} %taps_ref.1, s32[8,128]{1,0:T(8,128)} %tile.2.order_ref), custom_call_target="tpu_custom_call" | custom-call | tf_op jit(solution)/shard_map/spread_kernel/pallas_call | solution.py:303
  152.7 1.7 %collective-permute-done.5 = bf16[8,32,128]{2,1,0:T(8,128)(2,1)S(1)} collective-permute-done((bf16[8,32,128]{2,1,0:T(8,128)(2,1)S(1)}, bf16[8,32,128]{2,1,0:T(8,128)(2,1)S(1)}, u32[]{:S(2)}, u32[]{:S(2)}) %collective-permute-start.5) | collective-permute-done | bytes 65568 | tf_op jit(solution)/shard_map/ppermute | solution.py:427
  155.1 12.2 %filter_frames.1 = bf16[128,8,32,128]{3,2,1,0:T(8,128)(2,1)} custom-call(bf16[1024,1024]{1,0:T(8,128)(2,1)} %get-tuple-element.6.refs_0_, f32[1024,128]{1,0:T(8,128)} %get-tuple-element.7.refs_1_, bf16[16,2,8,32,128]{4,3,2,1,0:T(8,128)(2,1)} %copy-done, bf16[16,6,8,32,128]{4,3,2,1,0:T(8,128)(2,1)} %all-to-all-done.1.refs_3_), custom_call_target="tpu_custom_call" | custom-call | tf_op jit(solution)/shard_map/filter_frames/pallas_call | solution.py:365
  (26 shorter events, 3.6 us)
Async XLA Ops:
  0.6 12.4 %copy-start.3 = (s32[8,3]{0,1:T(4,128)S(1)}, s32[8,3]{0,1:T(4,128)}, u32[]{:S(2)}) copy-start(s32[8,3]{0,1:T(4,128)} %param.5) | copy-start | bytes 292
  7.1 10.1 %collective-permute-start = (bf16[2,512,128]{2,1,0:T(8,128)(2,1)}, bf16[2,512,128]{2,1,0:T(8,128)(2,1)S(1)}, u32[]{:S(2)}, u32[]{:S(2)}) collective-permute-start(bf16[2,512,128]{2,1,0:T(8,128)(2,1)} %get-tuple-element.8), channel_id=1, source_target_pairs={{0,1},{1,2},{2,3},{3,4},{4,5},{5,6},{6,7},{8,9},{9,10},{10,11},{11... | collective-permute-start | bytes 786440 | tf_op jit(solution)/shard_map/ppermute | solution.py:385
  10.7 13.5 %collective-permute-start.1 = (bf16[2,512,128]{2,1,0:T(8,128)(2,1)}, bf16[2,512,128]{2,1,0:T(8,128)(2,1)S(1)}, u32[]{:S(2)}, u32[]{:S(2)}) collective-permute-start(bf16[2,512,128]{2,1,0:T(8,128)(2,1)} %get-tuple-element.9), channel_id=1, source_target_pairs={{1,0},{2,1},{3,2},{4,3},{5,4},{6,5},{7,6},{9,8},{10,9},{11,10},{12... | collective-permute-start | bytes 786440 | tf_op jit(solution)/shard_map/ppermute | solution.py:386
  17.3 6.9 %copy-start.1 = (bf16[2,512,128]{2,1,0:T(8,128)(2,1)}, bf16[2,512,128]{2,1,0:T(8,128)(2,1)S(1)}, u32[]{:S(2)}) copy-start(bf16[2,512,128]{2,1,0:T(8,128)(2,1)S(1)} %collective-permute-done.refs_2_.left_ref) | copy-start | bytes 786436
  24.2 0.7 copy-start.2
  34.0 32.4 %all-to-all-start = ((bf16[16,2,8,32,128]{4,3,2,1,0:T(8,128)(2,1)}), bf16[16,2,8,32,128]{4,3,2,1,0:T(8,128)(2,1)S(1)}, u32[]{:S(2)}, u32[]{:S(2)}) async-start(bf16[16,2,8,32,128]{4,3,2,1,0:T(8,128)(2,1)} %shard_map.59), calls=%async_computation | async-start | bytes 4194304 | tf_op jit(solution)/shard_map/all_to_all | solution.py:405
  66.4 1.4 copy-start
  67.8 87.3 %all-to-all-start.1 = ((bf16[16,6,8,32,128]{4,3,2,1,0:T(8,128)(2,1)}), bf16[16,6,8,32,128]{4,3,2,1,0:T(8,128)(2,1)}, u32[]{:S(2)}, u32[]{:S(2)}) async-start(bf16[16,6,8,32,128]{4,3,2,1,0:T(8,128)(2,1)} %shard_map.60), calls=%async_computation.1 | async-start | bytes 12582912 | tf_op jit(solution)/shard_map/all_to_all | solution.py:405
  95.6 53.2 %copy-start.4 = (s32[128]{0:T(128)S(1)}, s32[128]{0:T(128)}, u32[]{:S(2)}) copy-start(s32[128]{0:T(128)} %constant.55.clone) | copy-start | bytes 1540
  95.6 2.7 %collective-permute-start.2 = (f32[8,8,32,128]{3,2,0,1:T(8,128)S(1)}, f32[8,8,32,128]{3,2,0,1:T(8,128)S(1)}, u32[]{:S(2)}, u32[]{:S(2)}) collective-permute-start(f32[8,8,32,128]{3,2,0,1:T(8,128)S(1)} %bitcast.39), channel_id=1, source_target_pairs={{0,8},{8,0},{16,24},{24,16},{32,40},{40,32},{48,56},{56,48},{64,72... | collective-permute-start | bytes 3145736 | tf_op jit(solution)/shard_map/ppermute | solution.py:421
  98.6 49.1 %collective-permute-start.3 = (bf16[8,32,128]{2,1,0:T(8,128)(2,1)S(1)}, bf16[8,32,128]{2,1,0:T(8,128)(2,1)S(1)}, u32[]{:S(2)}, u32[]{:S(2)}) collective-permute-start(bf16[8,32,128]{2,1,0:T(8,128)(2,1)S(1)} %get-tuple-element.12), channel_id=1, source_target_pairs={{0,16},{8,24},{16,32},{24,40},{32,48},{40,56},{48,64},{56,72},{64,... | collective-permute-start | bytes 196616 | tf_op jit(solution)/shard_map/ppermute | solution.py:427
  100.4 47.3 %collective-permute-start.9 = (bf16[8,32,128]{2,1,0:T(8,128)(2,1)S(1)}, bf16[8,32,128]{2,1,0:T(8,128)(2,1)S(1)}, u32[]{:S(2)}, u32[]{:S(2)}) collective-permute-start(bf16[8,32,128]{2,1,0:T(8,128)(2,1)S(1)} %get-tuple-element.13), channel_id=1, source_target_pairs={{0,112},{8,120},{16,0},{24,8},{32,16},{40,24},{48,32},{56,40},{64,... | collective-permute-start | bytes 196616 | tf_op jit(solution)/shard_map/ppermute | solution.py:427
  102.8 49.8 %collective-permute-start.8 = (bf16[8,32,128]{2,1,0:T(8,128)(2,1)S(1)}, bf16[8,32,128]{2,1,0:T(8,128)(2,1)S(1)}, u32[]{:S(2)}, u32[]{:S(2)}) collective-permute-start(bf16[8,32,128]{2,1,0:T(8,128)(2,1)S(1)} %get-tuple-element.14), channel_id=1, source_target_pairs={{0,96},{8,104},{16,112},{24,120},{32,0},{40,8},{48,16},{56,24},{64... | collective-permute-start | bytes 196616 | tf_op jit(solution)/shard_map/ppermute | solution.py:427
  104.6 48.0 %collective-permute-start.7 = (bf16[8,32,128]{2,1,0:T(8,128)(2,1)S(1)}, bf16[8,32,128]{2,1,0:T(8,128)(2,1)S(1)}, u32[]{:S(2)}, u32[]{:S(2)}) collective-permute-start(bf16[8,32,128]{2,1,0:T(8,128)(2,1)S(1)} %get-tuple-element.15), channel_id=1, source_target_pairs={{0,80},{8,88},{16,96},{24,104},{32,112},{40,120},{48,0},{56,8},{64... | collective-permute-start | bytes 196616 | tf_op jit(solution)/shard_map/ppermute | solution.py:427
  105.5 47.2 %collective-permute-start.6 = (bf16[8,32,128]{2,1,0:T(8,128)(2,1)S(1)}, bf16[8,32,128]{2,1,0:T(8,128)(2,1)S(1)}, u32[]{:S(2)}, u32[]{:S(2)}) collective-permute-start(bf16[8,32,128]{2,1,0:T(8,128)(2,1)S(1)} %get-tuple-element.16), channel_id=1, source_target_pairs={{0,64},{8,72},{16,80},{24,88},{32,96},{40,104},{48,112},{56,120},{... | collective-permute-start | bytes 196616 | tf_op jit(solution)/shard_map/ppermute | solution.py:427
  147.7 6.7 %collective-permute-start.5 = (bf16[8,32,128]{2,1,0:T(8,128)(2,1)S(1)}, bf16[8,32,128]{2,1,0:T(8,128)(2,1)S(1)}, u32[]{:S(2)}, u32[]{:S(2)}) collective-permute-start(bf16[8,32,128]{2,1,0:T(8,128)(2,1)S(1)} %get-tuple-element.17), channel_id=1, source_target_pairs={{0,48},{8,56},{16,64},{24,72},{32,80},{40,88},{48,96},{56,104},{64... | collective-permute-start | bytes 196616 | tf_op jit(solution)/shard_map/ppermute | solution.py:427
  147.7 6.7 %collective-permute-start.4 = (bf16[8,32,128]{2,1,0:T(8,128)(2,1)S(1)}, bf16[8,32,128]{2,1,0:T(8,128)(2,1)S(1)}, u32[]{:S(2)}, u32[]{:S(2)}) collective-permute-start(bf16[8,32,128]{2,1,0:T(8,128)(2,1)S(1)} %get-tuple-element.18), channel_id=1, source_target_pairs={{0,32},{8,40},{16,48},{24,56},{32,64},{40,72},{48,80},{56,88},{64,... | collective-permute-start | bytes 196616 | tf_op jit(solution)/shard_map/ppermute | solution.py:427

commit v6 on v5

--- a/solution.py
+++ b/solution.py
@@ -223,7 +223,7 @@
             ],
         ),
         out_shape=jax.ShapeDtypeStruct((owners, count, planes, strip, lanes), jnp.bfloat16),
-        compiler_params=pltpu.CompilerParams(vmem_limit_bytes=VMEM),
+        compiler_params=pltpu.CompilerParams(vmem_limit_bytes=62 << 20),
     )(meta, raw, left, right)
 
 
@@ -282,29 +282,41 @@
 
 
 def spread_body(taps_ref, order_ref, kernel_ref, rowsum_ref):
-    total = order_ref.shape[1]
-    frame = iota((total, total), 0)
-    lag = frame - jnp.broadcast_to(order_ref[0:1, :], (total, total))
-    value = jnp.zeros((total, total), jnp.float32)
+    total = rowsum_ref.shape[0] // SUB
+    frames = order_ref.shape[1] // 2
+    reach = kernel_ref.shape[1] // (frames * SUB) - 1
+    for back in range(reach + 1):
+        lag = iota((frames, 2 * frames), 0) + (back * frames - order_ref[0:1, :])
+        value = jnp.zeros(lag.shape, jnp.float32)
+        for tap in range(TAPS):
+            value = jnp.where(lag == tap, taps_ref[tap], value)
+        small = value.astype(jnp.bfloat16)
+        shape = (2 * frames, frames * SUB)
+        repeat = iota(shape, 1) // SUB == iota(shape, 0)
+        wide = dot(small, repeat.astype(jnp.float32).astype(jnp.bfloat16))
+        width = frames * SUB
+        tall = jnp.broadcast_to(wide[:, None, :], (frames, SUB, width)).reshape(width, width)
+        same = iota(tall.shape, 0) % SUB == iota(tall.shape, 1) % SUB
+        low = (reach - back) * width
+        kernel_ref[:, low : low + width] = jnp.where(same, tall, 0.0).astype(jnp.bfloat16)
+
+    lag = iota((total, LANES), 0) - iota((total, LANES), 1)
+    value = jnp.zeros(lag.shape, jnp.float32)
     for tap in range(TAPS):
-        value = jnp.where(lag == tap, taps_ref[tap], value)
-    small = value.astype(jnp.bfloat16)
-    rowsum = jnp.sum(small.astype(jnp.float32), axis=1, keepdims=True) * (1.0 / total)
-    rowsum_ref[...] = jnp.broadcast_to(rowsum[:, :, None], (total, SUB, LANES)).reshape(total * SUB, LANES)
-    repeat = iota((total, total * SUB), 1) // SUB == iota((total, total * SUB), 0)
-    wide = dot(small, repeat.astype(jnp.float32).astype(jnp.bfloat16))
-    tall = jnp.broadcast_to(wide[:, None, :], (total, SUB, total * SUB)).reshape(total * SUB, total * SUB)
-    same = iota(tall.shape, 0) % SUB == iota(tall.shape, 1) % SUB
-    kernel_ref[...] = jnp.where(same, tall, 0.0).astype(jnp.bfloat16)
-
-
-def spread_kernel(taps, order):
-    total = order.shape[1]
+        value = jnp.where((lag >= 0) & (iota(lag.shape, 1) == tap), taps_ref[tap], value)
+    rowsum = dot(value.astype(jnp.bfloat16), jnp.ones((LANES, LANES), jnp.bfloat16)) * (1.0 / total)
+    rowsum_ref[...] = jnp.broadcast_to(rowsum[:, None, :], (total, SUB, LANES)).reshape(total * SUB, LANES)
+
+
+def spread_kernel(taps, order, total, frames, reach):
+    def body(*refs):
+        spread_body(*refs)
+
     return pl.pallas_call(
-        spread_body,
+        body,
         in_specs=[pl.BlockSpec(memory_space=pltpu.SMEM), pl.BlockSpec(memory_space=pltpu.VMEM)],
         out_shape=(
-            jax.ShapeDtypeStruct((total * SUB, total * SUB), jnp.bfloat16),
+            jax.ShapeDtypeStruct((frames * SUB, (reach + 1) * frames * SUB), jnp.bfloat16),
             jax.ShapeDtypeStruct((total * SUB, LANES), jnp.float32),
         ),
         compiler_params=pltpu.CompilerParams(vmem_limit_bytes=VMEM),
@@ -318,9 +330,9 @@
     total, _, strip, lanes = out_ref.shape
     frames = group * (total // owners)
     width = frames * SUB
-    reach = -(-TAPS // frames)
-
-    for pair in range(strip // (2 * SUB)):
+    reach = kernel_ref.shape[1] // width - 1
+
+    for z, pair in [(z, pair) for z in range(out_ref.shape[1]) for pair in range(strip // (2 * SUB))]:
         tiles = []
         for j in range(owners // group):
             halves = []
@@ -328,7 +340,7 @@
                 low = (2 * pair + half) * SUB
                 parts = []
                 for ref, count in zip(got, CHUNKS):
-                    part = ref[group * j : group * (j + 1), 0:count, 0, low : low + SUB, :]
+                    part = ref[group * j : group * (j + 1), 0:count, z, low : low + SUB, :]
                     parts.append(part.reshape(group * count * SUB, lanes))
                 halves.append(jnp.concatenate(parts, axis=0))
             tiles.append(jnp.concatenate(halves, axis=1))
@@ -338,7 +350,8 @@
             rows = slice(i * width, (i + 1) * width)
             value = None
             for j in range(lowest, i + 1):
-                part = dot(kernel_ref[rows, j * width : (j + 1) * width], tiles[j])
+                low = (reach - i + j) * width
+                part = dot(kernel_ref[:, low : low + width], tiles[j])
                 value = part if value is None else value + part
             rowsum = rowsum_ref[rows, :].reshape(frames, SUB, lanes)
             value = value.reshape(frames, SUB, 2 * lanes)
@@ -347,7 +360,7 @@
                 for h in range(2)
             ]
             both = jnp.concatenate(done, axis=1).astype(jnp.bfloat16)
-            out_ref[i * frames : (i + 1) * frames, 0, 2 * SUB * pair : 2 * SUB * (pair + 1), :] = both
+            out_ref[i * frames : (i + 1) * frames, z, 2 * SUB * pair : 2 * SUB * (pair + 1), :] = both
 
 
 def filter_frames(kernel, rowsum, got, total, group):
@@ -357,16 +370,16 @@
         pl.BlockSpec(rowsum.shape, lambda z: (0, 0)),
     ]
     for part in got:
-        in_specs.append(pl.BlockSpec((owners, part.shape[1], 1, strip, lanes), lambda z: (0, 0, z, 0, 0)))
+        in_specs.append(pl.BlockSpec((owners, part.shape[1], 2, strip, lanes), lambda z: (0, 0, z, 0, 0)))
 
     def body(*refs):
         filter_body(group, *refs)
 
     return pl.pallas_call(
         body,
-        grid=(planes,),
+        grid=(planes // 2,),
         in_specs=in_specs,
-        out_specs=pl.BlockSpec((total, 1, strip, lanes), lambda z: (0, z, 0, 0)),
+        out_specs=pl.BlockSpec((total, 2, strip, lanes), lambda z: (0, z, 0, 0)),
         out_shape=jax.ShapeDtypeStruct((total, planes, strip, lanes), jnp.bfloat16),
         compiler_params=pltpu.CompilerParams(vmem_limit_bytes=VMEM),
         name="filter_frames",
@@ -390,13 +403,15 @@
     meta = jnp.concatenate([offsets.reshape(-1), ends])
 
     order = []
-    for block in range(owners // group):
-        low = 0
-        for count in CHUNKS:
-            for owner in range(group * block, group * (block + 1)):
-                order += [owner * frame_dev + low + f for f in range(count)]
-            low += count
-    kernel, rowsum = spread_kernel(taps, jnp.tile(jnp.array(order, jnp.int32)[None], (SUB, 1)))
+    low = 0
+    for count in CHUNKS:
+        for owner in range(group):
+            order += [owner * frame_dev + low + f for f in range(count)]
+        low += count
+    frames = group * frame_dev
+    reach = min(-(-TAPS // frames), owners // group - 1)
+    order = jnp.array(order + [1 << 20] * frames, jnp.int32)
+    kernel, rowsum = spread_kernel(taps, jnp.tile(order[None], (SUB, 1)), total, frames, reach)
 
     got = []
     low = 0

time: 168 us -> 165 us (0.982)
  Pallas kernels: 73.4 us -> 70.5 us
    pallas_call x2, Pallas kernels: 15.6 us -> 12.8 us  [the longest x1 10.3 us: filter_frames(): pl.pallas_call(body, grid=(planes // 2,), in_specs=in_specs, out_specs=pl...]
where the time goes in v6:
time: 165 us; the launch traced here: 164 us
  Pallas kernels  70.5 us (43%)
  waiting for transfers between devices  61.7 us (37%)
  starting transfers between devices  26 us (16%)
  local copies, waits for them, and re-layouts  3.46 us (2%)
    ppermute x7, waiting for transfers between devices, summed_over_frames(): lax.ppermute(sent, 'frames', [(i, (i + 2 * turn) % owners) for i in range...  42.1 us
    pallas_call x2, Pallas kernels, register(): pl.pallas_call(body, grid_spec=pltpu.PrefetchScalarGridSpec(num_scalar_pr...  30.1 us
    pallas_call x1, Pallas kernels, frame_sum(): pl.pallas_call(frame_sum_body, grid_spec=pltpu.PrefetchScalarGridSpec(num...  21.2 us
    ppermute x7, starting transfers between devices, summed_over_frames(): lax.ppermute(sent, 'frames', [(i, (i + 2 * turn) % owners) for i in range...  10.6 us
    pallas_call x1, Pallas kernels, filter_frames(): pl.pallas_call(body, grid=(planes // 2,), in_specs=in_specs, out_specs=pl...  10.3 us
    all_to_all x2, starting transfers between devices, local(): lax.all_to_all(sent, 'frames', split_axis=0, concat_axis=0, tiled=True)  9.3 us
    ppermute x1, waiting for transfers between devices, local(): right = lax.ppermute(first_columns, 'tiles', [(j, i) for i, j in upward])  6.9 us
    all_to_all x2, waiting for transfers between devices, local(): lax.all_to_all(sent, 'frames', split_axis=0, concat_axis=0, tiled=True)  6.85 us
  transfers between devices with their start and end apart: 12, of which 6 were waited for; matrix products, arithmetic and copies ran while one was open for 3% of the time, Pallas kernels for 27%

profile of v6, /device:TPU:96, one launch (start us, length us, event | category | flops | bytes accessed | tf_op | source)
XLA Modules:
  0.0 164.1 jit_solution(17506394768839748463)
XLA Ops:
  0.6 6.5 %pack_edges.1 = (bf16[2,512,128]{2,1,0:T(8,128)(2,1)}, bf16[2,512,128]{2,1,0:T(8,128)(2,1)}) custom-call(bf16[8,8,512,128]{3,2,1,0:T(8,128)(2,1)} %raw_ref.1, bf16[8,8,512,128]{3,2,1,0:T(8,128)(2,1)} %raw_ref.1), custom_call_target="tpu_custom_call" | custom-call | tf_op jit(solution)/shard_map/pack_edges/pallas_call | solution.py:68
  7.1 3.6 %collective-permute-start = (bf16[2,512,128]{2,1,0:T(8,128)(2,1)}, bf16[2,512,128]{2,1,0:T(8,128)(2,1)S(1)}, u32[]{:S(2)}, u32[]{:S(2)}) collective-permute-start(bf16[2,512,128]{2,1,0:T(8,128)(2,1)} %get-tuple-element.8), channel_id=1, source_target_pairs={{0,1},{1,2},{2,3},{3,4},{4,5},{5,6},{6,7},{8,9},{9,10},{10,11},{11... | collective-permute-start | bytes 786440 | tf_op jit(solution)/shard_map/ppermute | solution.py:398
  10.7 2.3 %collective-permute-start.1 = (bf16[2,512,128]{2,1,0:T(8,128)(2,1)}, bf16[2,512,128]{2,1,0:T(8,128)(2,1)S(1)}, u32[]{:S(2)}, u32[]{:S(2)}) collective-permute-start(bf16[2,512,128]{2,1,0:T(8,128)(2,1)} %get-tuple-element.9), channel_id=1, source_target_pairs={{1,0},{2,1},{3,2},{4,3},{5,4},{6,5},{7,6},{9,8},{10,9},{11,10},{12... | collective-permute-start | bytes 786440 | tf_op jit(solution)/shard_map/ppermute | solution.py:399
  13.8 3.4 %collective-permute-done.refs_2_.left_ref = bf16[2,512,128]{2,1,0:T(8,128)(2,1)S(1)} collective-permute-done((bf16[2,512,128]{2,1,0:T(8,128)(2,1)}, bf16[2,512,128]{2,1,0:T(8,128)(2,1)S(1)}, u32[]{:S(2)}, u32[]{:S(2)}) %collective-permute-start) | collective-permute-done | bytes 262176 | tf_op jit(solution)/shard_map/ppermute | solution.py:398
  17.3 6.9 %collective-permute-done.1.refs_3_.right_ref = bf16[2,512,128]{2,1,0:T(8,128)(2,1)S(1)} collective-permute-done((bf16[2,512,128]{2,1,0:T(8,128)(2,1)}, bf16[2,512,128]{2,1,0:T(8,128)(2,1)S(1)}, u32[]{:S(2)}, u32[]{:S(2)}) %collective-permute-start.1) | collective-permute-done | bytes 262176 | tf_op jit(solution)/shard_map/ppermute | solution.py:399
  24.9 9.1 %shard_map.59 = bf16[16,2,8,32,128]{4,3,2,1,0:T(8,128)(2,1)} custom-call(s32[26]{0:T(128)} %pad_add_fusion.refs_0_.meta_ref, bf16[8,8,512,128]{3,2,1,0:T(8,128)(2,1)} %raw_ref.1, bf16[2,512,128]{2,1,0:T(8,128)(2,1)} %copy-done, bf16[2,512,128]{2,1,0:T(8,128)(2,1)} %copy-done.1), custom_call_target="tpu_custom_call" | custom-call | tf_op jit(solution)/shard_map/pallas_call | solution.py:208
  33.9 4.7 %all-to-all-start = ((bf16[16,2,8,32,128]{4,3,2,1,0:T(8,128)(2,1)}), bf16[16,2,8,32,128]{4,3,2,1,0:T(8,128)(2,1)}, u32[]{:S(2)}, u32[]{:S(2)}) async-start(bf16[16,2,8,32,128]{4,3,2,1,0:T(8,128)(2,1)} %shard_map.59), calls=%async_computation | async-start | bytes 4194304 | tf_op jit(solution)/shard_map/all_to_all | solution.py:420
  38.6 21.0 %shard_map.60 = bf16[16,6,8,32,128]{4,3,2,1,0:T(8,128)(2,1)} custom-call(s32[26]{0:T(128)} %pad_add_fusion.refs_0_.meta_ref, bf16[8,8,512,128]{3,2,1,0:T(8,128)(2,1)} %raw_ref.1, bf16[2,512,128]{2,1,0:T(8,128)(2,1)} %copy-done, bf16[2,512,128]{2,1,0:T(8,128)(2,1)} %copy-done.1), custom_call_target="tpu_custom_call" | custom-call | tf_op jit(solution)/shard_map/pallas_call | solution.py:208
  59.6 6.8 %all-to-all-done.refs_2_ = bf16[16,2,8,32,128]{4,3,2,1,0:T(8,128)(2,1)} async-done(((bf16[16,2,8,32,128]{4,3,2,1,0:T(8,128)(2,1)}), bf16[16,2,8,32,128]{4,3,2,1,0:T(8,128)(2,1)}, u32[]{:S(2)}, u32[]{:S(2)}) %all-to-all-start) | async-done | bytes 2097184 | tf_op jit(solution)/shard_map/all_to_all | solution.py:420
  66.5 4.6 %all-to-all-start.1 = ((bf16[16,6,8,32,128]{4,3,2,1,0:T(8,128)(2,1)}), bf16[16,6,8,32,128]{4,3,2,1,0:T(8,128)(2,1)}, u32[]{:S(2)}, u32[]{:S(2)}) async-start(bf16[16,6,8,32,128]{4,3,2,1,0:T(8,128)(2,1)} %shard_map.60), calls=%async_computation.1 | async-start | bytes 12582912 | tf_op jit(solution)/shard_map/all_to_all | solution.py:420
  71.1 21.2 %frame_sum.1 = f32[8,512,128]{2,1,0:T(8,128)} custom-call(s32[26]{0:T(128)} %pad_add_fusion.refs_0_.meta_ref, bf16[8,8,512,128]{3,2,1,0:T(8,128)(2,1)} %raw_ref.1, bf16[2,512,128]{2,1,0:T(8,128)(2,1)} %copy-done, bf16[2,512,128]{2,1,0:T(8,128)(2,1)} %copy-done.1), custom_call_target="tpu_custom_call" | custom-call | tf_op jit(solution)/shard_map/frame_sum/pallas_call | solution.py:265
  92.3 1.8 %constant_dynamic-slice_fusion.1 = (f32[8,8,1,32,128]{4,3,2,1,0:T(8,128)S(1)}, f32[8,8,1,32,128]{4,3,2,1,0:T(8,128)S(1)}) fusion(f32[8,8,2,32,128]{4,3,2,1,0:T(8,128)} %bitcast.38, s32[]{:T(128)S(6)} %select_n.32, s32[]{:T(128)S(6)} %select_n.33), kind=kLoop, calls=%fused_computation.25 | loop fusion | bytes 4194312 | tf_op jit(solution)/shard_map/jit(dynamic_index_in_dim)/dynamic_slice | solution.py:434
  94.6 2.4 %collective-permute-done.2 = f32[8,8,32,128]{3,2,0,1:T(8,128)S(1)} collective-permute-done((f32[8,8,32,128]{3,2,0,1:T(8,128)S(1)}, f32[8,8,32,128]{3,2,0,1:T(8,128)S(1)}, u32[]{:S(2)}, u32[]{:S(2)}) %collective-permute-start.2) | collective-permute-done | bytes 1048608 | tf_op jit(solution)/shard_map/ppermute | solution.py:436
  97.3 1.8 %collective-permute-start.3 = (bf16[8,32,128]{2,1,0:T(8,128)(2,1)S(1)}, bf16[8,32,128]{2,1,0:T(8,128)(2,1)S(1)}, u32[]{:S(2)}, u32[]{:S(2)}) collective-permute-start(bf16[8,32,128]{2,1,0:T(8,128)(2,1)S(1)} %get-tuple-element.12), channel_id=1, source_target_pairs={{0,16},{8,24},{16,32},{24,40},{32,48},{40,56},{48,64},{56,72},{64,... | collective-permute-start | bytes 196616 | tf_op jit(solution)/shard_map/ppermute | solution.py:442
  99.1 2.4 %collective-permute-start.9 = (bf16[8,32,128]{2,1,0:T(8,128)(2,1)S(1)}, bf16[8,32,128]{2,1,0:T(8,128)(2,1)S(1)}, u32[]{:S(2)}, u32[]{:S(2)}) collective-permute-start(bf16[8,32,128]{2,1,0:T(8,128)(2,1)S(1)} %get-tuple-element.13), channel_id=1, source_target_pairs={{0,112},{8,120},{16,0},{24,8},{32,16},{40,24},{48,32},{56,40},{64,... | collective-permute-start | bytes 196616 | tf_op jit(solution)/shard_map/ppermute | solution.py:442
  101.5 1.8 %collective-permute-start.8 = (bf16[8,32,128]{2,1,0:T(8,128)(2,1)S(1)}, bf16[8,32,128]{2,1,0:T(8,128)(2,1)S(1)}, u32[]{:S(2)}, u32[]{:S(2)}) collective-permute-start(bf16[8,32,128]{2,1,0:T(8,128)(2,1)S(1)} %get-tuple-element.14), channel_id=1, source_target_pairs={{0,96},{8,104},{16,112},{24,120},{32,0},{40,8},{48,16},{56,24},{64... | collective-permute-start | bytes 196616 | tf_op jit(solution)/shard_map/ppermute | solution.py:442
  103.3 0.8 collective-permute-start.7
  104.1 2.7 %collective-permute-start.6 = (bf16[8,32,128]{2,1,0:T(8,128)(2,1)S(1)}, bf16[8,32,128]{2,1,0:T(8,128)(2,1)S(1)}, u32[]{:S(2)}, u32[]{:S(2)}) collective-permute-start(bf16[8,32,128]{2,1,0:T(8,128)(2,1)S(1)} %get-tuple-element.16), channel_id=1, source_target_pairs={{0,64},{8,72},{16,80},{24,88},{32,96},{40,104},{48,112},{56,120},{... | collective-permute-start | bytes 196616 | tf_op jit(solution)/shard_map/ppermute | solution.py:442
  106.9 39.5 %collective-permute-done.3 = bf16[8,32,128]{2,1,0:T(8,128)(2,1)S(1)} collective-permute-done((bf16[8,32,128]{2,1,0:T(8,128)(2,1)S(1)}, bf16[8,32,128]{2,1,0:T(8,128)(2,1)S(1)}, u32[]{:S(2)}, u32[]{:S(2)}) %collective-permute-start.3) | collective-permute-done | bytes 65568 | tf_op jit(solution)/shard_map/ppermute | solution.py:442
  146.4 1.0 collective-permute-start.4
  148.0 2.5 %spread_kernel.1 = (bf16[256,768]{1,0:T(8,128)(2,1)}, f32[1024,128]{1,0:T(8,128)}) custom-call(f32[64]{0:T(128)} %refs_0_.2, s32[8,64]{1,0:T(8,128)} %tile.2.refs_1_), custom_call_target="tpu_custom_call" | custom-call | tf_op jit(solution)/shard_map/spread_kernel/pallas_call | solution.py:315
  150.5 2.6 %collective-permute-done.5 = bf16[8,32,128]{2,1,0:T(8,128)(2,1)S(1)} collective-permute-done((bf16[8,32,128]{2,1,0:T(8,128)(2,1)S(1)}, bf16[8,32,128]{2,1,0:T(8,128)(2,1)S(1)}, u32[]{:S(2)}, u32[]{:S(2)}) %collective-permute-start.5) | collective-permute-done | bytes 65568 | tf_op jit(solution)/shard_map/ppermute | solution.py:442
  153.1 0.7 fusion.6
  153.8 10.3 %filter_frames.1 = bf16[128,8,32,128]{3,2,1,0:T(8,128)(2,1)} custom-call(bf16[256,768]{1,0:T(8,128)(2,1)} %get-tuple-element.6.refs_0_, f32[1024,128]{1,0:T(8,128)} %get-tuple-element.7.refs_1_, bf16[16,2,8,32,128]{4,3,2,1,0:T(8,128)(2,1)} %all-to-all-done.refs_2_, bf16[16,6,8,32,128]{4,3,2,1,0:T(8,128)(2,1)} %all-to-all-done.1.refs_3_), custom_call_target="tpu_custom_call" | custom-call | tf_op jit(solution)/shard_map/filter_frames/pallas_call | solution.py:378
  (24 shorter events, 2.8 us)
Async XLA Ops:
  0.6 12.4 %copy-start.2 = (s32[8,3]{0,1:T(4,128)S(1)}, s32[8,3]{0,1:T(4,128)}, u32[]{:S(2)}) copy-start(s32[8,3]{0,1:T(4,128)} %param.5) | copy-start | bytes 292
  7.1 10.1 %collective-permute-start = (bf16[2,512,128]{2,1,0:T(8,128)(2,1)}, bf16[2,512,128]{2,1,0:T(8,128)(2,1)S(1)}, u32[]{:S(2)}, u32[]{:S(2)}) collective-permute-start(bf16[2,512,128]{2,1,0:T(8,128)(2,1)} %get-tuple-element.8), channel_id=1, source_target_pairs={{0,1},{1,2},{2,3},{3,4},{4,5},{5,6},{6,7},{8,9},{9,10},{10,11},{11... | collective-permute-start | bytes 786440 | tf_op jit(solution)/shard_map/ppermute | solution.py:398
  10.7 13.5 %collective-permute-start.1 = (bf16[2,512,128]{2,1,0:T(8,128)(2,1)}, bf16[2,512,128]{2,1,0:T(8,128)(2,1)S(1)}, u32[]{:S(2)}, u32[]{:S(2)}) collective-permute-start(bf16[2,512,128]{2,1,0:T(8,128)(2,1)} %get-tuple-element.9), channel_id=1, source_target_pairs={{1,0},{2,1},{3,2},{4,3},{5,4},{6,5},{7,6},{9,8},{10,9},{11,10},{12... | collective-permute-start | bytes 786440 | tf_op jit(solution)/shard_map/ppermute | solution.py:399
  17.3 6.9 %copy-start = (bf16[2,512,128]{2,1,0:T(8,128)(2,1)}, bf16[2,512,128]{2,1,0:T(8,128)(2,1)S(1)}, u32[]{:S(2)}) copy-start(bf16[2,512,128]{2,1,0:T(8,128)(2,1)S(1)} %collective-permute-done.refs_2_.left_ref) | copy-start | bytes 786436
  24.2 0.7 copy-start.1
  33.9 32.5 %all-to-all-start = ((bf16[16,2,8,32,128]{4,3,2,1,0:T(8,128)(2,1)}), bf16[16,2,8,32,128]{4,3,2,1,0:T(8,128)(2,1)}, u32[]{:S(2)}, u32[]{:S(2)}) async-start(bf16[16,2,8,32,128]{4,3,2,1,0:T(8,128)(2,1)} %shard_map.59), calls=%async_computation | async-start | bytes 4194304 | tf_op jit(solution)/shard_map/all_to_all | solution.py:420
  66.5 87.3 %all-to-all-start.1 = ((bf16[16,6,8,32,128]{4,3,2,1,0:T(8,128)(2,1)}), bf16[16,6,8,32,128]{4,3,2,1,0:T(8,128)(2,1)}, u32[]{:S(2)}, u32[]{:S(2)}) async-start(bf16[16,6,8,32,128]{4,3,2,1,0:T(8,128)(2,1)} %shard_map.60), calls=%async_computation.1 | async-start | bytes 12582912 | tf_op jit(solution)/shard_map/all_to_all | solution.py:420
  92.3 55.1 %copy-start.3 = (s32[64]{0:T(128)S(1)}, s32[64]{0:T(128)}, u32[]{:S(2)}) copy-start(s32[64]{0:T(128)} %constant.55.clone) | copy-start | bytes 772
  94.3 2.7 %collective-permute-start.2 = (f32[8,8,32,128]{3,2,0,1:T(8,128)S(1)}, f32[8,8,32,128]{3,2,0,1:T(8,128)S(1)}, u32[]{:S(2)}, u32[]{:S(2)}) collective-permute-start(f32[8,8,32,128]{3,2,0,1:T(8,128)S(1)} %bitcast.39), channel_id=1, source_target_pairs={{0,8},{8,0},{16,24},{24,16},{32,40},{40,32},{48,56},{56,48},{64,72... | collective-permute-start | bytes 3145736 | tf_op jit(solution)/shard_map/ppermute | solution.py:436
  97.3 49.1 %collective-permute-start.3 = (bf16[8,32,128]{2,1,0:T(8,128)(2,1)S(1)}, bf16[8,32,128]{2,1,0:T(8,128)(2,1)S(1)}, u32[]{:S(2)}, u32[]{:S(2)}) collective-permute-start(bf16[8,32,128]{2,1,0:T(8,128)(2,1)S(1)} %get-tuple-element.12), channel_id=1, source_target_pairs={{0,16},{8,24},{16,32},{24,40},{32,48},{40,56},{48,64},{56,72},{64,... | collective-permute-start | bytes 196616 | tf_op jit(solution)/shard_map/ppermute | solution.py:442
  99.1 47.3 %collective-permute-start.9 = (bf16[8,32,128]{2,1,0:T(8,128)(2,1)S(1)}, bf16[8,32,128]{2,1,0:T(8,128)(2,1)S(1)}, u32[]{:S(2)}, u32[]{:S(2)}) collective-permute-start(bf16[8,32,128]{2,1,0:T(8,128)(2,1)S(1)} %get-tuple-element.13), channel_id=1, source_target_pairs={{0,112},{8,120},{16,0},{24,8},{32,16},{40,24},{48,32},{56,40},{64,... | collective-permute-start | bytes 196616 | tf_op jit(solution)/shard_map/ppermute | solution.py:442
  101.5 49.0 %collective-permute-start.8 = (bf16[8,32,128]{2,1,0:T(8,128)(2,1)S(1)}, bf16[8,32,128]{2,1,0:T(8,128)(2,1)S(1)}, u32[]{:S(2)}, u32[]{:S(2)}) collective-permute-start(bf16[8,32,128]{2,1,0:T(8,128)(2,1)S(1)} %get-tuple-element.14), channel_id=1, source_target_pairs={{0,96},{8,104},{16,112},{24,120},{32,0},{40,8},{48,16},{56,24},{64... | collective-permute-start | bytes 196616 | tf_op jit(solution)/shard_map/ppermute | solution.py:442
  103.3 47.2 %collective-permute-start.7 = (bf16[8,32,128]{2,1,0:T(8,128)(2,1)S(1)}, bf16[8,32,128]{2,1,0:T(8,128)(2,1)S(1)}, u32[]{:S(2)}, u32[]{:S(2)}) collective-permute-start(bf16[8,32,128]{2,1,0:T(8,128)(2,1)S(1)} %get-tuple-element.15), channel_id=1, source_target_pairs={{0,80},{8,88},{16,96},{24,104},{32,112},{40,120},{48,0},{56,8},{64... | collective-permute-start | bytes 196616 | tf_op jit(solution)/shard_map/ppermute | solution.py:442
  104.1 46.3 %collective-permute-start.6 = (bf16[8,32,128]{2,1,0:T(8,128)(2,1)S(1)}, bf16[8,32,128]{2,1,0:T(8,128)(2,1)S(1)}, u32[]{:S(2)}, u32[]{:S(2)}) collective-permute-start(bf16[8,32,128]{2,1,0:T(8,128)(2,1)S(1)} %get-tuple-element.16), channel_id=1, source_target_pairs={{0,64},{8,72},{16,80},{24,88},{32,96},{40,104},{48,112},{56,120},{... | collective-permute-start | bytes 196616 | tf_op jit(solution)/shard_map/ppermute | solution.py:442
  146.4 6.7 %collective-permute-start.5 = (bf16[8,32,128]{2,1,0:T(8,128)(2,1)S(1)}, bf16[8,32,128]{2,1,0:T(8,128)(2,1)S(1)}, u32[]{:S(2)}, u32[]{:S(2)}) collective-permute-start(bf16[8,32,128]{2,1,0:T(8,128)(2,1)S(1)} %get-tuple-element.17), channel_id=1, source_target_pairs={{0,48},{8,56},{16,64},{24,72},{32,80},{40,88},{48,96},{56,104},{64... | collective-permute-start | bytes 196616 | tf_op jit(solution)/shard_map/ppermute | solution.py:442
  146.4 6.7 %collective-permute-start.4 = (bf16[8,32,128]{2,1,0:T(8,128)(2,1)S(1)}, bf16[8,32,128]{2,1,0:T(8,128)(2,1)S(1)}, u32[]{:S(2)}, u32[]{:S(2)}) collective-permute-start(bf16[8,32,128]{2,1,0:T(8,128)(2,1)S(1)} %get-tuple-element.18), channel_id=1, source_target_pairs={{0,32},{8,40},{16,48},{24,56},{32,64},{40,72},{48,80},{56,88},{64,... | collective-permute-start | bytes 196616 | tf_op jit(solution)/shard_map/ppermute | solution.py:442
